TPU v7x, 32 devices: a whole 2x2x4 slice. The times are simulated.
32 devices in a mesh: dp: 4 (over z), ep: 8 (over y, x, core).
Axes of the slice: x: 2, y: 2, z: 4, core: 2. Of those that a mesh axis runs over, the one named last changes fastest.
Arguments:
- tokens: bfloat16 [16384, 1024], P(('dp', 'ep')), may hold values from -6 to 6
- bucket: int32 [32], P(('dp', 'ep')), may hold values from 0 to 1
- expert_ids: int32 [16384, 1], P(('dp', 'ep')), may hold values from 0 to 7
- ln1_gain: float32 [1024], replicated, may hold values from 0.5 to 1.5
- qkv_weight: bfloat16 [1024, 3072], P('ep'), may hold values from -0.1875 to 0.1875
- out_weight: bfloat16 [1024, 1024], P('ep'), may hold values from -0.75 to 0.75
- ln2_gain: float32 [1024], replicated, may hold values from 0.5 to 1.5
- up_weight: bfloat16 [1024, 4096], P('ep'), may hold values from -0.1875 to 0.1875
- down_weight: bfloat16 [4096, 1024], P('ep'), may hold values from -0.1875 to 0.1875
- mix_weight: bfloat16 [1024, 2], replicated, may hold values from -0.1875 to 0.1875
- expert_up: bfloat16 [8, 1024, 4096], P('ep', None, 'dp'), may hold values from -0.1875 to 0.1875
- expert_down: bfloat16 [8, 4096, 1024], P('ep', 'dp'), may hold values from -0.1875 to 0.1875
- cotangent: bfloat16 [16384, 1024], P(('dp', 'ep')), may hold values from -6 to 6
Outputs:
- output: bfloat16 [16384, 1024], P(('dp', 'ep'))
- tokens_grad: float32 [16384, 1024], P(('dp', 'ep'))
- ln1_gain_grad: float32 [1024], replicated
- qkv_weight_grad: float32 [1024, 3072], P('ep')
- out_weight_grad: float32 [1024, 1024], P('ep')
- ln2_gain_grad: float32 [1024], replicated
- up_weight_grad: float32 [1024, 4096], P('ep')
- down_weight_grad: float32 [4096, 1024], P('ep')
- mix_weight_grad: float32 [1024, 2], replicated
- expert_up_grad: float32 [8, 1024, 4096], P('ep', None, 'dp')
- expert_down_grad: float32 [8, 4096, 1024], P('ep', 'dp')
All inputs are finite; a program needn't handle non-finite values.
Results may differ from a plain program's by a relative error of at most 0.02.
Values may be sent and summed in bfloat16 or wider, within the bound.
A program may use at most 320 MiB of HBM per device.

v0:
```python
import jax
import jax.numpy as jnp
from jax import lax
from jax.sharding import PartitionSpec as P

HEAD = 64
SHORT_SEQS = 4


def layer_norm(values_in, gain_vec):
    centred = values_in - jnp.mean(values_in, axis=-1, keepdims=True)
    inverse = lax.rsqrt(jnp.mean(centred * centred, axis=-1, keepdims=True) + 1e-05)
    return centred * inverse * gain_vec


def softmax_last(scores):
    row_peak = jnp.max(scores, axis=-1, keepdims=True)
    weights = jnp.exp(scores - row_peak)
    return weights / jnp.sum(weights, axis=-1, keepdims=True)


def gelu_backward(pre_act, act_grad):
    unused, pullback = jax.vjp(jax.nn.gelu, pre_act)
    return pullback(act_grad)[0]


def head_split(qkv_rows):
    length = qkv_rows.shape[0]
    width = qkv_rows.shape[1] // 3
    shaped = qkv_rows.reshape(length, 3, width // HEAD, HEAD)
    return (shaped[:, 0], shaped[:, 1], shaped[:, 2])


def masked_scores(query_rows, key_rows, allowed):
    scores = jnp.einsum(
        "qhd,khd->hqk", query_rows, key_rows, preferred_element_type=jnp.float32
    ) * HEAD ** (-0.5)
    return jnp.where(allowed[None], scores, -1e30)


def attention_forward(qkv_rows, allowed):
    length = qkv_rows.shape[0]
    query_rows, key_rows, value_rows = head_split(qkv_rows)
    scores = masked_scores(query_rows, key_rows, allowed)
    row_peak = jnp.max(scores, axis=-1, keepdims=True)
    weights = jnp.exp(scores - row_peak)
    totals = jnp.sum(weights, axis=-1, keepdims=True)
    prob_low = (weights / totals).astype(jnp.bfloat16)
    mixed_rows = jnp.einsum(
        "hqk,khd->qhd", prob_low, value_rows, preferred_element_type=jnp.float32
    )
    return (mixed_rows.reshape(length, -1).astype(jnp.bfloat16), row_peak + jnp.log(totals))


def attention_backward(qkv_rows, allowed, log_total, attended_grad):
    length = qkv_rows.shape[0]
    query_rows, key_rows, value_rows = head_split(qkv_rows)
    probs_full = jnp.exp(masked_scores(query_rows, key_rows, allowed) - log_total)
    grad_heads = attended_grad.reshape(query_rows.shape)
    prob_grad = jnp.einsum(
        "qhd,khd->hqk", grad_heads, value_rows, preferred_element_type=jnp.float32
    )
    centre = jnp.sum(probs_full * prob_grad, axis=-1, keepdims=True)
    score_grad = (probs_full * (prob_grad - centre)).astype(jnp.bfloat16)
    factor = HEAD ** (-0.5)
    query_grad = (
        jnp.einsum("hqk,khd->qhd", score_grad, key_rows, preferred_element_type=jnp.float32)
        * factor
    )
    key_grad = (
        jnp.einsum("hqk,qhd->khd", score_grad, query_rows, preferred_element_type=jnp.float32)
        * factor
    )
    value_grad = jnp.einsum(
        "hqk,qhd->khd",
        probs_full.astype(jnp.bfloat16),
        grad_heads,
        preferred_element_type=jnp.float32,
    )
    stacked = jnp.stack([query_grad, key_grad, value_grad], axis=1)
    return stacked.reshape(length, -1).astype(jnp.bfloat16)


def on_device(
    tokens,
    bucket,
    expert_ids,
    ln1_gain,
    qkv_weight,
    out_weight,
    ln2_gain,
    up_weight,
    down_weight,
    mix_weight,
    expert_up,
    expert_down,
    cotangent,
):
    length = tokens.shape[0]
    experts = lax.axis_size("ep") * expert_up.shape[0]
    capacity = 5 * length // (4 * experts)
    qkv_full, out_full, up_full, down_full = (
        lax.all_gather(qkv_weight, "ep", axis=0, tiled=True),
        lax.all_gather(out_weight, "ep", axis=0, tiled=True),
        lax.all_gather(up_weight, "ep", axis=0, tiled=True),
        lax.all_gather(down_weight, "ep", axis=0, tiled=True),
    )
    token_rows = tokens.astype(jnp.float32)
    normed_in = layer_norm(token_rows, ln1_gain).astype(jnp.bfloat16)
    qkv_rows = jnp.dot(normed_in, qkv_full, preferred_element_type=jnp.float32).astype(jnp.bfloat16)
    position = jnp.arange(length, dtype=jnp.int32)
    sequence = jnp.where(bucket[0] == 1, 0, position // (length // SHORT_SEQS))
    allowed = jnp.logical_and(
        sequence[:, None] == sequence[None, :], position[None, :] <= position[:, None]
    )
    attended, log_total = attention_forward(qkv_rows, allowed)
    attn_out = jnp.dot(attended, out_full, preferred_element_type=jnp.float32)
    hidden_res = token_rows + attn_out
    mid_low = layer_norm(hidden_res, ln2_gain).astype(jnp.bfloat16)
    dense_pre = jnp.dot(mid_low, up_full, preferred_element_type=jnp.float32)
    dense_act = jax.nn.gelu(dense_pre).astype(jnp.bfloat16)
    dense_out = jnp.dot(dense_act, down_full, preferred_element_type=jnp.float32)
    mixing = softmax_last(jnp.dot(mid_low, mix_weight, preferred_element_type=jnp.float32))
    chosen = expert_ids[:, 0]
    one_hot = (chosen[:, None] == jnp.arange(experts, dtype=jnp.int32)[None, :]).astype(jnp.int32)
    slot_index = jnp.sum(one_hot * (jnp.cumsum(one_hot, axis=0) - 1), axis=1)
    slot_match = (
        slot_index[:, None, None] == jnp.arange(capacity, dtype=jnp.int32)[None, None, :]
    ).astype(jnp.int32)
    table_flat = (
        (one_hot[:, :, None] * slot_match).reshape(length, experts * capacity).astype(jnp.bfloat16)
    )
    sent_rows = jnp.einsum(
        "tk,td->kd", table_flat, mid_low, preferred_element_type=jnp.float32
    ).astype(jnp.bfloat16)
    arrived = lax.all_to_all(
        sent_rows.reshape(experts, capacity, -1), "ep", split_axis=0, concat_axis=1, tiled=True
    )
    slot_rows = lax.all_gather(arrived, "dp", axis=1, tiled=True)
    expert_pre = jnp.einsum(
        "erd,edf->erf", slot_rows, expert_up, preferred_element_type=jnp.float32
    )
    expert_act = jax.nn.gelu(expert_pre).astype(jnp.bfloat16)
    partial_out = jnp.einsum(
        "erf,efd->erd", expert_act, expert_down, preferred_element_type=jnp.float32
    )
    summed_out = lax.psum_scatter(
        partial_out.astype(jnp.bfloat16), "dp", scatter_dimension=1, tiled=True
    )
    returned = lax.all_to_all(summed_out, "ep", split_axis=1, concat_axis=0, tiled=True)
    expert_out = jnp.dot(
        table_flat, returned.reshape(experts * capacity, -1), preferred_element_type=jnp.float32
    )
    result = hidden_res + mixing[:, 0:1] * dense_out + mixing[:, 1:2] * expert_out
    grad_out = cotangent.astype(jnp.float32)
    mix_grad = jnp.stack(
        [jnp.sum(grad_out * dense_out, axis=-1), jnp.sum(grad_out * expert_out, axis=-1)], axis=-1
    )
    logit_grad = (mixing * (mix_grad - jnp.sum(mixing * mix_grad, axis=-1, keepdims=True))).astype(
        jnp.bfloat16
    )
    mix_weight_grad = jnp.einsum(
        "td,tk->dk", mid_low, logit_grad, preferred_element_type=jnp.float32
    )
    dense_grad = (mixing[:, 0:1] * grad_out).astype(jnp.bfloat16)
    down_weight_grad = jnp.einsum(
        "tf,td->fd", dense_act, dense_grad, preferred_element_type=jnp.float32
    )
    dense_act_grad = jnp.einsum(
        "td,fd->tf", dense_grad, down_full, preferred_element_type=jnp.float32
    )
    dense_pre_grad = gelu_backward(dense_pre, dense_act_grad).astype(jnp.bfloat16)
    up_weight_grad = jnp.einsum(
        "td,tf->df", mid_low, dense_pre_grad, preferred_element_type=jnp.float32
    )
    mid_grad = jnp.einsum("tf,df->td", dense_pre_grad, up_full, preferred_element_type=jnp.float32)
    mid_grad = mid_grad + jnp.einsum(
        "tk,dk->td", logit_grad, mix_weight, preferred_element_type=jnp.float32
    )
    expert_grad = (mixing[:, 1:2] * grad_out).astype(jnp.bfloat16)
    sent_grad = jnp.einsum(
        "tk,td->kd", table_flat, expert_grad, preferred_element_type=jnp.float32
    ).astype(jnp.bfloat16)
    arrived_grad = lax.all_to_all(
        sent_grad.reshape(experts, capacity, -1), "ep", split_axis=0, concat_axis=1, tiled=True
    )
    slot_grad = lax.all_gather(arrived_grad, "dp", axis=1, tiled=True)
    expert_act_grad = jnp.einsum(
        "erd,efd->erf", slot_grad, expert_down, preferred_element_type=jnp.float32
    )
    expert_pre_grad = gelu_backward(expert_pre, expert_act_grad).astype(jnp.bfloat16)
    expert_down_grad = jnp.einsum(
        "erf,erd->efd", expert_act, slot_grad, preferred_element_type=jnp.float32
    )
    expert_up_grad = jnp.einsum(
        "erd,erf->edf", slot_rows, expert_pre_grad, preferred_element_type=jnp.float32
    )
    partial_in = jnp.einsum(
        "erf,edf->erd", expert_pre_grad, expert_up, preferred_element_type=jnp.float32
    )
    summed_in = lax.psum_scatter(
        partial_in.astype(jnp.bfloat16), "dp", scatter_dimension=1, tiled=True
    )
    back_rows = lax.all_to_all(summed_in, "ep", split_axis=1, concat_axis=0, tiled=True)
    mid_grad = mid_grad + jnp.dot(
        table_flat, back_rows.reshape(experts * capacity, -1), preferred_element_type=jnp.float32
    )
    unused_mid, mid_pull = jax.vjp(layer_norm, hidden_res, ln2_gain)
    res_part, ln2_gain_grad = mid_pull(mid_grad)
    res_grad = grad_out + res_part
    attn_out_grad = res_grad.astype(jnp.bfloat16)
    out_weight_grad = jnp.einsum(
        "td,te->de", attended, attn_out_grad, preferred_element_type=jnp.float32
    )
    attended_grad = jnp.einsum(
        "te,de->td", attn_out_grad, out_full, preferred_element_type=jnp.float32
    ).astype(jnp.bfloat16)
    qkv_grad = attention_backward(qkv_rows, allowed, log_total, attended_grad)
    qkv_weight_grad = jnp.einsum(
        "td,tk->dk", normed_in, qkv_grad, preferred_element_type=jnp.float32
    )
    normed_grad = jnp.einsum("tk,dk->td", qkv_grad, qkv_full, preferred_element_type=jnp.float32)
    unused_in, in_pull = jax.vjp(layer_norm, token_rows, ln1_gain)
    token_part, ln1_gain_grad = in_pull(normed_grad)
    tokens_grad = res_grad + token_part
    batch_sums = (
        lax.psum_scatter(
            qkv_weight_grad.astype(jnp.bfloat16), "ep", scatter_dimension=0, tiled=True
        ).astype(jnp.float32),
        lax.psum_scatter(
            out_weight_grad.astype(jnp.bfloat16), "ep", scatter_dimension=0, tiled=True
        ).astype(jnp.float32),
        lax.psum_scatter(
            up_weight_grad.astype(jnp.bfloat16), "ep", scatter_dimension=0, tiled=True
        ).astype(jnp.float32),
        lax.psum_scatter(
            down_weight_grad.astype(jnp.bfloat16), "ep", scatter_dimension=0, tiled=True
        ).astype(jnp.float32),
    )
    dense_shards = (
        lax.psum(batch_sums[0].astype(jnp.bfloat16), "dp").astype(jnp.float32),
        lax.psum(batch_sums[1].astype(jnp.bfloat16), "dp").astype(jnp.float32),
        lax.psum(batch_sums[2].astype(jnp.bfloat16), "dp").astype(jnp.float32),
        lax.psum(batch_sums[3].astype(jnp.bfloat16), "dp").astype(jnp.float32),
    )
    small_sums = lax.psum((ln1_gain_grad, ln2_gain_grad, mix_weight_grad), ("dp", "ep"))
    return (
        result.astype(jnp.bfloat16),
        tokens_grad,
        small_sums[0],
        dense_shards[0],
        dense_shards[1],
        small_sums[1],
        dense_shards[2],
        dense_shards[3],
        small_sums[2],
        expert_up_grad,
        expert_down_grad,
    )


def solution(mesh):
    placed = (
        P(("dp", "ep"), None),
        P(("dp", "ep")),
        P(("dp", "ep"), None),
        P(),
        P("ep", None),
        P("ep", None),
        P(),
        P("ep", None),
        P("ep", None),
        P(),
        P("ep", None, "dp"),
        P("ep", "dp", None),
        P(("dp", "ep"), None),
    )
    return jax.shard_map(
        on_device,
        mesh=mesh,
        in_specs=placed,
        out_specs=(
            P(("dp", "ep"), None),
            P(("dp", "ep"), None),
            P(),
            P("ep", None),
            P("ep", None),
            P(),
            P("ep", None),
            P("ep", None),
            P(),
            P("ep", None, "dp"),
            P("ep", "dp", None),
        ),
        check_vma=False,
    )
```

profile of v0, /device:TPU:0, one launch (start us, length us, event | category | flops | bytes accessed | tf_op | source)
XLA Modules:
  0.0 1117.8 jit_solution(12316198265122830779)
XLA Ops:
  17.8 40.4 %all-gather.7.cloned.1.call-done = bf16[1024,3072]{1,0:T(8,128)(2,1)} async-done(((bf16[128,3072]{1,0:T(8,128)(2,1)}), bf16[1024,3072]{1,0:T(8,128)(2,1)}) %all-gather.7.cloned.1.call-update) | async-done | bytes 6291472 | tf_op jit(solution)/shard_map/all_gather | solution.py:103
  70.8 10.1 fusion.99
  80.9 8.4 fusion
  89.3 10.1 fusion.56
  105.2 21.3 %all_to_all.42 = bf16[8,80,1024]{2,1,0:T(8,128)(2,1)} all-to-all(bf16[8,80,1024]{2,1,0:T(8,128)(2,1)S(1)} %bitcast.156), channel_id=1, replica_groups=mesh['dp'=4,'ep'=8] {'ep'}, dimensions={0} | all-to-all | bytes 2621440 | tf_op jit(solution)/shard_map/all_to_all | solution.py:136
  126.5 97.3 %all-gather.15.cloned.1.call-done = bf16[1,2560,1024]{2,1,0:T(8,128)(2,1)} async-done(((bf16[1,640,1024]{2,1,0:T(8,128)(2,1)}), bf16[1,2560,1024]{2,1,0:T(8,128)(2,1)}) %all-gather.15.cloned.1.call-update) | async-done | bytes 5242896 | tf_op jit(solution)/shard_map/all_gather | solution.py:139
  223.8 8.6 fusion.28
  246.3 90.7 %reduce-scatter.7.cloned.1.call-done = bf16[1,640,1024]{2,1,0:T(8,128)(2,1)} async-done(((bf16[1,2560,1024]{2,1,0:T(8,128)(2,1)}), bf16[1,640,1024]{2,1,0:T(8,128)(2,1)}) %reduce-scatter.7.cloned.1.call-update) | async-done | bytes 1310736 | tf_op jit(solution)/shard_map/reduce_scatter | solution.py:147
  342.3 10.7 reduce.2
  361.9 41.4 %all-gather.11.cloned.1.call-done = bf16[1024,4096]{1,0:T(8,128)(2,1)} async-done(((bf16[128,4096]{1,0:T(8,128)(2,1)}), bf16[1024,4096]{1,0:T(8,128)(2,1)}) %all-gather.11.cloned.1.call-update) | async-done | bytes 8388624 | tf_op jit(solution)/shard_map/all_gather | solution.py:105
  403.4 10.0 fusion.104
  423.9 35.3 %all-gather.13.cloned.1.call-done = bf16[4096,1024]{1,0:T(8,128)(2,1)} async-done(((bf16[512,1024]{1,0:T(8,128)(2,1)}), bf16[4096,1024]{1,0:T(8,128)(2,1)}) %all-gather.13.cloned.1.call-update) | async-done | bytes 8388624 | tf_op jit(solution)/shard_map/all_gather | solution.py:106
  459.1 13.3 %fusion.49 = (f32[512]{0:T(512)S(1)}, f32[512]{0:T(512)S(1)}, f32[512,1024]{1,0:T(8,128)}) fusion(bf16[512,1024]{1,0:T(8,128)(2,1)} %param.25, f32[512,1024]{1,0:T(8,128)} %fusion.68, bf16[4096,1024]{1,0:T(8,128)(2,1)} %all-gather.13.cloned.1.call-done, f32[512,4096]{1,0:T(8,128)} %fusion.104), kind=kOutput, calls=%fused_computation.71 | convolution fusion | flops 4316462080 | bytes 22024192 | tf_op jit(solution)/shard_map/dot_general | solution.py:122
  473.5 21.3 %all_to_all.43 = bf16[8,80,1024]{2,1,0:T(8,128)(2,1)} all-to-all(bf16[8,80,1024]{2,1,0:T(8,128)(2,1)S(1)} %bitcast.157), channel_id=1, replica_groups=mesh['dp'=4,'ep'=8] {'ep'}, dimensions={0} | all-to-all | bytes 2621440 | tf_op jit(solution)/shard_map/all_to_all | solution.py:184
  495.1 97.0 %all-gather.17.cloned.1.call-done = bf16[1,2560,1024]{2,1,0:T(8,128)(2,1)} async-done(((bf16[1,640,1024]{2,1,0:T(8,128)(2,1)}), bf16[1,2560,1024]{2,1,0:T(8,128)(2,1)}) %all-gather.17.cloned.1.call-update) | async-done | bytes 5242896 | tf_op jit(solution)/shard_map/all_gather | solution.py:187
  592.1 14.9 %fusion.8 = bf16[2560,1024]{1,0:T(8,128)(2,1)S(1)} fusion(f32[2560,1024]{1,0:T(8,128)} %copy-done.41, bf16[1,2560,1024]{2,1,0:T(8,128)(2,1)} %all-gather.17.cloned.1.call-done, bf16[1,1024,1024]{2,1,0:T(8,128)(2,1)S(1)} %copy-done), kind=kOutput, calls=%fused_computation.18 | convolution fusion | flops 5421137920 | bytes 23068672 | tf_op jit(solution)/shard_map/erd,efd->erf/dot_general | solution.py:188
  618.4 10.3 convolution_convert_fusion
  629.0 12.5 %fusion.15 = bf16[512,4096]{1,0:T(8,128)(2,1)S(1)} fusion(f32[512,4096]{1,0:T(8,128)} %fusion.104, bf16[4096,1024]{1,0:T(8,128)(2,1)} %all-gather.13.cloned.1.call-done, bf16[512,1024]{1,0:T(8,128)(2,1)S(1)} %copy-done.13, f32[512]{0:T(512)S(1)} %bitcast.170), kind=kOutput, calls=%fused_computation.26 | convolution fusion | flops 4338483200 | bytes 22022144 | tf_op jit(solution)/shard_map/td,fd->tf/dot_general | solution.py:169
  652.9 56.6 %reduce-scatter.9.cloned.1.call-done = bf16[1,640,1024]{2,1,0:T(8,128)(2,1)} async-done(((bf16[1,2560,1024]{2,1,0:T(8,128)(2,1)}), bf16[1,640,1024]{2,1,0:T(8,128)(2,1)}) %reduce-scatter.9.cloned.1.call-update) | async-done | bytes 1310736 | tf_op jit(solution)/shard_map/reduce_scatter | solution.py:201
  714.4 9.6 reduce.3
  730.3 10.6 fusion.105
  740.9 14.5 %all-to-all-done.3 = bf16[8,2,40960]{2,1,0:T(2,128)(2,1)} async-done(((bf16[8,2,40960]{2,1,0:T(2,128)(2,1)}), bf16[8,2,40960]{2,1,0:T(2,128)(2,1)}, u32[]{:S(2)}, u32[]{:S(2)}) %all-to-all-start.3) | async-done | bytes 1310752 | tf_op jit(solution)/shard_map/all_to_all | solution.py:204
  780.1 11.5 %multiply_reduce_fusion = (f32[16,512]{1,0:T(8,128)S(1)}, f32[16,512,512]{1,2,0:T(8,128)}) fusion(f32[16,512,512]{1,2,0:T(8,128)} %get-tuple-element.32, f32[16,512]{1,0:T(8,128)S(1)} %log_add_fusion, bf16[512,16,64]{0,2,1:T(8,128)(2,1)S(1)} %bitcast.144, bf16[512,3,16,64]{0,3,2,1:T(8,128)(2,1)} %bitcast.139), kind=kOutput, calls=%fused_computation.1 | convolution fusion | flops 549445632 | bytes 35717120 | tf_op jit(solution)/shard_map/qhd,khd->hqk/dot_general | solution.py:60
  791.6 12.9 %multiply_convert_fusion = bf16[16,512,512]{1,2,0:T(8,128)(2,1)S(1)} fusion(f32[16,512,512]{1,2,0:T(8,128)} %get-tuple-element.40, f32[16,512,512]{1,2,0:T(8,128)} %get-tuple-element.32, f32[16,512]{1,0:T(8,128)S(1)} %get-tuple-element.39, f32[16,512]{1,0:T(8,128)S(1)} %log_add_fusion), kind=kLoop, calls=%fused_computation | loop fusion | flops 16777216 | bytes 42008576 | tf_op jit(solution)/shard_map/convert_element_type | solution.py:64
  809.0 9.0 fusion.62
  826.7 10.7 fusion.41
  837.4 28.6 %reduce-scatter.15.cloned.1.call-done = bf16[128,4096]{1,0:T(8,128)(2,1)} async-done(((bf16[1024,4096]{1,0:T(8,128)(2,1)}), bf16[128,4096]{1,0:T(8,128)(2,1)}) %reduce-scatter.15.cloned.1.call-update) | async-done | bytes 1048592 | tf_op jit(solution)/shard_map/reduce_scatter | solution.py:233
  866.0 45.1 %reduce-scatter.13.cloned.1.call-done = bf16[128,1024]{1,0:T(8,128)(2,1)} async-done(((bf16[1024,1024]{1,0:T(8,128)(2,1)}), bf16[128,1024]{1,0:T(8,128)(2,1)}) %reduce-scatter.13.cloned.1.call-update) | async-done | bytes 262160 | tf_op jit(solution)/shard_map/reduce_scatter | solution.py:230
  911.1 65.4 %reduce-scatter.11.cloned.1.call-done = bf16[128,3072]{1,0:T(8,128)(2,1)} async-done(((bf16[1024,3072]{1,0:T(8,128)(2,1)}), bf16[128,3072]{1,0:T(8,128)(2,1)}) %reduce-scatter.11.cloned.1.call-update) | async-done | bytes 786448 | tf_op jit(solution)/shard_map/reduce_scatter | solution.py:227
  976.5 11.6 %fusion.38 = f32[1,1024,1024]{2,1,0:T(8,128)} fusion(bf16[1,2560,1024]{2,1,0:T(8,128)(2,1)} %all-gather.17.cloned.1.call-done, f32[2560,1024]{1,0:T(8,128)} %copy-done.41), kind=kOutput, calls=%fused_computation.64 | convolution fusion | flops 5392302080 | bytes 19922944 | tf_op jit(solution)/shard_map/erf,erd->efd/dot_general | solution.py:192
  996.5 42.8 %all-reduce = (f32[1024]{0:T(1024)}, f32[1024]{0:T(1024)}, f32[1024,2]{0,1:T(2,128)}) all-reduce(f32[1024]{0:T(1024)S(1)} %get-tuple-element.13, f32[1024]{0:T(1024)S(1)} %get-tuple-element.11, f32[1024,2]{0,1:T(2,128)S(1)} %fusion.102), channel_id=1, replica_groups=mesh['dp'=4,'ep'=8] {'dp','ep'}, use_global_device_ids=true, to_apply=%region_22.23 | all-reduce | flops 4096 | bytes 32768 | tf_op jit(solution)/shard_map/psum | solution.py:246
  1043.8 58.4 %all-reduce.4.cloned.1.call-done = (bf16[128,3072]{1,0:T(8,128)(2,1)}, bf16[128,1024]{1,0:T(8,128)(2,1)}, bf16[128,4096]{1,0:T(8,128)(2,1)}, bf16[512,1024]{1,0:T(8,128)(2,1)}) async-done(((bf16[128,3072]{1,0:T(8,128)(2,1)}, bf16[128,1024]{1,0:T(8,128)(2,1)}, bf16[128,4096]{1,0:T(8,128)(2,1)}, bf16[512,1024]{1,0:T(8,128)(2,1)}), (bf16[128,3072]{1,0:T(8,128)(2,1)}, bf16[128,1024]{1,0:T(8,128)(2,1)}, ...) | async-done | bytes 3145744 | tf_op jit(solution)/shard_map/psum | solution.py:241
  (180 shorter events, 161.5 us)
Async XLA Ops:
  7.2 229.2 %copy-start = (bf16[1,1024,1024]{2,1,0:T(8,128)(2,1)S(1)}, bf16[1,1024,1024]{2,1,0:T(8,128)(2,1)}, u32[]{:S(2)}) copy-start(bf16[1,1024,1024]{2,1,0:T(8,128)(2,1)} %param.24) | copy-start | bytes 6291460
  7.2 51.0 %copy-start.5 = (bf16[512,1024]{1,0:T(8,128)(2,1)S(1)}, bf16[512,1024]{1,0:T(8,128)(2,1)}, u32[]{:S(2)}) copy-start(bf16[512,1024]{1,0:T(8,128)(2,1)} %param.13) | copy-start | bytes 3145732
  7.2 51.0 %copy-start.36 = (f32[1024]{0:T(1024)S(1)}, f32[1024]{0:T(1024)}, u32[]{:S(2)}) copy-start(f32[1024]{0:T(1024)} %param.16) | copy-start | bytes 12292
  7.2 51.0 %all-gather.7.cloned.1.call-start = ((), (), s32[]{:S(2)}) async-start(), calls=%async_computation.10 | async-start | bytes 7077888 | tf_op jit(solution)/shard_map/all_gather | solution.py:103
  8.0 91.4 %all-gather.9.cloned.1.call-start = ((), (), s32[]{:S(2)}) async-start(), calls=%async_computation.11 | async-start | bytes 2359296 | tf_op jit(solution)/shard_map/all_gather | solution.py:104
  8.7 215.1 %all-gather.15.cloned.1.call-start = ((), (), s32[]{:S(2)}) async-start(), calls=%async_computation.14 | async-start | bytes 6553600 | tf_op jit(solution)/shard_map/all_gather | solution.py:139
  10.9 55.1 %copy-start.26 = (f32[512]{0:T(512)}, f32[512]{0:T(512)S(1)}, u32[]{:S(2)}) copy-start(f32[512]{0:T(512)S(1)} %broadcast_multiply_fusion.1) | copy-start | bytes 6148
  12.5 53.4 %copy-start.30 = (f32[512]{0:T(512)}, f32[512]{0:T(512)S(1)}, u32[]{:S(2)}) copy-start(f32[512]{0:T(512)S(1)} %fusion.90) | copy-start | bytes 6148
  103.1 23.4 %copy-start.34 = (f32[512]{0:T(512)}, f32[512]{0:T(512)S(1)}, u32[]{:S(2)}) copy-start(f32[512]{0:T(512)S(1)} %multiply_reduce_fusion.3) | copy-start | bytes 6148
  103.1 23.4 %copy-start.28 = (f32[512]{0:T(512)}, f32[512]{0:T(512)S(1)}, u32[]{:S(2)}) copy-start(f32[512]{0:T(512)S(1)} %fusion.91) | copy-start | bytes 6148
  126.5 210.5 %reduce-scatter.7.cloned.1.call-start = ((), (), s32[]{:S(2)}) async-start(), calls=%async_computation.15 | async-start | bytes 6553600 | tf_op jit(solution)/shard_map/reduce_scatter | solution.py:147
  244.7 158.7 %all-gather.11.cloned.1.call-start = ((), (), s32[]{:S(2)}) async-start(), calls=%async_computation.12 | async-start | bytes 9437184 | tf_op jit(solution)/shard_map/all_gather | solution.py:105
  245.3 213.9 %all-gather.13.cloned.1.call-start = ((), (), s32[]{:S(2)}) async-start(), calls=%async_computation.13 | async-start | bytes 9437184 | tf_op jit(solution)/shard_map/all_gather | solution.py:106
  357.4 56.0 %all-to-all-start.1 = ((bf16[8,2,40960]{2,1,0:T(2,128)(2,1)}), bf16[8,2,40960]{2,1,0:T(2,128)(2,1)}, u32[]{:S(2)}, u32[]{:S(2)}) async-start(bf16[8,2,40960]{2,1,0:T(2,128)(2,1)} %reshape.349), calls=%async_computation.2 | async-start | bytes 2621440 | tf_op jit(solution)/shard_map/all_to_all | solution.py:150
  361.7 230.4 %all-gather.17.cloned.1.call-start = ((), (), s32[]{:S(2)}) async-start(), calls=%async_computation.16 | async-start | bytes 6553600 | tf_op jit(solution)/shard_map/all_gather | solution.py:187
  459.1 13.4 %copy-start.11 = (bf16[512,8,80]{0,2,1:T(8,128)(2,1)S(1)}, bf16[512,8,80]{0,2,1:T(8,128)(2,1)}, u32[]{:S(2)}) copy-start(bf16[512,8,80]{0,2,1:T(8,128)(2,1)} %multiply_convert_fusion.6) | copy-start | bytes 1966084
  459.1 13.4 %copy-start.12 = (bf16[512,1024]{1,0:T(8,128)(2,1)S(1)}, bf16[512,1024]{1,0:T(8,128)(2,1)}, u32[]{:S(2)}) copy-start(bf16[512,1024]{1,0:T(8,128)(2,1)} %param.25) | copy-start | bytes 3145732
  494.8 214.6 %reduce-scatter.9.cloned.1.call-start = ((), (), s32[]{:S(2)}) async-start(), calls=%async_computation.17 | async-start | bytes 6553600 | tf_op jit(solution)/shard_map/reduce_scatter | solution.py:201
  592.1 17.3 %copy-start.39 = (bf16[1,1024,1024]{2,1,0:T(8,128)(2,1)S(1)}, bf16[1,1024,1024]{2,1,0:T(8,128)(2,1)}, u32[]{:S(2)}) copy-start(bf16[1,1024,1024]{2,1,0:T(8,128)(2,1)} %param.23) | copy-start | bytes 6291460
  617.2 220.2 %reduce-scatter.17.cloned.1.call-start = ((), (), s32[]{:S(2)}) async-start(), calls=%async_computation.21 | async-start | bytes 9437184 | tf_op jit(solution)/shard_map/reduce_scatter | solution.py:236
  628.7 237.3 %reduce-scatter.15.cloned.1.call-start = ((), (), s32[]{:S(2)}) async-start(), calls=%async_computation.20 | async-start | bytes 9437184 | tf_op jit(solution)/shard_map/reduce_scatter | solution.py:233
  725.8 29.6 %all-to-all-start.3 = ((bf16[8,2,40960]{2,1,0:T(2,128)(2,1)}), bf16[8,2,40960]{2,1,0:T(2,128)(2,1)}, u32[]{:S(2)}, u32[]{:S(2)}) async-start(bf16[8,2,40960]{2,1,0:T(2,128)(2,1)} %reshape.351), calls=%async_computation.5 | async-start | bytes 2621440 | tf_op jit(solution)/shard_map/all_to_all | solution.py:204
  730.1 31.5 %copy-start.23 = (f32[512]{0:T(512)S(1)}, f32[512]{0:T(512)}, u32[]{:S(2)}) copy-start(f32[512]{0:T(512)} %copy-done.22) | copy-start | bytes 6148
  730.1 31.5 %copy-start.25 = (f32[1024]{0:T(1024)S(1)}, f32[1024]{0:T(1024)}, u32[]{:S(2)}) copy-start(f32[1024]{0:T(1024)} %param.19) | copy-start | bytes 12292
  730.1 31.5 %copy-start.29 = (f32[512]{0:T(512)S(1)}, f32[512]{0:T(512)}, u32[]{:S(2)}) copy-start(f32[512]{0:T(512)} %copy-done.28) | copy-start | bytes 6148
  730.1 181.0 %reduce-scatter.13.cloned.1.call-start = ((), (), s32[]{:S(2)}) async-start(), calls=%async_computation.19 | async-start | bytes 2359296 | tf_op jit(solution)/shard_map/reduce_scatter | solution.py:230
  740.9 20.7 %copy-start.3 = (f32[512,1024]{1,0:T(8,128)S(1)}, f32[512,1024]{1,0:T(8,128)}, u32[]{:S(2)}) copy-start(f32[512,1024]{1,0:T(8,128)} %copy-done.2) | copy-start | bytes 6291460
  779.8 196.7 %reduce-scatter.11.cloned.1.call-start = ((), (), s32[]{:S(2)}) async-start(), calls=%async_computation.18 | async-start | bytes 7077888 | tf_op jit(solution)/shard_map/reduce_scatter | solution.py:227
  791.6 13.2 %copy-start.4 = (bf16[512,3072]{0,1:T(8,128)(2,1)S(1)}, bf16[512,3072]{0,1:T(8,128)(2,1)}, u32[]{:S(2)}) copy-start(bf16[512,3072]{0,1:T(8,128)(2,1)} %copy.47) | copy-start | bytes 9437188
  826.1 276.0 %all-reduce.4.cloned.1.call-start = ((), (), s32[]{:S(2)}) async-start(), calls=%async_computation.22 | async-start | bytes 6291456 | tf_op jit(solution)/shard_map/psum | solution.py:241
  976.5 11.6 %copy-start.17 = (bf16[512,3,16,64]{0,3,2,1:T(8,128)(2,1)S(1)}, bf16[512,3,16,64]{0,3,2,1:T(8,128)(2,1)}, u32[]{:S(2)}) copy-start(bf16[512,3,16,64]{0,3,2,1:T(8,128)(2,1)} %copy-done.16) | copy-start | bytes 9437188
  988.1 51.2 %copy-start.15 = (bf16[512,1024]{1,0:T(8,128)(2,1)S(1)}, bf16[512,1024]{1,0:T(8,128)(2,1)}, u32[]{:S(2)}) copy-start(bf16[512,1024]{1,0:T(8,128)(2,1)} %param.25) | copy-start | bytes 3145732
  (26 other events, 76.5 us)
Sparse Core Ops, SparseCore 0:
  9.9 48.2 all-gather.6
  60.1 27.8 all-gather.8
  126.6 97.1 all-gather.14
  244.8 92.1 reduce-scatter.6
  338.7 64.6 all-gather.10
  405.1 53.9 all-gather.12
  494.9 97.1 all-gather.16
  617.3 92.1 reduce-scatter.8
  712.9 78.0 reduce-scatter.16
  794.7 71.2 reduce-scatter.14
  869.9 41.1 reduce-scatter.12
  914.7 61.7 reduce-scatter.10
  979.1 123.0 all-reduce.3
where the time goes:
time: 1120 us
  waiting for transfers between devices  673 us (60%)
  matrix products  214 us (19%)
  blocking collectives  85.4 us (8%)
  other arithmetic  67 us (6%)
  local copies, waits for them, and re-layouts  52 us (5%)
  between operations  15.4 us (1%)
    all_gather x1, waiting for transfers between devices, on_device(): slot_rows = lax.all_gather(arrived, 'dp', axis=1, tiled=True)  97.3 us
    all_gather x1, waiting for transfers between devices, on_device(): slot_grad = lax.all_gather(arrived_grad, 'dp', axis=1, tiled=True)  97 us
    reduce_scatter x1, waiting for transfers between devices, on_device(): lax.psum_scatter(partial_out.astype(jnp.bfloat16), 'dp', scatter_dimensio...  90.7 us
    reduce_scatter x1, waiting for transfers between devices, on_device(): lax.psum_scatter(qkv_weight_grad.astype(jnp.bfloat16), 'ep', scatter_dime...  65.4 us
    psum x1, waiting for transfers between devices, on_device(): lax.psum(batch_sums[0].astype(jnp.bfloat16), 'dp').astype(jnp.float32)  58.4 us
    reduce_scatter x1, waiting for transfers between devices, on_device(): lax.psum_scatter(partial_in.astype(jnp.bfloat16), 'dp', scatter_dimension...  56.6 us
    reduce_scatter x1, waiting for transfers between devices, on_device(): lax.psum_scatter(out_weight_grad.astype(jnp.bfloat16), 'ep', scatter_dime...  45.1 us
    psum x1, blocking collectives, on_device(): lax.psum((ln1_gain_grad, ln2_gain_grad, mix_weight_grad), ('dp', 'ep'))  42.8 us
  transfers between devices with their start and end apart: 15, of which 12 were waited for; matrix products, arithmetic and copies ran while one was open for 22% of the time, Pallas kernels for 0%

commit v1 on v0

v1 whole, which is shorter than its diff:
```python
import functools

import jax
import jax.numpy as jnp
from jax import lax
from jax.experimental import pallas as pl
from jax.experimental.pallas import tpu as pltpu
from jax.sharding import PartitionSpec as P

HEAD = 64
SHORT_SEQS = 4
PAIR = 2 * HEAD
NEG = -1e30
ROOT = 0.7978845608028654
CUBE = 0.044715
F32 = jnp.float32
BF16 = jnp.bfloat16


def dot_nn(a, b):
    return lax.dot_general(a, b, (((1,), (0,)), ((), ())), preferred_element_type=F32)


def dot_nt(a, b):
    return lax.dot_general(a, b, (((1,), (1,)), ((), ())), preferred_element_type=F32)


def dot_tn(a, b):
    return lax.dot_general(a, b, (((0,), (0,)), ((), ())), preferred_element_type=F32)


def gelu_pair(v):
    sq = v * v
    t = jnp.tanh(v * (ROOT + (ROOT * CUBE) * sq))
    half = 0.5 * (1.0 + t)
    slope = half + (0.5 * v) * (1.0 - t * t) * (ROOT + (3.0 * ROOT * CUBE) * sq)
    return v * half, slope


def params(vmem_mib):
    return pltpu.CompilerParams(vmem_limit_bytes=vmem_mib << 20)


def cost(flops, nbytes):
    return pl.CostEstimate(flops=int(flops), bytes_accessed=int(nbytes), transcendentals=0)


def allowed_block(flag, row0, rows, cols, short):
    r = row0 + lax.broadcasted_iota(jnp.int32, (rows, cols), 0)
    c = lax.broadcasted_iota(jnp.int32, (rows, cols), 1)
    shift = short.bit_length() - 1
    same = jnp.logical_or(flag == 1, lax.shift_right_logical(r, shift) == lax.shift_right_logical(c, shift))
    return jnp.logical_and(c <= r, same)


def attn_fwd_kernel(tile, flag_ref, q_ref, k_ref, v_ref, o_ref, lse_ref):
    length = q_ref.shape[0]
    flag = flag_ref[0]
    lane = lax.broadcasted_iota(jnp.int32, (1, PAIR), 1)
    first = lane < HEAD
    scale = HEAD ** (-0.5)
    for row0 in range(0, length, tile):
        cols = row0 + tile
        ok = allowed_block(flag, row0, tile, cols, length // SHORT_SEQS)
        q = q_ref[row0 : row0 + tile, :]
        k = k_ref[0:cols, :]
        v = v_ref[0:cols, :]
        outs, lses = [], []
        for h in range(2):
            qh = jnp.where(first if h == 0 else jnp.logical_not(first), q, jnp.zeros_like(q))
            s = jnp.where(ok, dot_nt(qh, k) * scale, NEG)
            peak = jnp.max(s, axis=-1, keepdims=True)
            p = jnp.exp(s - peak)
            total = jnp.sum(p, axis=-1, keepdims=True)
            outs.append(dot_nn((p * (1.0 / total)).astype(BF16), v))
            lses.append(peak + jnp.log(total))
        o_ref[row0 : row0 + tile, :] = jnp.where(first, outs[0], outs[1]).astype(BF16)
        lse_ref[row0 : row0 + tile, :] = jnp.where(first, lses[0], lses[1])


def attention_forward(qkv, flag, tile=256):
    length, width = qkv.shape[0], qkv.shape[1] // 3
    pairs = width // PAIR
    spec = lambda off: pl.BlockSpec((length, PAIR), lambda j: (0, off + j))
    return pl.pallas_call(
        functools.partial(attn_fwd_kernel, tile),
        grid=(pairs,),
        in_specs=[pl.BlockSpec(memory_space=pltpu.SMEM), spec(0), spec(pairs), spec(2 * pairs)],
        out_specs=[spec(0), spec(0)],
        out_shape=[jax.ShapeDtypeStruct((length, width), BF16), jax.ShapeDtypeStruct((length, width), F32)],
        compiler_params=params(32),
        cost_estimate=cost(8 * length * length * width, 10 * length * width),
        name="attn_fwd",
    )(flag, qkv, qkv, qkv)


def attn_bwd_kernel(tile, flag_ref, q_ref, k_ref, v_ref, g_ref, lse_ref, o_ref):
    length = q_ref.shape[0]
    width = o_ref.shape[1] // 3
    flag = flag_ref[0]
    lane = lax.broadcasted_iota(jnp.int32, (1, PAIR), 1)
    first = lane < HEAD
    scale = HEAD ** (-0.5)
    starts = list(range(0, length, tile))
    dk = [None] * len(starts)
    dv = [None] * len(starts)
    col = pl.multiple_of(pl.program_id(0) * PAIR, PAIR)
    for i, row0 in enumerate(starts):
        cols = row0 + tile
        ok = allowed_block(flag, row0, tile, cols, length // SHORT_SEQS)
        q = q_ref[row0 : row0 + tile, :]
        g = g_ref[row0 : row0 + tile, :]
        lse = lse_ref[row0 : row0 + tile, :]
        k = k_ref[0:cols, :]
        v = v_ref[0:cols, :]
        dqs, dks, dvs = [], [], []
        for h in range(2):
            mine = first if h == 0 else jnp.logical_not(first)
            qh = jnp.where(mine, q, jnp.zeros_like(q))
            gh = jnp.where(mine, g, jnp.zeros_like(g))
            s = jnp.where(ok, dot_nt(qh, k) * scale, NEG)
            p = jnp.exp(s - lse[:, h * HEAD : h * HEAD + 1])
            dp = dot_nt(gh, v)
            centre = jnp.sum(p * dp, axis=-1, keepdims=True)
            ds = (p * (dp - centre)).astype(BF16)
            dqs.append(dot_nn(ds, k))
            dks.append(dot_tn(ds, qh))
            dvs.append(dot_tn(p.astype(BF16), gh))
        o_ref[row0 : row0 + tile, pl.ds(col, PAIR)] = (
            jnp.where(first, dqs[0], dqs[1]) * scale
        ).astype(BF16)
        dk_all = dks[0] + dks[1]
        dv_all = dvs[0] + dvs[1]
        for j in range(i + 1):
            part_k = dk_all[j * tile : (j + 1) * tile]
            part_v = dv_all[j * tile : (j + 1) * tile]
            dk[j] = part_k if dk[j] is None else dk[j] + part_k
            dv[j] = part_v if dv[j] is None else dv[j] + part_v
    for j, row0 in enumerate(starts):
        o_ref[row0 : row0 + tile, pl.ds(width + col, PAIR)] = (dk[j] * scale).astype(BF16)
        o_ref[row0 : row0 + tile, pl.ds(2 * width + col, PAIR)] = dv[j].astype(BF16)


def attention_backward(qkv, flag, grad, lse, tile=256):
    length, width = qkv.shape[0], qkv.shape[1] // 3
    pairs = width // PAIR
    spec = lambda off: pl.BlockSpec((length, PAIR), lambda j: (0, off + j))
    return pl.pallas_call(
        functools.partial(attn_bwd_kernel, tile),
        grid=(pairs,),
        in_specs=[
            pl.BlockSpec(memory_space=pltpu.SMEM),
            spec(0),
            spec(pairs),
            spec(2 * pairs),
            spec(0),
            spec(0),
        ],
        out_specs=pl.BlockSpec((length, 3 * width), lambda j: (0, 0)),
        out_shape=jax.ShapeDtypeStruct((length, 3 * width), BF16),
        compiler_params=params(40),
        cost_estimate=cost(20 * length * length * width, 20 * length * width),
        name="attn_bwd",
    )(flag, qkv, qkv, qkv, grad, lse)


def dense_kernel(mid_ref, dg_ref, up_ref, down_ref, out_ref, mg_ref, wu_ref, wd_ref):
    mid = mid_ref[...]
    dg = dg_ref[...]
    up = up_ref[...]
    down = down_ref[...]
    act, slope = gelu_pair(dot_nn(mid, up))
    act = act.astype(BF16)
    pg = (dot_nt(dg, down) * slope).astype(BF16)
    out = dot_nn(act, down)
    mg = dot_nt(pg, up)
    wu_ref[...] = dot_tn(mid, pg).astype(BF16)
    wd_ref[...] = dot_tn(act, dg).astype(BF16)

    @pl.when(pl.program_id(0) == 0)
    def _():
        out_ref[...] = out
        mg_ref[...] = mg

    @pl.when(pl.program_id(0) > 0)
    def _():
        out_ref[...] += out
        mg_ref[...] += mg


def dense_branch(mid, dg, up, down, tile=512):
    length, width = mid.shape
    ff = up.shape[1]
    whole = pl.BlockSpec((length, width), lambda j: (0, 0))
    cols = pl.BlockSpec((width, tile), lambda j: (0, j))
    rows = pl.BlockSpec((tile, width), lambda j: (j, 0))
    return pl.pallas_call(
        dense_kernel,
        grid=(ff // tile,),
        in_specs=[whole, whole, cols, rows],
        out_specs=[whole, whole, cols, rows],
        out_shape=[
            jax.ShapeDtypeStruct((length, width), F32),
            jax.ShapeDtypeStruct((length, width), F32),
            jax.ShapeDtypeStruct((width, ff), BF16),
            jax.ShapeDtypeStruct((ff, width), BF16),
        ],
        compiler_params=params(48),
        cost_estimate=cost(12 * length * width * ff, 8 * width * ff + 12 * length * width),
        name="dense_branch",
    )(mid, dg, up, down)


def expert_kernel(mid_ref, g_ref, mix_ref, up_ref, down_ref, po_ref, pi_ref, act_ref, pg_ref, eg_ref, dot_ref):
    mid = mid_ref[...]
    g = g_ref[...].astype(F32)
    logits = dot_nn(mid, mix_ref[...])
    share = 1.0 / (1.0 + jnp.exp(logits[:, 0:1] - logits[:, 1:2]))
    eg = (share * g).astype(BF16)
    eg_ref[...] = eg
    act, slope = gelu_pair(dot_nn(mid, up_ref[...]))
    act = act.astype(BF16)
    act_ref[...] = act
    pg = (dot_nt(eg, down_ref[...]) * slope).astype(BF16)
    pg_ref[...] = pg
    pi_ref[...] = dot_nt(pg, up_ref[...]).astype(BF16)
    po = dot_nn(act, down_ref[...])
    po_ref[...] = po.astype(BF16)
    dot_ref[...] = jnp.sum(po * g, axis=-1, keepdims=True)


def expert_chunk(mid, g, mix_pad, up, down, tile=320):
    rows, width = mid.shape
    hidden = up.shape[1]
    block = pl.BlockSpec((tile, width), lambda i: (i, 0))
    hblock = pl.BlockSpec((tile, hidden), lambda i: (i, 0))
    full = lambda a: pl.BlockSpec(a.shape, lambda i: (0, 0))
    return pl.pallas_call(
        expert_kernel,
        grid=(rows // tile,),
        in_specs=[block, block, full(mix_pad), full(up), full(down)],
        out_specs=[block, block, hblock, hblock, block, pl.BlockSpec((tile, 1), lambda i: (i, 0))],
        out_shape=[
            jax.ShapeDtypeStruct((rows, width), BF16),
            jax.ShapeDtypeStruct((rows, width), BF16),
            jax.ShapeDtypeStruct((rows, hidden), BF16),
            jax.ShapeDtypeStruct((rows, hidden), BF16),
            jax.ShapeDtypeStruct((rows, width), BF16),
            jax.ShapeDtypeStruct((rows, 1), F32),
        ],
        compiler_params=params(48),
        cost_estimate=cost(8 * rows * width * hidden, 14 * rows * width + 4 * width * hidden),
        name="expert_chunk",
    )(mid, g, mix_pad, up, down)


def expert_grad_kernel(count, *refs):
    mids, pgs, acts, egs = (refs[i * count : (i + 1) * count] for i in range(4))
    du_ref, dd_ref = refs[4 * count :]
    up_sum = dot_tn(mids[0][...], pgs[0][...])
    down_sum = dot_tn(acts[0][...], egs[0][...])
    for i in range(1, count):
        up_sum += dot_tn(mids[i][...], pgs[i][...])
        down_sum += dot_tn(acts[i][...], egs[i][...])
    du_ref[...] = up_sum
    dd_ref[...] = down_sum


def expert_weight_grads(mids, pgs, acts, egs, tile=256):
    count = len(mids)
    rows, width = mids[0].shape
    hidden = pgs[0].shape[1]
    full = lambda a: pl.BlockSpec(a.shape, lambda j: (0, 0))
    cols = lambda a: pl.BlockSpec((a.shape[0], tile), lambda j: (0, j))
    return pl.pallas_call(
        functools.partial(expert_grad_kernel, count),
        grid=(hidden // tile,),
        in_specs=[full(a) for a in mids]
        + [cols(a) for a in pgs]
        + [cols(a) for a in acts]
        + [full(a) for a in egs],
        out_specs=[
            pl.BlockSpec((width, tile), lambda j: (0, j)),
            pl.BlockSpec((tile, width), lambda j: (j, 0)),
        ],
        out_shape=[jax.ShapeDtypeStruct((width, hidden), F32), jax.ShapeDtypeStruct((hidden, width), F32)],
        compiler_params=params(48),
        cost_estimate=cost(4 * count * rows * width * hidden, 8 * count * rows * width + 8 * width * hidden),
        name="expert_weight_grads",
    )(*mids, *pgs, *acts, *egs)


def normalise(values_in):
    centred = values_in - jnp.mean(values_in, axis=-1, keepdims=True)
    inverse = lax.rsqrt(jnp.mean(centred * centred, axis=-1, keepdims=True) + 1e-05)
    return centred * inverse, inverse


def norm_backward(grad, gain_vec, unit, inverse):
    m = grad * gain_vec
    return inverse * (
        m
        - jnp.mean(m, axis=-1, keepdims=True)
        - unit * jnp.mean(m * unit, axis=-1, keepdims=True)
    )


def shifted(rows, step):
    size = lax.axis_size("dp")
    return lax.ppermute(rows, "dp", [((i + step) % size, i) for i in range(size)])


def on_device(
    tokens,
    bucket,
    expert_ids,
    ln1_gain,
    qkv_weight,
    out_weight,
    ln2_gain,
    up_weight,
    down_weight,
    mix_weight,
    expert_up,
    expert_down,
    cotangent,
):
    length, width = tokens.shape
    groups = lax.axis_size("ep")
    layers = lax.axis_size("dp")
    experts = groups * expert_up.shape[0]
    capacity = 5 * length // (4 * experts)
    slots = experts * capacity
    gather = lambda w: lax.all_gather(w, "ep", axis=0, tiled=True)
    exchange_out = lambda a: lax.all_to_all(a, "ep", split_axis=0, concat_axis=1, tiled=True)
    qkv_full, out_full, up_full, down_full = (
        gather(qkv_weight),
        gather(out_weight),
        gather(up_weight),
        gather(down_weight),
    )
    expert_up2 = expert_up[0]
    expert_down2 = expert_down[0]
    mix_pad = jnp.pad(mix_weight, ((0, 0), (0, 126)))

    chosen = expert_ids[:, 0]
    one_hot = chosen[:, None] == jnp.arange(experts, dtype=jnp.int32)[None, :]
    place = jnp.arange(length, dtype=jnp.int32)
    earlier = (place[None, :] < place[:, None]).astype(BF16)
    before = dot_nn(earlier, one_hot.astype(BF16))
    slot_index = jnp.sum(jnp.where(one_hot, before, 0.0), axis=1).astype(jnp.int32)
    target = jnp.where(slot_index < capacity, chosen * capacity + slot_index, -1)
    table = (target[:, None] == jnp.arange(slots, dtype=jnp.int32)[None, :]).astype(BF16)

    def dispatch(rows):
        sent = dot_tn(table, rows).astype(BF16)
        return exchange_out(sent.reshape(experts, capacity, width)).reshape(groups * capacity, width)

    g_own = dispatch(cotangent)
    gs = [g_own] + [shifted(g_own, k) for k in range(1, layers)]

    token_rows = tokens.astype(F32)
    unit1, inverse1 = normalise(token_rows)
    normed_in = (unit1 * ln1_gain).astype(BF16)
    qkv_rows = dot_nn(normed_in, qkv_full).astype(BF16)
    attended, lse = attention_forward(qkv_rows, bucket)
    hidden_res = token_rows + dot_nn(attended, out_full)
    unit2, inverse2 = normalise(hidden_res)
    mid_low = (unit2 * ln2_gain).astype(BF16)
    mid_own = dispatch(mid_low)
    mids = [mid_own] + [shifted(mid_own, k) for k in range(1, layers)]

    grad_out = cotangent.astype(F32)
    logits = dot_nn(mid_low, mix_weight)
    mix1 = 1.0 / (1.0 + jnp.exp(logits[:, 0:1] - logits[:, 1:2]))
    mix0 = 1.0 / (1.0 + jnp.exp(logits[:, 1:2] - logits[:, 0:1]))
    dense_grad = (mix0 * grad_out).astype(BF16)
    dense_out, mid_grad_dense, up_grad, down_grad = dense_branch(mid_low, dense_grad, up_full, down_full)

    chunks = [
        expert_chunk(mids[k], gs[k], mix_pad, expert_up2, expert_down2) for k in range(layers)
    ]
    back = lambda k, a: shifted(a, layers - k) if k else a
    ins = [back(k, chunks[k][1]) for k in range(layers)]
    dots = [back(k, chunks[k][5].reshape(groups, capacity)) for k in range(layers)]
    outs = [back(k, chunks[k][0]) for k in range(layers)]
    expert_up_grad, expert_down_grad = expert_weight_grads(
        mids, [c[3] for c in chunks], [c[2] for c in chunks], [c[4] for c in chunks]
    )

    def total(parts):
        acc = parts[0].astype(F32)
        for part in parts[1:]:
            acc = acc + part.astype(F32)
        return acc

    dot_sum = total(dots)
    dot_high = lax.reduce_precision(dot_sum, 8, 7)
    dot_low = dot_sum - dot_high
    extra = jnp.stack([dot_high, dot_low], axis=1)
    extra = jnp.pad(extra, ((0, 0), (0, 14), (0, width - capacity)))
    in_sum = total(ins).reshape(groups, capacity, width)
    packed = jnp.concatenate([in_sum, extra], axis=1).astype(BF16)
    returned = lax.all_to_all(packed, "ep", split_axis=0, concat_axis=0, tiled=True)
    in_rows = returned[:, :capacity].reshape(slots, width)
    dot_back = (
        returned[:, capacity, :capacity].astype(F32) + returned[:, capacity + 1, :capacity].astype(F32)
    ).reshape(1, slots)
    mix_dot1 = jnp.sum(table.astype(F32) * dot_back, axis=1, keepdims=True)
    mix_dot0 = jnp.sum(grad_out * dense_out, axis=-1, keepdims=True)
    mean_dot = mix0 * mix_dot0 + mix1 * mix_dot1
    logit_grad = jnp.concatenate(
        [mix0 * (mix_dot0 - mean_dot), mix1 * (mix_dot1 - mean_dot)], axis=1
    ).astype(BF16)
    mix_weight_grad = dot_tn(mid_low, logit_grad)
    mid_grad = mid_grad_dense + dot_nt(logit_grad, mix_weight) + dot_nn(table, in_rows)
    ln2_gain_grad = jnp.sum(mid_grad * unit2, axis=0)
    res_grad = grad_out + norm_backward(mid_grad, ln2_gain, unit2, inverse2)
    attn_out_grad = res_grad.astype(BF16)
    out_weight_grad = dot_tn(attended, attn_out_grad)
    attended_grad = dot_nt(attn_out_grad, out_full).astype(BF16)
    qkv_grad = attention_backward(qkv_rows, bucket, attended_grad, lse)
    qkv_weight_grad = dot_tn(normed_in, qkv_grad)
    normed_grad = dot_nt(qkv_grad, qkv_full)
    ln1_gain_grad = jnp.sum(normed_grad * unit1, axis=0)
    tokens_grad = res_grad + norm_backward(normed_grad, ln1_gain, unit1, inverse1)

    out_sum = total(outs).astype(BF16).reshape(groups, capacity, width)
    out_back = lax.all_to_all(out_sum, "ep", split_axis=0, concat_axis=0, tiled=True)
    expert_out = dot_nn(table, out_back.reshape(slots, width))
    result = (hidden_res + mix0 * dense_out + mix1 * expert_out).astype(BF16)

    scatter = lambda a: lax.psum_scatter(a.astype(BF16), "ep", scatter_dimension=0, tiled=True)
    merge = lambda a: lax.psum(a, "dp").astype(F32)
    up_shard, down_shard = scatter(up_grad), scatter(down_grad)
    out_shard, qkv_shard = scatter(out_weight_grad), scatter(qkv_weight_grad)
    small_sums = lax.psum((ln1_gain_grad, ln2_gain_grad, mix_weight_grad), ("dp", "ep"))
    return (
        result,
        tokens_grad,
        small_sums[0],
        merge(qkv_shard),
        merge(out_shard),
        small_sums[1],
        merge(up_shard),
        merge(down_shard),
        small_sums[2],
        expert_up_grad[None],
        expert_down_grad[None],
    )


def solution(mesh):
    placed = (
        P(("dp", "ep"), None),
        P(("dp", "ep")),
        P(("dp", "ep"), None),
        P(),
        P("ep", None),
        P("ep", None),
        P(),
        P("ep", None),
        P("ep", None),
        P(),
        P("ep", None, "dp"),
        P("ep", "dp", None),
        P(("dp", "ep"), None),
    )
    return jax.shard_map(
        on_device,
        mesh=mesh,
        in_specs=placed,
        out_specs=(
            P(("dp", "ep"), None),
            P(("dp", "ep"), None),
            P(),
            P("ep", None),
            P("ep", None),
            P(),
            P("ep", None),
            P("ep", None),
            P(),
            P("ep", None, "dp"),
            P("ep", "dp", None),
        ),
        check_vma=False,
    )
```

time: 1120 us -> 935 us (0.83)
  matrix products: 214 us -> 43.6 us
  Pallas kernels: 0 us -> 130 us
  waiting for transfers between devices: 673 us -> 599 us
  blocking collectives: 85.4 us -> 42.8 us
  other arithmetic: 67 us -> 25.3 us
  starting transfers between devices: 10.4 us -> 39.2 us
  local copies, waits for them, and re-layouts: 52 us -> 31.7 us
    ppermute x0 -> x15, waiting for transfers between devices: none -> 258 us  [shifted(): lax.ppermute(rows, 'dp', [((i + step) % size, i) for i in range(size)])]
    all_gather x6 -> x4, waiting for transfers between devices: 311 us -> 56.6 us  [on_device(): gather = lambda w: lax.all_gather(w, 'ep', axis=0, tiled=True)]
    dot_general x31 -> x14, matrix products: 214 us -> 43.6 us  [the longest x6 18 us: dot_nn(): lax.dot_general(a, b, (((1,), (0,)), ((), ())), preferred_element_type=F32)]
    pallas_call x0 -> x8, Pallas kernels: none -> 130 us  [the longest x4 38.9 us: expert_chunk(): pl.pallas_call(expert_kernel, grid=(rows // tile,), in_specs=[block, bloc...]
    reduce_scatter x6 -> x4, waiting for transfers between devices: 286 us -> 220 us  [on_device(): lax.psum_scatter(a.astype(BF16), 'ep', scatter_dimension=0, tiled=True)]
    all_to_all x2 -> x0, blocking collectives: 42.6 us -> none  [the longest x1 21.3 us: on_device(): lax.all_to_all(sent_grad.reshape(experts, capacity, -1), 'ep', split_axis...]
    psum x1, waiting for transfers between devices: 58.4 us -> 37.1 us  [on_device(): merge = lambda a: lax.psum(a, 'dp').astype(F32)]
    unnamed x2 -> x0, other arithmetic: 20.2 us -> none
  transfers between devices with their start and end apart: 15 -> 28, of which waited for: 12 -> 12; matrix products, arithmetic and copies ran while one was open for 22% -> 6% of each run, Pallas kernels for 0% -> 14%
where the time goes in v1:
time: 935 us; the launch traced here: 927 us
  waiting for transfers between devices  599 us (64%)
  Pallas kernels  130 us (14%)
  matrix products  43.6 us (5%)
  blocking collectives  42.8 us (5%)
  starting transfers between devices  39.2 us (4%)
  local copies, waits for them, and re-layouts  31.7 us (3%)
  other arithmetic  25.3 us (3%)
  between operations  15.5 us (2%)
    ppermute x15, waiting for transfers between devices, shifted(): lax.ppermute(rows, 'dp', [((i + step) % size, i) for i in range(size)])  258 us
    reduce_scatter x4, waiting for transfers between devices, on_device(): lax.psum_scatter(a.astype(BF16), 'ep', scatter_dimension=0, tiled=True)  220 us
    all_gather x4, waiting for transfers between devices, on_device(): gather = lambda w: lax.all_gather(w, 'ep', axis=0, tiled=True)  56.6 us
    psum x1, blocking collectives, on_device(): lax.psum((ln1_gain_grad, ln2_gain_grad, mix_weight_grad), ('dp', 'ep'))  42.8 us
    pallas_call x4, Pallas kernels, expert_chunk(): pl.pallas_call(expert_kernel, grid=(rows // tile,), in_specs=[block, bloc...  38.9 us
    psum x1, waiting for transfers between devices, on_device(): merge = lambda a: lax.psum(a, 'dp').astype(F32)  37.1 us
    pallas_call x1, Pallas kernels, dense_branch(): pl.pallas_call(dense_kernel, grid=(ff // tile,), in_specs=[whole, whole,...  36.3 us
    unnamed x106, local copies, waits for them, and re-layouts  29.6 us
  transfers between devices with their start and end apart: 28, of which 12 were waited for; matrix products, arithmetic and copies ran while one was open for 6% of the time, Pallas kernels for 14%

profile of v1, /device:TPU:0, one launch (start us, length us, event | category | flops | bytes accessed | tf_op | source)
XLA Modules:
  0.0 927.4 jit_solution(14823213400286805641)
XLA Ops:
  12.3 5.3 all-to-all-start.1
  18.9 51.5 %all-gather.5.cloned.1.call-done = bf16[1024,3072]{1,0:T(8,128)(2,1)} async-done(((bf16[128,3072]{1,0:T(8,128)(2,1)}), bf16[1024,3072]{1,0:T(8,128)(2,1)}) %all-gather.5.cloned.1.call-update) | async-done | bytes 6291472 | tf_op jit(solution)/shard_map/all_gather | solution.py:334
  70.4 6.6 convolution_convert_fusion.1.q_ref.k_ref.v_ref
  77.0 15.8 %attn_fwd.1 = (bf16[512,1024]{1,0:T(8,128)(2,1)S(1)}, f32[512,1024]{1,0:T(8,128)S(1)}) custom-call(s32[1]{0:T(128)S(6)} %copy.35.flag_ref, bf16[512,3072]{1,0:T(8,128)(2,1)S(1)} %convolution_convert_fusion.1.q_ref.k_ref.v_ref, bf16[512,3072]{1,0:T(8,128)(2,1)S(1)} %convolution_convert_fusion.1.q_ref.k_ref.v_ref, ...), custom_call_target="tpu_custom_call" | custom-call | flops 2147483648 | bytes 5242880 | tf_op jit(solution)/shard_map/attn_fwd/pallas_call | solution.py:85
  95.1 5.1 all-gather.7.cloned.1.call-done
  108.1 4.4 all-to-all-start
  115.9 23.1 %all-to-all-done = bf16[8,80,1024]{2,1,0:T(8,128)(2,1)} async-done(((bf16[8,80,1024]{2,1,0:T(8,128)(2,1)}), bf16[8,80,1024]{2,1,0:T(8,128)(2,1)}, u32[]{:S(2)}, u32[]{:S(2)}) %all-to-all-start) | async-done | bytes 1310752 | tf_op jit(solution)/shard_map/all_to_all | solution.py:335
  148.3 25.3 %collective-permute-done.mid_ref.refs_1_ = bf16[640,1024]{1,0:T(8,128)(2,1)} collective-permute-done((bf16[640,1024]{1,0:T(8,128)(2,1)}, bf16[640,1024]{1,0:T(8,128)(2,1)}, u32[]{:S(2)}, u32[]{:S(2)}) %collective-permute-start) | collective-permute-done | bytes 1310752 | tf_op jit(solution)/shard_map/ppermute | solution.py:310
  173.5 9.4 %expert_chunk.5 = (bf16[640,1024]{1,0:T(8,128)(2,1)S(1)}, bf16[640,1024]{1,0:T(8,128)(2,1)S(1)}, bf16[640,1024]{1,0:T(8,128)(2,1)S(1)}, bf16[640,1024]{1,0:T(8,1...) custom-call(bf16[640,1024]{1,0:T(8,128)(2,1)} %collective-permute-done.mid_ref.refs_1_, ...), custom_call_target="tpu_custom_call" | custom-call | flops 5368709120 | bytes 13369344 | tf_op jit(solution)/shard_map/expert_chunk/pallas_call | solution.py:238
  188.3 125.8 %collective-permute-done.4.g_ref = bf16[640,1024]{1,0:T(8,128)(2,1)} collective-permute-done((bf16[640,1024]{1,0:T(8,128)(2,1)}, bf16[640,1024]{1,0:T(8,128)(2,1)}, u32[]{:S(2)}, u32[]{:S(2)}) %collective-permute-start.4) | collective-permute-done | bytes 1310752 | tf_op jit(solution)/shard_map/ppermute | solution.py:310
  314.1 83.7 %collective-permute-done.3.mid_ref.refs_2_ = bf16[640,1024]{1,0:T(8,128)(2,1)} collective-permute-done((bf16[640,1024]{1,0:T(8,128)(2,1)}, bf16[640,1024]{1,0:T(8,128)(2,1)}, u32[]{:S(2)}, u32[]{:S(2)}) %collective-permute-start.3) | collective-permute-done | bytes 1310752 | tf_op jit(solution)/shard_map/ppermute | solution.py:310
  398.7 10.1 %expert_chunk.6 = (bf16[640,1024]{1,0:T(8,128)(2,1)S(1)}, bf16[640,1024]{1,0:T(8,128)(2,1)}, bf16[640,1024]{1,0:T(8,128)(2,1)S(1)}, bf16[640,1024]{1,0:T(8,128)(...) custom-call(bf16[640,1024]{1,0:T(8,128)(2,1)} %collective-permute-done.3.mid_ref.refs_2_, ...), custom_call_target="tpu_custom_call" | custom-call | flops 5368709120 | bytes 13369344 | tf_op jit(solution)/shard_map/expert_chunk/pallas_call | solution.py:238
  412.0 10.1 %expert_chunk.7 = (bf16[640,1024]{1,0:T(8,128)(2,1)S(1)}, bf16[640,1024]{1,0:T(8,128)(2,1)}, bf16[640,1024]{1,0:T(8,128)(2,1)S(1)}, bf16[640,1024]{1,0:T(8,128)(...) custom-call(bf16[640,1024]{1,0:T(8,128)(2,1)} %collective-permute-done.6.mid_ref.refs_3_, ...), custom_call_target="tpu_custom_call" | custom-call | flops 5368709120 | bytes 13369344 | tf_op jit(solution)/shard_map/expert_chunk/pallas_call | solution.py:238
  434.4 9.3 %expert_chunk.4 = (bf16[640,1024]{1,0:T(8,128)(2,1)S(1)}, bf16[640,1024]{1,0:T(8,128)(2,1)S(1)}, bf16[640,1024]{1,0:T(8,128)(2,1)S(1)}, bf16[640,1024]{1,0:T(8,1...) custom-call(bf16[640,1024]{1,0:T(8,128)(2,1)} %bitcast.6.mid_ref.refs_0_, bf16[640,1024]{1,0:T(8,128)(2,1)} %bitcast.8.g_ref, ...), custom_call_target="tpu_custom_call" | custom-call | flops 5368709120 | bytes 13369344 | tf_op jit(solution)/shard_map/expert_chunk/pallas_call | solution.py:238
  448.2 23.4 %collective-permute-done.13 = f32[8,80]{1,0:T(8,128)S(1)} collective-permute-done((f32[8,80]{1,0:T(8,128)S(1)}, f32[8,80]{1,0:T(8,128)S(1)}, u32[]{:S(2)}, u32[]{:S(2)}) %collective-permute-start.13) | collective-permute-done | bytes 2592 | tf_op jit(solution)/shard_map/ppermute | solution.py:310
  471.7 3.7 add_convert_fusion
  476.7 4.3 all-to-all-start.3
  483.6 36.3 %dense_branch.1 = (f32[512,1024]{1,0:T(8,128)S(1)}, f32[512,1024]{1,0:T(8,128)}, bf16[1024,4096]{1,0:T(8,128)(2,1)}, bf16[4096,1024]{1,0:T(8,128)(2,1)}) custom-call(bf16[512,1024]{1,0:T(8,128)(2,1)S(1)} %copy-done.1, bf16[512,1024]{1,0:T(8,128)(2,1)S(1)} %copy-done.8, bf16[1024,4096]{1,0:T(8,128)(2,1)} %all-gather.9.cloned.1.call-done.up_ref, ...), custom_call_target="tpu_custom_call" | custom-call | flops 25769803776 | bytes 39845888 | tf_op jit(solution)/shard_map/dense_branch/pallas_call | solution.py:197
  532.3 3.7 convolution_convert_fusion.5.g_ref
  536.0 18.8 %attn_bwd.1 = bf16[512,3072]{1,0:T(8,128)(2,1)S(1)} custom-call(s32[1]{0:T(128)S(6)} %copy.35.flag_ref, bf16[512,3072]{1,0:T(8,128)(2,1)S(1)} %convolution_convert_fusion.1.q_ref.k_ref.v_ref, bf16[512,3072]{1,0:T(8,128)(2,1)S(1)} %convolution_convert_fusion.1.q_ref.k_ref.v_ref, bf16[512,3072]{1,0:T(8,128)(2,1)S(1)} %convolution_convert_fusion.1.q_ref.k_ref.v_ref, ...), custom_call_target="tpu_custom_call" | custom-call | flops 5368709120 | bytes 10485760 | tf_op jit(solution)/shard_map/attn_bwd/pallas_call | solution.py:148
  556.5 5.6 convolution_convert_fusion
  568.1 4.5 reduce-scatter.7.cloned.1.call-done
  572.5 65.4 %reduce-scatter.5.cloned.1.call-done = bf16[128,3072]{1,0:T(8,128)(2,1)} async-done(((bf16[1024,3072]{1,0:T(8,128)(2,1)}), bf16[128,3072]{1,0:T(8,128)(2,1)}) %reduce-scatter.5.cloned.1.call-update) | async-done | bytes 786448 | tf_op jit(solution)/shard_map/reduce_scatter | solution.py:433
  638.0 74.7 %reduce-scatter.9.cloned.1.call-done = bf16[128,4096]{1,0:T(8,128)(2,1)} async-done(((bf16[1024,4096]{1,0:T(8,128)(2,1)}), bf16[128,4096]{1,0:T(8,128)(2,1)}) %reduce-scatter.9.cloned.1.call-update) | async-done | bytes 1048592 | tf_op jit(solution)/shard_map/reduce_scatter | solution.py:433
  712.7 75.1 %reduce-scatter.11.cloned.1.call-done = bf16[512,1024]{1,0:T(8,128)(2,1)} async-done(((bf16[4096,1024]{1,0:T(8,128)(2,1)}), bf16[512,1024]{1,0:T(8,128)(2,1)}) %reduce-scatter.11.cloned.1.call-update) | async-done | bytes 1048592 | tf_op jit(solution)/shard_map/reduce_scatter | solution.py:433
  787.9 20.6 %expert_weight_grads.1 = (f32[1024,1024]{1,0:T(8,128)}, f32[1024,1024]{1,0:T(8,128)}) custom-call(bf16[640,1024]{1,0:T(8,128)(2,1)} %bitcast.6.mid_ref.refs_0_, bf16[640,1024]{1,0:T(8,128)(2,1)} %collective-permute-done.mid_ref.refs_1_, bf16[640,1024]{1,0:T(8,128)(2,1)} %collective-permute-done.3.mid_ref.refs_2_, ...), custom_call_target="tpu_custom_call" | custom-call | flops 10737418240 | bytes 29360128 | tf_op jit(solution)/shard_map/expert_weight_grads/pallas_call | solution.py:275
  808.5 4.4 add_convert_fusion.1
  812.9 4.6 all-to-all-start.2
  817.8 9.0 fusion.12
  826.8 42.8 %all-reduce.2 = (f32[1024]{0:T(1024)}, f32[1024]{0:T(1024)}, f32[1024,2]{0,1:T(2,128)}) all-reduce(f32[1024]{0:T(1024)S(1)} %get-tuple-element.77, f32[1024]{0:T(1024)S(1)} %get-tuple-element.75, f32[1024,2]{0,1:T(2,128)S(1)} %fusion.31), channel_id=1, replica_groups=mesh['dp'=4,'ep'=8] {'dp','ep'}, use_global_device_ids=true, to_apply=%region_12.13 | all-reduce | flops 4096 | bytes 32768 | tf_op jit(solution)/shard_map/psum | solution.py:437
  869.7 4.2 add_convert_fusion.2
  875.9 37.1 %all-reduce.6.cloned.1.call-done = (bf16[128,3072]{1,0:T(8,128)(2,1)}, bf16[128,1024]{1,0:T(8,128)(2,1)}, bf16[128,4096]{1,0:T(8,128)(2,1)}, bf16[512,1024]{1,0:T(8,128)(2,1)}) async-done(((bf16[128,3072]{1,0:T(8,128)(2,1)}, bf16[128,1024]{1,0:T(8,128)(2,1)}, bf16[128,4096]{1,0:T(8,128)(2,1)}, bf16[512,1024]{1,0:T(8,128)(2,1)}), (bf16[128,3072]{1,0:T(8,128)(2,1)}, bf16[128,1024]{1,0:T(8,128)(2,1)}, ...) | async-done | bytes 3145744 | tf_op jit(solution)/shard_map/psum | solution.py:434
  (205 shorter events, 88.1 us)
Async XLA Ops:
  7.2 63.2 %all-gather.5.cloned.1.call-start = ((), (), s32[]{:S(2)}) async-start(), calls=%async_computation.8 | async-start | bytes 7077888 | tf_op jit(solution)/shard_map/all_gather | solution.py:334
  7.9 92.3 %all-gather.7.cloned.1.call-start = ((), (), s32[]{:S(2)}) async-start(), calls=%async_computation.9 | async-start | bytes 2359296 | tf_op jit(solution)/shard_map/all_gather | solution.py:334
  8.7 472.4 %all-gather.9.cloned.1.call-start = ((), (), s32[]{:S(2)}) async-start(), calls=%async_computation.10 | async-start | bytes 9437184 | tf_op jit(solution)/shard_map/all_gather | solution.py:334
  9.4 471.7 %all-gather.11.cloned.1.call-start = ((), (), s32[]{:S(2)}) async-start(), calls=%async_computation.11 | async-start | bytes 9437184 | tf_op jit(solution)/shard_map/all_gather | solution.py:334
  12.3 58.1 %copy-start.50 = (f32[1024]{0:T(1024)S(1)}, f32[1024]{0:T(1024)}, u32[]{:S(2)}) copy-start(f32[1024]{0:T(1024)} %param.16) | copy-start | bytes 12292
  12.3 95.8 %all-to-all-start.1 = ((bf16[8,80,1024]{2,1,0:T(8,128)(2,1)}), bf16[8,80,1024]{2,1,0:T(8,128)(2,1)}, u32[]{:S(2)}, u32[]{:S(2)}) async-start(bf16[8,80,1024]{2,1,0:T(8,128)(2,1)} %bitcast.7), calls=%async_computation.1 | async-start | bytes 2621440 | tf_op jit(solution)/shard_map/all_to_all | solution.py:335
  108.1 30.9 %all-to-all-start = ((bf16[8,80,1024]{2,1,0:T(8,128)(2,1)}), bf16[8,80,1024]{2,1,0:T(8,128)(2,1)}, u32[]{:S(2)}, u32[]{:S(2)}) async-start(bf16[8,80,1024]{2,1,0:T(8,128)(2,1)} %bitcast.42), calls=%async_computation | async-start | bytes 2621440 | tf_op jit(solution)/shard_map/all_to_all | solution.py:335
  112.5 33.1 %collective-permute-start.1 = (bf16[640,1024]{1,0:T(8,128)(2,1)}, bf16[640,1024]{1,0:T(8,128)(2,1)}, u32[]{:S(2)}, u32[]{:S(2)}) collective-permute-start(bf16[640,1024]{1,0:T(8,128)(2,1)} %bitcast.8.g_ref), channel_id=1, source_target_pairs={{8,0},{16,8},{24,16},{0,24},{9,1},{17,9},{25,17},{1,25},{10,2},{18... | collective-permute-start | bytes 3932168 | tf_op jit(solution)/shard_map/ppermute | solution.py:310
  139.0 34.5 %collective-permute-start = (bf16[640,1024]{1,0:T(8,128)(2,1)}, bf16[640,1024]{1,0:T(8,128)(2,1)}, u32[]{:S(2)}, u32[]{:S(2)}) collective-permute-start(bf16[640,1024]{1,0:T(8,128)(2,1)} %bitcast.6.mid_ref.refs_0_), channel_id=1, source_target_pairs={{8,0},{16,8},{24,16},{0,24},{9,1},{17,9},{25,17},{1,25},{10,2},{18... | collective-permute-start | bytes 3932168 | tf_op jit(solution)/shard_map/ppermute | solution.py:310
  142.3 171.7 %collective-permute-start.4 = (bf16[640,1024]{1,0:T(8,128)(2,1)}, bf16[640,1024]{1,0:T(8,128)(2,1)}, u32[]{:S(2)}, u32[]{:S(2)}) collective-permute-start(bf16[640,1024]{1,0:T(8,128)(2,1)} %bitcast.8.g_ref), channel_id=1, source_target_pairs={{16,0},{24,8},{0,16},{8,24},{17,1},{25,9},{1,17},{9,25},{18,2},{26... | collective-permute-start | bytes 3932168 | tf_op jit(solution)/shard_map/ppermute | solution.py:310
  142.3 255.4 %collective-permute-start.3 = (bf16[640,1024]{1,0:T(8,128)(2,1)}, bf16[640,1024]{1,0:T(8,128)(2,1)}, u32[]{:S(2)}, u32[]{:S(2)}) collective-permute-start(bf16[640,1024]{1,0:T(8,128)(2,1)} %bitcast.6.mid_ref.refs_0_), channel_id=1, source_target_pairs={{16,0},{24,8},{0,16},{8,24},{17,1},{25,9},{1,17},{9,25},{18,2},{26... | collective-permute-start | bytes 3932168 | tf_op jit(solution)/shard_map/ppermute | solution.py:310
  145.5 37.4 %copy-start.10 = (bf16[1024,128]{1,0:T(8,128)(2,1)}, bf16[1024,128]{1,0:T(8,128)(2,1)S(1)}, u32[]{:S(2)}) copy-start(bf16[1024,128]{1,0:T(8,128)(2,1)S(1)} %pad.9.mix_ref) | copy-start | bytes 786436
  145.5 266.5 %collective-permute-start.7 = (bf16[640,1024]{1,0:T(8,128)(2,1)}, bf16[640,1024]{1,0:T(8,128)(2,1)}, u32[]{:S(2)}, u32[]{:S(2)}) collective-permute-start(bf16[640,1024]{1,0:T(8,128)(2,1)} %bitcast.8.g_ref), channel_id=1, source_target_pairs={{24,0},{0,8},{8,16},{16,24},{25,1},{1,9},{9,17},{17,25},{26,2},{2,... | collective-permute-start | bytes 3932168 | tf_op jit(solution)/shard_map/ppermute | solution.py:310
  145.6 266.4 %collective-permute-start.6 = (bf16[640,1024]{1,0:T(8,128)(2,1)}, bf16[640,1024]{1,0:T(8,128)(2,1)}, u32[]{:S(2)}, u32[]{:S(2)}) collective-permute-start(bf16[640,1024]{1,0:T(8,128)(2,1)} %bitcast.6.mid_ref.refs_0_), channel_id=1, source_target_pairs={{24,0},{0,8},{8,16},{16,24},{25,1},{1,9},{9,17},{17,25},{26,2},{2,... | collective-permute-start | bytes 3932168 | tf_op jit(solution)/shard_map/ppermute | solution.py:310
  187.5 244.2 %collective-permute-start.12 = (f32[8,80]{1,0:T(8,128)S(1)}, f32[8,80]{1,0:T(8,128)S(1)}, u32[]{:S(2)}, u32[]{:S(2)}) collective-permute-start(f32[8,80]{1,0:T(8,128)S(1)} %reshape.146), channel_id=1, source_target_pairs={{24,0},{0,8},{8,16},{16,24},{25,1},{1,9},{9,17},{17,25},{26,2},{2,... | collective-permute-start | bytes 7688 | tf_op jit(solution)/shard_map/ppermute | solution.py:310
  314.1 157.7 %collective-permute-start.9 = (bf16[640,1024]{1,0:T(8,128)(2,1)}, bf16[640,1024]{1,0:T(8,128)(2,1)}, u32[]{:S(2)}, u32[]{:S(2)}) collective-permute-start(bf16[640,1024]{1,0:T(8,128)(2,1)} %copy-done.21), channel_id=1, source_target_pairs={{24,0},{0,8},{8,16},{16,24},{25,1},{1,9},{9,17},{17,25},{26,2},{2,... | collective-permute-start | bytes 3932168 | tf_op jit(solution)/shard_map/ppermute | solution.py:310
  412.0 59.7 %collective-permute-start.10 = (bf16[640,1024]{1,0:T(8,128)(2,1)}, bf16[640,1024]{1,0:T(8,128)(2,1)}, u32[]{:S(2)}, u32[]{:S(2)}) collective-permute-start(bf16[640,1024]{1,0:T(8,128)(2,1)} %get-tuple-element.52), channel_id=1, source_target_pairs={{16,0},{24,8},{0,16},{8,24},{17,1},{25,9},{1,17},{9,25},{18,2},{26... | collective-permute-start | bytes 3932168 | tf_op jit(solution)/shard_map/ppermute | solution.py:310
  426.1 45.7 %collective-permute-start.11 = (bf16[640,1024]{1,0:T(8,128)(2,1)}, bf16[640,1024]{1,0:T(8,128)(2,1)}, u32[]{:S(2)}, u32[]{:S(2)}) collective-permute-start(bf16[640,1024]{1,0:T(8,128)(2,1)} %get-tuple-element.53), channel_id=1, source_target_pairs={{8,0},{16,8},{24,16},{0,24},{9,1},{17,9},{25,17},{1,25},{10,2},{18... | collective-permute-start | bytes 3932168 | tf_op jit(solution)/shard_map/ppermute | solution.py:310
  427.5 44.1 %collective-permute-start.13 = (f32[8,80]{1,0:T(8,128)S(1)}, f32[8,80]{1,0:T(8,128)S(1)}, u32[]{:S(2)}, u32[]{:S(2)}) collective-permute-start(f32[8,80]{1,0:T(8,128)S(1)} %reshape.147), channel_id=1, source_target_pairs={{16,0},{24,8},{0,16},{8,24},{17,1},{25,9},{1,17},{9,25},{18,2},{26... | collective-permute-start | bytes 7688 | tf_op jit(solution)/shard_map/ppermute | solution.py:310
  431.6 40.0 %collective-permute-start.14 = (f32[8,80]{1,0:T(8,128)S(1)}, f32[8,80]{1,0:T(8,128)S(1)}, u32[]{:S(2)}, u32[]{:S(2)}) collective-permute-start(f32[8,80]{1,0:T(8,128)S(1)} %reshape.148), channel_id=1, source_target_pairs={{8,0},{16,8},{24,16},{0,24},{9,1},{17,9},{25,17},{1,25},{10,2},{18... | collective-permute-start | bytes 7688 | tf_op jit(solution)/shard_map/ppermute | solution.py:310
  476.7 44.8 %all-to-all-start.3 = ((bf16[8,96,1024]{2,1,0:T(8,128)(2,1)}), bf16[8,96,1024]{2,1,0:T(8,128)(2,1)}, u32[]{:S(2)}, u32[]{:S(2)}) async-start(bf16[8,96,1024]{2,1,0:T(8,128)(2,1)} %fusion.16), calls=%async_computation.3 | async-start | bytes 3145728 | tf_op jit(solution)/shard_map/all_to_all | solution.py:404
  481.1 91.5 %reduce-scatter.7.cloned.1.call-start = ((), (), s32[]{:S(2)}) async-start(), calls=%async_computation.13 | async-start | bytes 2359296 | tf_op jit(solution)/shard_map/reduce_scatter | solution.py:433
  483.6 37.6 %copy-start.37 = (bf16[512,1024]{1,0:T(8,128)(2,1)S(1)}, bf16[512,1024]{1,0:T(8,128)(2,1)}, u32[]{:S(2)}) copy-start(bf16[512,1024]{1,0:T(8,128)(2,1)} %param.25) | copy-start | bytes 3145732
  532.0 106.0 %reduce-scatter.5.cloned.1.call-start = ((), (), s32[]{:S(2)}) async-start(), calls=%async_computation.12 | async-start | bytes 7077888 | tf_op jit(solution)/shard_map/reduce_scatter | solution.py:433
  562.1 150.6 %reduce-scatter.9.cloned.1.call-start = ((), (), s32[]{:S(2)}) async-start(), calls=%async_computation.14 | async-start | bytes 9437184 | tf_op jit(solution)/shard_map/reduce_scatter | solution.py:433
  562.9 225.0 %reduce-scatter.11.cloned.1.call-start = ((), (), s32[]{:S(2)}) async-start(), calls=%async_computation.15 | async-start | bytes 9437184 | tf_op jit(solution)/shard_map/reduce_scatter | solution.py:433
  563.6 349.4 %all-reduce.6.cloned.1.call-start = ((), (), s32[]{:S(2)}) async-start(), calls=%async_computation.16 | async-start | bytes 6291456 | tf_op jit(solution)/shard_map/psum | solution.py:434
  564.2 244.2 %collective-permute-start.2 = (bf16[640,1024]{1,0:T(8,128)(2,1)S(1)}, bf16[640,1024]{1,0:T(8,128)(2,1)}, u32[]{:S(2)}, u32[]{:S(2)}) collective-permute-start(bf16[640,1024]{1,0:T(8,128)(2,1)S(1)} %copy-done.17), channel_id=1, source_target_pairs={{24,0},{0,8},{8,16},{16,24},{25,1},{1,9},{9,17},{17,25},{26,2},{2,... | collective-permute-start | bytes 3932168 | tf_op jit(solution)/shard_map/ppermute | solution.py:310
  564.8 243.6 %collective-permute-start.5 = (bf16[640,1024]{1,0:T(8,128)(2,1)S(1)}, bf16[640,1024]{1,0:T(8,128)(2,1)}, u32[]{:S(2)}, u32[]{:S(2)}) collective-permute-start(bf16[640,1024]{1,0:T(8,128)(2,1)S(1)} %copy-done.19), channel_id=1, source_target_pairs={{16,0},{24,8},{0,16},{8,24},{17,1},{25,9},{1,17},{9,25},{18,2},{26... | collective-permute-start | bytes 3932168 | tf_op jit(solution)/shard_map/ppermute | solution.py:310
  566.0 242.5 %collective-permute-start.8 = (bf16[640,1024]{1,0:T(8,128)(2,1)}, bf16[640,1024]{1,0:T(8,128)(2,1)}, u32[]{:S(2)}, u32[]{:S(2)}) collective-permute-start(bf16[640,1024]{1,0:T(8,128)(2,1)} %copy-done.20), channel_id=1, source_target_pairs={{8,0},{16,8},{24,16},{0,24},{9,1},{17,9},{25,17},{1,25},{10,2},{18... | collective-permute-start | bytes 3932168 | tf_op jit(solution)/shard_map/ppermute | solution.py:310
  812.9 56.7 %all-to-all-start.2 = ((bf16[8,80,1024]{2,1,0:T(8,128)(2,1)}), bf16[8,80,1024]{2,1,0:T(8,128)(2,1)}, u32[]{:S(2)}, u32[]{:S(2)}) async-start(bf16[8,80,1024]{2,1,0:T(8,128)(2,1)} %bitcast.39), calls=%async_computation.2 | async-start | bytes 2621440 | tf_op jit(solution)/shard_map/all_to_all | solution.py:429
  817.8 51.8 %copy-start.4 = (f32[512,1024]{1,0:T(8,128)S(1)}, f32[512,1024]{1,0:T(8,128)}, u32[]{:S(2)}) copy-start(f32[512,1024]{1,0:T(8,128)} %copy-done.3) | copy-start | bytes 6291460
  (48 other events, 186.9 us)
Sparse Core Ops, SparseCore 0:
  9.9 60.4 all-gather.4
  72.3 27.8 all-gather.6
  102.1 68.4 all-gather.8
  172.4 54.3 all-gather.10
  532.1 40.3 reduce-scatter.6
  576.1 61.7 reduce-scatter.4
  641.4 71.2 reduce-scatter.8
  716.5 71.2 reduce-scatter.10
  790.5 122.5 all-reduce.5

commit v2 on v1

--- a/solution.py
+++ b/solution.py
@@ -305,9 +305,72 @@
     )
 
 
+def hop(rows, step, stage):
+    size = lax.axis_size("dp")
+    if step > 0:
+        pairs = [(i, i + 1) for i in range(stage - 1, size - 1)]
+    else:
+        pairs = [(i + 1, i) for i in range(0, size - stage)]
+    return lax.ppermute(rows, "dp", pairs)
+
+
+def both_hops(low, high, stage):
+    return hop(low, 1, stage), hop(high, -1, stage)
+
+
+def send_hop(rows, step, stage):
+    size = lax.axis_size("dp")
+    if step > 0:
+        pairs = [(i, i + 1) for i in range(stage)]
+    else:
+        pairs = [(i, i - 1) for i in range(size - stage, size)]
+    return lax.ppermute(rows, "dp", pairs)
+
+
+def line_reduce(parts, work):
+    size = lax.axis_size("dp")
+    up = send_hop(parts[size - 1], 1, 1)
+    down = send_hop(parts[1], -1, 1)
+    for stage in range(2, size):
+        if stage - 2 < len(work):
+            up, down = after((up, down), work[stage - 2])
+        up = send_hop(up + parts[size - stage], 1, stage)
+        down = send_hop(down + parts[stage], -1, stage)
+    return parts[0].astype(F32) + up.astype(F32) + down.astype(F32)
+
+
 def shifted(rows, step):
     size = lax.axis_size("dp")
     return lax.ppermute(rows, "dp", [((i + step) % size, i) for i in range(size)])
+
+
+def after(values, *earlier):
+    many = isinstance(values, tuple)
+    held = lax.optimization_barrier((*values, *earlier) if many else (values, *earlier))
+    return held[: len(values)] if many else held[0]
+
+
+def sum_layers(rows):
+    size, here = lax.axis_size("dp"), lax.axis_index("dp")
+    pieces = rows.reshape(size, rows.shape[0] // size, rows.shape[1])
+    piece = lambda k: lax.dynamic_index_in_dim(pieces, lax.rem(here + k, size), 0, keepdims=False)
+    acc = piece(0).astype(F32)
+    for k in range(1, size):
+        acc = acc + shifted(piece(k), size - k).astype(F32)
+    mine = acc.astype(BF16)
+    ring = jnp.stack([mine] + [shifted(mine, k) for k in range(1, size)])
+    ordered = lax.dynamic_slice_in_dim(jnp.concatenate([ring, ring]), size - here, size, 0)
+    return ordered.reshape(rows.shape).astype(F32)
+
+
+def sum_everywhere(values):
+    for axis in ("dp", "ep"):
+        size = lax.axis_size(axis)
+        step = 1
+        while step < size:
+            values = values + lax.ppermute(values, axis, [(i, i ^ step) for i in range(size)])
+            step *= 2
+    return values
 
 
 def on_device(
@@ -352,42 +415,79 @@
     target = jnp.where(slot_index < capacity, chosen * capacity + slot_index, -1)
     table = (target[:, None] == jnp.arange(slots, dtype=jnp.int32)[None, :]).astype(BF16)
 
-    def dispatch(rows):
-        sent = dot_tn(table, rows).astype(BF16)
-        return exchange_out(sent.reshape(experts, capacity, width)).reshape(groups * capacity, width)
-
-    g_own = dispatch(cotangent)
-    gs = [g_own] + [shifted(g_own, k) for k in range(1, layers)]
+    pick = lambda rows: dot_tn(table, rows).astype(BF16).reshape(experts, capacity, width)
+    join = lambda lows, highs: [highs[k] + lows[layers - k] for k in range(1, layers)]
 
     token_rows = tokens.astype(F32)
     unit1, inverse1 = normalise(token_rows)
     normed_in = (unit1 * ln1_gain).astype(BF16)
+    g_own = exchange_out(pick(cotangent)).reshape(slots, width)
+    normed_in, g_own = lax.optimization_barrier((normed_in, g_own))
+    g_low, g_high = [g_own], [g_own]
+    mid_low_hops, mid_high_hops = [], []
+
+    def step(lows, highs, *others):
+        stage = len(lows)
+        held = lax.optimization_barrier((lows[-1], highs[-1], *others))
+        lows[-1], highs[-1] = held[:2]
+        if stage < layers:
+            low, high = both_hops(lows[-1], highs[-1], stage)
+            lows.append(low)
+            highs.append(high)
+        return held[2:]
+
+    step(g_low, g_high)
     qkv_rows = dot_nn(normed_in, qkv_full).astype(BF16)
+    (qkv_rows,) = step(g_low, g_high, qkv_rows)
     attended, lse = attention_forward(qkv_rows, bucket)
     hidden_res = token_rows + dot_nn(attended, out_full)
     unit2, inverse2 = normalise(hidden_res)
     mid_low = (unit2 * ln2_gain).astype(BF16)
-    mid_own = dispatch(mid_low)
-    mids = [mid_own] + [shifted(mid_own, k) for k in range(1, layers)]
+    mid_slots = pick(mid_low)
+    (mid_slots,) = step(g_low, g_high, mid_slots)
+    mid_own = exchange_out(mid_slots).reshape(slots, width)
+    (mid_own,) = step(g_low, g_high, mid_own)
+    gs = [g_own] + join(g_low, g_high)
+    m_low, m_high = [mid_own], [mid_own]
+    step(m_low, m_high)
+
+    chunk = lambda mid, g: expert_chunk(mid, g, mix_pad, expert_up2, expert_down2)
+    chunks = {0: chunk(mid_own, g_own)}
+    step(m_low, m_high, chunks[0][0])
 
     grad_out = cotangent.astype(F32)
     logits = dot_nn(mid_low, mix_weight)
     mix1 = 1.0 / (1.0 + jnp.exp(logits[:, 0:1] - logits[:, 1:2]))
     mix0 = 1.0 / (1.0 + jnp.exp(logits[:, 1:2] - logits[:, 0:1]))
     dense_grad = (mix0 * grad_out).astype(BF16)
-    dense_out, mid_grad_dense, up_grad, down_grad = dense_branch(mid_low, dense_grad, up_full, down_full)
-
-    chunks = [
-        expert_chunk(mids[k], gs[k], mix_pad, expert_up2, expert_down2) for k in range(layers)
-    ]
+    while len(m_low) < layers:
+        dense_grad, = step(m_low, m_high, dense_grad)
+    mids = {0: mid_own}
+    middle = layers // 2
+    mids[middle] = m_high[middle] + m_low[layers - middle]
+    chunks[middle] = chunk(mids[middle], gs[middle])
+    for k in [layers - 1] + list(range(1, layers - 1)):
+        if k != middle:
+            mids[k] = m_high[k] + m_low[layers - k]
+            chunks[k] = chunk(mids[k], gs[k])
+    mids = [mids[k] for k in range(layers)]
+    chunks = [chunks[k] for k in range(layers)]
     back = lambda k, a: shifted(a, layers - k) if k else a
-    ins = [back(k, chunks[k][1]) for k in range(layers)]
+    scatter = lambda a: lax.psum_scatter(a.astype(BF16), "ep", scatter_dimension=0, tiled=True)
+    dense_out, mid_grad_dense, up_grad, down_grad = dense_branch(
+        mid_low, after(dense_grad, chunks[1][0]), up_full, down_full
+    )
+    up_shard = scatter(up_grad)
+    down_shard = scatter(after(down_grad, chunks[1][0]))
+    expert_up_grad, expert_down_grad = expert_weight_grads(
+        mids,
+        [c[3] for c in chunks],
+        [c[2] for c in chunks],
+        [after(chunks[0][4], dense_out)] + [c[4] for c in chunks[1:]],
+    )
+    in_total = line_reduce([c[1] for c in chunks], [dense_out, expert_up_grad])
     dots = [back(k, chunks[k][5].reshape(groups, capacity)) for k in range(layers)]
-    outs = [back(k, chunks[k][0]) for k in range(layers)]
-    expert_up_grad, expert_down_grad = expert_weight_grads(
-        mids, [c[3] for c in chunks], [c[2] for c in chunks], [c[4] for c in chunks]
-    )
-
+    outs = [chunks[0][0]] + [back(k, after(chunks[k][0], in_total)) for k in range(1, layers)]
     def total(parts):
         acc = parts[0].astype(F32)
         for part in parts[1:]:
@@ -399,9 +499,10 @@
     dot_low = dot_sum - dot_high
     extra = jnp.stack([dot_high, dot_low], axis=1)
     extra = jnp.pad(extra, ((0, 0), (0, 14), (0, width - capacity)))
-    in_sum = total(ins).reshape(groups, capacity, width)
+    in_sum = in_total.reshape(groups, capacity, width)
     packed = jnp.concatenate([in_sum, extra], axis=1).astype(BF16)
     returned = lax.all_to_all(packed, "ep", split_axis=0, concat_axis=0, tiled=True)
+    returned, up_shard = lax.optimization_barrier((returned, up_shard))
     in_rows = returned[:, :capacity].reshape(slots, width)
     dot_back = (
         returned[:, capacity, :capacity].astype(F32) + returned[:, capacity + 1, :capacity].astype(F32)
@@ -419,32 +520,38 @@
     attn_out_grad = res_grad.astype(BF16)
     out_weight_grad = dot_tn(attended, attn_out_grad)
     attended_grad = dot_nt(attn_out_grad, out_full).astype(BF16)
+    attended_grad, outs[1] = lax.optimization_barrier((attended_grad, outs[1]))
     qkv_grad = attention_backward(qkv_rows, bucket, attended_grad, lse)
+    out_shard = scatter(after(out_weight_grad, up_shard))
+    qkv_grad, outs[2], down_shard = lax.optimization_barrier((qkv_grad, outs[2], down_shard))
     qkv_weight_grad = dot_tn(normed_in, qkv_grad)
     normed_grad = dot_nt(qkv_grad, qkv_full)
     ln1_gain_grad = jnp.sum(normed_grad * unit1, axis=0)
     tokens_grad = res_grad + norm_backward(normed_grad, ln1_gain, unit1, inverse1)
 
+    up_shard, down_shard, *outs = after((up_shard, down_shard, *outs), qkv_weight_grad)
     out_sum = total(outs).astype(BF16).reshape(groups, capacity, width)
     out_back = lax.all_to_all(out_sum, "ep", split_axis=0, concat_axis=0, tiled=True)
     expert_out = dot_nn(table, out_back.reshape(slots, width))
     result = (hidden_res + mix0 * dense_out + mix1 * expert_out).astype(BF16)
 
-    scatter = lambda a: lax.psum_scatter(a.astype(BF16), "ep", scatter_dimension=0, tiled=True)
-    merge = lambda a: lax.psum(a, "dp").astype(F32)
-    up_shard, down_shard = scatter(up_grad), scatter(down_grad)
-    out_shard, qkv_shard = scatter(out_weight_grad), scatter(qkv_weight_grad)
-    small_sums = lax.psum((ln1_gain_grad, ln2_gain_grad, mix_weight_grad), ("dp", "ep"))
+    up_final = sum_layers(up_shard)
+    down_final = sum_layers(down_shard)
+    out_final = sum_layers(after(out_shard, qkv_weight_grad))
+    qkv_final = sum_layers(scatter(qkv_weight_grad))
+    small_sums = sum_everywhere(
+        jnp.concatenate([ln1_gain_grad[None], ln2_gain_grad[None], mix_weight_grad.T], axis=0)
+    )
     return (
         result,
         tokens_grad,
         small_sums[0],
-        merge(qkv_shard),
-        merge(out_shard),
+        qkv_final,
+        out_final,
         small_sums[1],
-        merge(up_shard),
-        merge(down_shard),
-        small_sums[2],
+        up_final,
+        down_final,
+        small_sums[2:].T,
         expert_up_grad[None],
         expert_down_grad[None],
     )

time: 935 us -> 779 us (0.83)
  waiting for transfers between devices: 599 us -> 308 us
  starting transfers between devices: 39.2 us -> 158 us
  other arithmetic: 25.3 us -> 56.7 us
  blocking collectives: 42.8 us -> 22.9 us
    reduce_scatter x4, waiting for transfers between devices: 220 us -> 0.04 us  [on_device(): lax.psum_scatter(a.astype(BF16), 'ep', scatter_dimension=0, tiled=True)]
    ppermute x15 -> x30, waiting for transfers between devices: 258 us -> 117 us  [shifted(): lax.ppermute(rows, 'dp', [((i + step) % size, i) for i in range(size)])]
    ppermute x0 -> x23, waiting for transfers between devices: none -> 126 us  [the longest x12 87 us: hop(): return lax.ppermute(rows, 'dp', pairs)]
    ppermute x15 -> x30, starting transfers between devices: 20 us -> 99 us  [shifted(): lax.ppermute(rows, 'dp', [((i + step) % size, i) for i in range(size)])]
    ppermute x0 -> x23, starting transfers between devices: none -> 44.7 us  [the longest x12 19.7 us: hop(): return lax.ppermute(rows, 'dp', pairs)]
    psum x1 -> x0, blocking collectives: 42.8 us -> none  [on_device(): lax.psum((ln1_gain_grad, ln2_gain_grad, mix_weight_grad), ('dp', 'ep'))]
    psum x1 -> x0, waiting for transfers between devices: 37.1 us -> none  [on_device(): merge = lambda a: lax.psum(a, 'dp').astype(F32)]
    all_gather x4, waiting for transfers between devices: 56.6 us -> 19.5 us  [on_device(): gather = lambda w: lax.all_gather(w, 'ep', axis=0, tiled=True)]
  transfers between devices with their start and end apart: 28 -> 64, of which waited for: 12 -> 32; matrix products, arithmetic and copies ran while one was open for 6% -> 14% of each run, Pallas kernels for 14% -> 12%
where the time goes in v2:
time: 779 us; the launch traced here: 768 us
  waiting for transfers between devices  308 us (40%)
  starting transfers between devices  158 us (20%)
  Pallas kernels  132 us (17%)
  other arithmetic  56.7 us (7%)
  matrix products  46 us (6%)
  local copies, waits for them, and re-layouts  27.9 us (4%)
  blocking collectives  22.9 us (3%)
  between operations  16.4 us (2%)
    ppermute x30, waiting for transfers between devices, shifted(): lax.ppermute(rows, 'dp', [((i + step) % size, i) for i in range(size)])  117 us
    ppermute x30, starting transfers between devices, shifted(): lax.ppermute(rows, 'dp', [((i + step) % size, i) for i in range(size)])  99 us
    ppermute x12, waiting for transfers between devices, hop(): return lax.ppermute(rows, 'dp', pairs)  87 us
    pallas_call x4, Pallas kernels, expert_chunk(): pl.pallas_call(expert_kernel, grid=(rows // tile,), in_specs=[block, bloc...  41.7 us
    pallas_call x1, Pallas kernels, dense_branch(): pl.pallas_call(dense_kernel, grid=(ff // tile,), in_specs=[whole, whole,...  36.3 us
    ppermute x5, waiting for transfers between devices, sum_everywhere(): lax.ppermute(values, axis, [(i, i ^ step) for i in range(size)])  32.4 us
    all_to_all x1, waiting for transfers between devices, on_device(): lax.all_to_all(a, 'ep', split_axis=0, concat_axis=1, tiled=True)  24.6 us
    all_to_all x1, blocking collectives, on_device(): lax.all_to_all(a, 'ep', split_axis=0, concat_axis=1, tiled=True)  22.9 us
  transfers between devices with their start and end apart: 64, of which 32 were waited for; matrix products, arithmetic and copies ran while one was open for 14% of the time, Pallas kernels for 12%

profile of v2, /device:TPU:0, one launch (start us, length us, event | category | flops | bytes accessed | tf_op | source)
XLA Modules:
  0.0 768.4 jit_solution(2957323138833547148)
XLA Ops:
  12.3 5.3 all-to-all-start
  19.7 24.6 %all-to-all-done = bf16[8,80,1024]{2,1,0:T(8,128)(2,1)} async-done(((bf16[8,80,1024]{2,1,0:T(8,128)(2,1)}), bf16[8,80,1024]{2,1,0:T(8,128)(2,1)}, u32[]{:S(2)}, u32[]{:S(2)}) %all-to-all-start) | async-done | bytes 1310752 | tf_op jit(solution)/shard_map/all_to_all | solution.py:398
  51.3 19.2 %all-gather.5.cloned.1.call-done = bf16[1024,3072]{1,0:T(8,128)(2,1)} async-done(((bf16[128,3072]{1,0:T(8,128)(2,1)}), bf16[1024,3072]{1,0:T(8,128)(2,1)}) %all-gather.5.cloned.1.call-update) | async-done | bytes 6291472 | tf_op jit(solution)/shard_map/all_gather | solution.py:397
  70.4 6.5 convolution_convert_fusion.q_ref.k_ref.v_ref
  81.8 15.8 %attn_fwd.1 = (bf16[512,1024]{1,0:T(8,128)(2,1)S(1)}, f32[512,1024]{1,0:T(8,128)S(1)}) custom-call(s32[1]{0:T(128)S(6)} %copy.59.flag_ref, bf16[512,3072]{1,0:T(8,128)(2,1)S(1)} %convolution_convert_fusion.q_ref.k_ref.v_ref, bf16[512,3072]{1,0:T(8,128)(2,1)S(1)} %convolution_convert_fusion.q_ref.k_ref.v_ref, ...), custom_call_target="tpu_custom_call" | custom-call | flops 2147483648 | bytes 5242880 | tf_op jit(solution)/shard_map/attn_fwd/pallas_call | solution.py:85
  106.1 8.0 %collective-permute-done.3 = bf16[640,1024]{1,0:T(8,128)(2,1)} collective-permute-done((bf16[640,1024]{1,0:T(8,128)(2,1)}, bf16[640,1024]{1,0:T(8,128)(2,1)}, u32[]{:S(2)}, u32[]{:S(2)}) %collective-permute-start.3) | collective-permute-done | bytes 1310752 | tf_op jit(solution)/shard_map/ppermute | solution.py:314
  116.1 22.9 %all_to_all.28 = bf16[8,80,1024]{2,1,0:T(8,128)(2,1)} all-to-all(bf16[8,80,1024]{2,1,0:T(8,128)(2,1)S(1)} %bitcast.154), channel_id=1, replica_groups=mesh['dp'=4,'ep'=8] {'ep'}, dimensions={0} | all-to-all | bytes 2621440 | tf_op jit(solution)/shard_map/all_to_all | solution.py:398
  140.1 6.1 collective-permute-done.5
  150.4 9.5 %expert_chunk.4 = (bf16[640,1024]{1,0:T(8,128)(2,1)S(1)}, bf16[640,1024]{1,0:T(8,128)(2,1)S(1)}, bf16[640,1024]{1,0:T(8,128)(2,1)S(1)}, bf16[640,1024]{1,0:T(8,1...) custom-call(bf16[640,1024]{1,0:T(8,128)(2,1)} %bitcast.7.mid_ref.refs_0_, bf16[640,1024]{1,0:T(8,128)(2,1)} %bitcast.4.g_ref, ...), custom_call_target="tpu_custom_call" | custom-call | flops 5368709120 | bytes 13369344 | tf_op jit(solution)/shard_map/expert_chunk/pallas_call | solution.py:238
  160.0 13.7 %collective-permute-done.6 = bf16[640,1024]{1,0:T(8,128)(2,1)} collective-permute-done((bf16[640,1024]{1,0:T(8,128)(2,1)}, bf16[640,1024]{1,0:T(8,128)(2,1)}, u32[]{:S(2)}, u32[]{:S(2)}) %collective-permute-start.6) | collective-permute-done | bytes 1310752 | tf_op jit(solution)/shard_map/ppermute | solution.py:314
  182.6 28.2 %collective-permute-done.9 = bf16[640,1024]{1,0:T(8,128)(2,1)S(1)} collective-permute-done((bf16[640,1024]{1,0:T(8,128)(2,1)}, bf16[640,1024]{1,0:T(8,128)(2,1)S(1)}, u32[]{:S(2)}, u32[]{:S(2)}) %collective-permute-start.9) | collective-permute-done | bytes 1310752 | tf_op jit(solution)/shard_map/ppermute | solution.py:314
  217.5 10.3 %expert_chunk.5 = (bf16[640,1024]{1,0:T(8,128)(2,1)}, bf16[640,1024]{1,0:T(8,128)(2,1)S(1)}, bf16[640,1024]{1,0:T(8,128)(2,1)S(1)}, bf16[640,1024]{1,0:T(8,128)(...) custom-call(bf16[640,1024]{1,0:T(8,128)(2,1)} %add.235.mid_ref.refs_1_, bf16[640,1024]{1,0:T(8,128)(2,1)} %add.236.g_ref, ...), custom_call_target="tpu_custom_call" | custom-call | flops 5368709120 | bytes 13369344 | tf_op jit(solution)/shard_map/expert_chunk/pallas_call | solution.py:238
  234.3 36.3 %dense_branch.1 = (f32[512,1024]{1,0:T(8,128)S(1)}, f32[512,1024]{1,0:T(8,128)}, bf16[1024,4096]{1,0:T(8,128)(2,1)}, bf16[4096,1024]{1,0:T(8,128)(2,1)}) custom-call(bf16[512,1024]{1,0:T(8,128)(2,1)S(1)} %copy-done.2, bf16[512,1024]{1,0:T(8,128)(2,1)S(1)} %copy-done.14, bf16[1024,4096]{1,0:T(8,128)(2,1)} %all-gather.9.cloned.1.call-done.up_ref, ...), custom_call_target="tpu_custom_call" | custom-call | flops 25769803776 | bytes 39845888 | tf_op jit(solution)/shard_map/dense_branch/pallas_call | solution.py:197
  277.4 24.0 %collective-permute-done.11 = bf16[640,1024]{1,0:T(8,128)(2,1)S(1)} collective-permute-done((bf16[640,1024]{1,0:T(8,128)(2,1)}, bf16[640,1024]{1,0:T(8,128)(2,1)S(1)}, u32[]{:S(2)}, u32[]{:S(2)}) %collective-permute-start.11) | collective-permute-done | bytes 1310752 | tf_op jit(solution)/shard_map/ppermute | solution.py:314
  304.6 11.4 %expert_chunk.6 = (bf16[640,1024]{1,0:T(8,128)(2,1)}, bf16[640,1024]{1,0:T(8,128)(2,1)S(1)}, bf16[640,1024]{1,0:T(8,128)(2,1)S(1)}, bf16[640,1024]{1,0:T(8,128)(...) custom-call(bf16[640,1024]{1,0:T(8,128)(2,1)} %add.239.mid_ref.refs_3_, bf16[640,1024]{1,0:T(8,128)(2,1)} %add.240.g_ref, ...), custom_call_target="tpu_custom_call" | custom-call | flops 5368709120 | bytes 13369344 | tf_op jit(solution)/shard_map/expert_chunk/pallas_call | solution.py:238
  323.7 10.5 %expert_chunk.7 = (bf16[640,1024]{1,0:T(8,128)(2,1)}, bf16[640,1024]{1,0:T(8,128)(2,1)S(1)}, bf16[640,1024]{1,0:T(8,128)(2,1)S(1)}, bf16[640,1024]{1,0:T(8,128)(...) custom-call(bf16[640,1024]{1,0:T(8,128)(2,1)} %add.241.mid_ref.refs_2_, bf16[640,1024]{1,0:T(8,128)(2,1)} %add.242.g_ref, ...), custom_call_target="tpu_custom_call" | custom-call | flops 5368709120 | bytes 13369344 | tf_op jit(solution)/shard_map/expert_chunk/pallas_call | solution.py:238
  349.5 19.4 %expert_weight_grads.1 = (f32[1024,1024]{1,0:T(8,128)}, f32[1024,1024]{1,0:T(8,128)}) custom-call(bf16[640,1024]{1,0:T(8,128)(2,1)} %bitcast.7.mid_ref.refs_0_, bf16[640,1024]{1,0:T(8,128)(2,1)S(1)} %copy-done.11, bf16[640,1024]{1,0:T(8,128)(2,1)S(1)} %copy-done.13, bf16[640,1024]{1,0:T(8,128)(2,1)S(1)} %copy-done.12, bf16[640,1024]{1,0:T(8,128)(2,1)} %copy-done.26, ...), custom_call_target="tpu_custom_call" | custom-call | flops 10737418240 | bytes 29360128 | tf_op jit(solution)/shard_map/expert_weight_grads/pallas_call | solution.py:275
  372.6 7.4 collective-permute-start.16
  391.8 14.8 %collective-permute-done.19 = f32[8,80]{1,0:T(8,128)S(1)} collective-permute-done((f32[8,80]{1,0:T(8,128)S(1)}, f32[8,80]{1,0:T(8,128)S(1)}, u32[]{:S(2)}, u32[]{:S(2)}) %collective-permute-start.19) | collective-permute-done | bytes 2592 | tf_op jit(solution)/shard_map/ppermute | solution.py:344
  422.7 17.2 %all-to-all-done.2 = bf16[8,96,1024]{2,1,0:T(8,128)(2,1)} async-done(((bf16[8,96,1024]{2,1,0:T(8,128)(2,1)}), bf16[8,96,1024]{2,1,0:T(8,128)(2,1)}, u32[]{:S(2)}, u32[]{:S(2)}) %all-to-all-start.2) | async-done | bytes 1572896 | tf_op jit(solution)/shard_map/all_to_all | solution.py:504
  457.7 21.1 %collective-permute-done.21 = bf16[640,1024]{1,0:T(8,128)(2,1)} collective-permute-done((bf16[640,1024]{1,0:T(8,128)(2,1)}, bf16[640,1024]{1,0:T(8,128)(2,1)}, u32[]{:S(2)}, u32[]{:S(2)}) %collective-permute-start.21) | collective-permute-done | bytes 1310752 | tf_op jit(solution)/shard_map/ppermute | solution.py:344
  478.8 18.8 %attn_bwd.1 = bf16[512,3072]{1,0:T(8,128)(2,1)S(1)} custom-call(s32[1]{0:T(128)S(6)} %copy.59.flag_ref, bf16[512,3072]{1,0:T(8,128)(2,1)S(1)} %convolution_convert_fusion.q_ref.k_ref.v_ref, bf16[512,3072]{1,0:T(8,128)(2,1)S(1)} %convolution_convert_fusion.q_ref.k_ref.v_ref, bf16[512,3072]{1,0:T(8,128)(2,1)S(1)} %convolution_convert_fusion.q_ref.k_ref.v_ref, ...), custom_call_target="tpu_custom_call" | custom-call | flops 5368709120 | bytes 10485760 | tf_op jit(solution)/shard_map/attn_bwd/pallas_call | solution.py:148
  499.3 7.1 collective-permute-done.22
  506.4 8.4 %fusion.53 = bf16[1024,3072]{1,0:T(8,128)(2,1)} fusion(bf16[512,1024]{1,0:T(8,128)(2,1)} %fusion.7, bf16[512,3072]{1,0:T(8,128)(2,1)} %copy-done.24), kind=kOutput, calls=%fused_computation.154 | convolution fusion | flops 3221225472 | bytes 10485760 | tf_op jit(solution)/shard_map/dot_general | solution.py:29
  515.7 46.0 %collective-permute-start.47 = (bf16[128,1024]{1,0:T(8,128)(2,1)}, bf16[128,1024]{1,0:T(8,128)(2,1)}, u32[]{:S(2)}, u32[]{:S(2)}) collective-permute-start(bf16[128,1024]{1,0:T(8,128)(2,1)} %get-tuple-element.185), channel_id=1, source_target_pairs={{24,0},{0,8},{8,16},{16,24},{25,1},{1,9},{9,17},{17,25},{26,2},{2,... | collective-permute-start | bytes 786440 | tf_op jit(solution)/shard_map/ppermute | solution.py:344
  562.0 8.9 %fusion.12 = (f32[1024]{0:T(1024)S(1)}, f32[512]{0:T(512)S(1)}, f32[512]{0:T(512)S(1)}, f32[512,1024]{1,0:T(8,128)}) fusion(bf16[512,1024]{1,0:T(8,128)(2,1)S(1)} %copy-done.36, f32[512]{0:T(512)S(1)} %add_rsqrt_fusion.1, f32[512]{0:T(512)S(1)} %broadcast_multiply_fusion.5, f32[1024]{0:T(1024)S(1)} %copy-done.54, bf16[512,3072]{1,0:T(8,128)(2,1)} %copy-done.24, ...), kind=kOutput, calls=%fused_computation.22 | convolution fusion | flops 3225942016 | bytes 12599296 | tf_op jit(solution)/shard_map/dot_general | solution.py:25
  584.7 15.9 %collective-permute-done.25 = f32[4,1024]{1,0:T(4,128)S(1)} collective-permute-done((f32[4,1024]{1,0:T(4,128)S(1)}, f32[4,1024]{1,0:T(4,128)S(1)}, u32[]{:S(2)}, u32[]{:S(2)}) %collective-permute-start.25) | collective-permute-done | bytes 16416 | tf_op jit(solution)/shard_map/ppermute | solution.py:371
  614.1 15.4 %collective-permute-done.28 = f32[4,1024]{1,0:T(4,128)S(1)} collective-permute-done((f32[4,1024]{1,0:T(4,128)S(1)}, f32[4,1024]{1,0:T(4,128)S(1)}, u32[]{:S(2)}, u32[]{:S(2)}) %collective-permute-start.28) | collective-permute-done | bytes 16416 | tf_op jit(solution)/shard_map/ppermute | solution.py:371
  646.0 10.7 %collective-permute-start.50 = (bf16[128,1024]{1,0:T(8,128)(2,1)S(1)}, bf16[128,1024]{1,0:T(8,128)(2,1)S(1)}, u32[]{:S(2)}, u32[]{:S(2)}) collective-permute-start(bf16[128,1024]{1,0:T(8,128)(2,1)S(1)} %get-tuple-element.172), channel_id=1, source_target_pairs={{8,0},{16,8},{24,16},{0,24},{9,1},{17,9},{25,17},{1,25},{10,2},{18... | collective-permute-start | bytes 786440 | tf_op jit(solution)/shard_map/ppermute | solution.py:344
  663.5 26.8 %collective-permute-done.51 = bf16[128,1024]{1,0:T(8,128)(2,1)S(1)} collective-permute-done((bf16[128,1024]{1,0:T(8,128)(2,1)S(1)}, bf16[128,1024]{1,0:T(8,128)(2,1)S(1)}, u32[]{:S(2)}, u32[]{:S(2)}) %collective-permute-start.51) | collective-permute-done | bytes 262176 | tf_op jit(solution)/shard_map/ppermute | solution.py:344
  726.6 5.5 collective-permute-done.29
  747.4 12.2 %collective-permute-done.33 = bf16[32,3072]{1,0:T(8,128)(2,1)S(1)} collective-permute-done((bf16[32,3072]{1,0:T(8,128)(2,1)S(1)}, bf16[32,3072]{1,0:T(8,128)(2,1)S(1)}, u32[]{:S(2)}, u32[]{:S(2)}) %collective-permute-start.33) | collective-permute-done | bytes 196640 | tf_op jit(solution)/shard_map/ppermute | solution.py:344
  (342 shorter events, 244.2 us)
Async XLA Ops:
  7.2 63.2 %all-gather.5.cloned.1.call-start = ((), (), s32[]{:S(2)}) async-start(), calls=%async_computation.8 | async-start | bytes 7077888 | tf_op jit(solution)/shard_map/all_gather | solution.py:397
  7.9 92.3 %all-gather.7.cloned.1.call-start = ((), (), s32[]{:S(2)}) async-start(), calls=%async_computation.9 | async-start | bytes 2359296 | tf_op jit(solution)/shard_map/all_gather | solution.py:397
  8.7 223.1 %all-gather.11.cloned.1.call-start = ((), (), s32[]{:S(2)}) async-start(), calls=%async_computation.11 | async-start | bytes 9437184 | tf_op jit(solution)/shard_map/all_gather | solution.py:397
  9.4 222.4 %all-gather.9.cloned.1.call-start = ((), (), s32[]{:S(2)}) async-start(), calls=%async_computation.10 | async-start | bytes 9437184 | tf_op jit(solution)/shard_map/all_gather | solution.py:397
  12.3 32.0 %all-to-all-start = ((bf16[8,80,1024]{2,1,0:T(8,128)(2,1)}), bf16[8,80,1024]{2,1,0:T(8,128)(2,1)}, u32[]{:S(2)}, u32[]{:S(2)}) async-start(bf16[8,80,1024]{2,1,0:T(8,128)(2,1)} %bitcast.3), calls=%async_computation | async-start | bytes 2621440 | tf_op jit(solution)/shard_map/all_to_all | solution.py:398
  17.6 422.3 %reduce-scatter.5.cloned.1.call-start = ((), (), s32[]{:S(2)}) async-start(), calls=%async_computation.12 | async-start | bytes 9437184 | tf_op jit(solution)/shard_map/reduce_scatter | solution.py:476
  44.3 32.6 %collective-permute-start = (bf16[640,1024]{1,0:T(8,128)(2,1)}, bf16[640,1024]{1,0:T(8,128)(2,1)}, u32[]{:S(2)}, u32[]{:S(2)}) collective-permute-start(bf16[640,1024]{1,0:T(8,128)(2,1)} %bitcast.4.g_ref), channel_id=1, source_target_pairs={{0,8},{8,16},{16,24},{1,9},{9,17},{17,25},{2,10},{10,18},{18,26},{... | collective-permute-start | bytes 3932168 | tf_op jit(solution)/shard_map/ppermute | solution.py:314
  49.3 29.4 %collective-permute-start.1 = (bf16[640,1024]{1,0:T(8,128)(2,1)}, bf16[640,1024]{1,0:T(8,128)(2,1)}, u32[]{:S(2)}, u32[]{:S(2)}) collective-permute-start(bf16[640,1024]{1,0:T(8,128)(2,1)} %bitcast.4.g_ref), channel_id=1, source_target_pairs={{8,0},{16,8},{24,16},{9,1},{17,9},{25,17},{10,2},{18,10},{26,18},{... | collective-permute-start | bytes 3932168 | tf_op jit(solution)/shard_map/ppermute | solution.py:314
  80.5 33.6 %collective-permute-start.3 = (bf16[640,1024]{1,0:T(8,128)(2,1)}, bf16[640,1024]{1,0:T(8,128)(2,1)}, u32[]{:S(2)}, u32[]{:S(2)}) collective-permute-start(bf16[640,1024]{1,0:T(8,128)(2,1)} %collective-permute-done.1), channel_id=1, source_target_pairs={{8,0},{16,8},{9,1},{17,9},{10,2},{18,10},{11,3},{19,11},{12,4},{20... | collective-permute-start | bytes 3932168 | tf_op jit(solution)/shard_map/ppermute | solution.py:314
  114.8 31.3 %collective-permute-start.5 = (bf16[640,1024]{1,0:T(8,128)(2,1)}, bf16[640,1024]{1,0:T(8,128)(2,1)}, u32[]{:S(2)}, u32[]{:S(2)}) collective-permute-start(bf16[640,1024]{1,0:T(8,128)(2,1)} %collective-permute-done.3), channel_id=1, source_target_pairs={{8,0},{9,1},{10,2},{11,3},{12,4},{13,5},{14,6},{15,7}} | collective-permute-start | bytes 3932168 | tf_op jit(solution)/shard_map/ppermute | solution.py:314
  146.1 27.6 %collective-permute-start.6 = (bf16[640,1024]{1,0:T(8,128)(2,1)}, bf16[640,1024]{1,0:T(8,128)(2,1)}, u32[]{:S(2)}, u32[]{:S(2)}) collective-permute-start(bf16[640,1024]{1,0:T(8,128)(2,1)} %bitcast.7.mid_ref.refs_0_), channel_id=1, source_target_pairs={{0,8},{8,16},{16,24},{1,9},{9,17},{17,25},{2,10},{10,18},{18,26},{... | collective-permute-start | bytes 3932168 | tf_op jit(solution)/shard_map/ppermute | solution.py:314
  148.6 30.2 %collective-permute-start.7 = (bf16[640,1024]{1,0:T(8,128)(2,1)}, bf16[640,1024]{1,0:T(8,128)(2,1)}, u32[]{:S(2)}, u32[]{:S(2)}) collective-permute-start(bf16[640,1024]{1,0:T(8,128)(2,1)} %bitcast.7.mid_ref.refs_0_), channel_id=1, source_target_pairs={{8,0},{16,8},{24,16},{9,1},{17,9},{25,17},{10,2},{18,10},{26,18},{... | collective-permute-start | bytes 3932168 | tf_op jit(solution)/shard_map/ppermute | solution.py:314
  179.6 31.1 %collective-permute-start.9 = (bf16[640,1024]{1,0:T(8,128)(2,1)}, bf16[640,1024]{1,0:T(8,128)(2,1)S(1)}, u32[]{:S(2)}, u32[]{:S(2)}) collective-permute-start(bf16[640,1024]{1,0:T(8,128)(2,1)} %collective-permute-done.7), channel_id=1, source_target_pairs={{8,0},{16,8},{9,1},{17,9},{10,2},{18,10},{11,3},{19,11},{12,4},{20... | collective-permute-start | bytes 3932168 | tf_op jit(solution)/shard_map/ppermute | solution.py:314
  271.9 234.5 %reduce-scatter.7.cloned.1.call-start = ((), (), s32[]{:S(2)}) async-start(), calls=%async_computation.13 | async-start | bytes 9437184 | tf_op jit(solution)/shard_map/reduce_scatter | solution.py:476
  272.4 29.0 %collective-permute-start.11 = (bf16[640,1024]{1,0:T(8,128)(2,1)}, bf16[640,1024]{1,0:T(8,128)(2,1)S(1)}, u32[]{:S(2)}, u32[]{:S(2)}) collective-permute-start(bf16[640,1024]{1,0:T(8,128)(2,1)} %copy-done.43), channel_id=1, source_target_pairs={{8,0},{9,1},{10,2},{11,3},{12,4},{13,5},{14,6},{15,7}} | collective-permute-start | bytes 3932168 | tf_op jit(solution)/shard_map/ppermute | solution.py:314
  372.6 35.3 %collective-permute-start.16 = (bf16[640,1024]{1,0:T(8,128)(2,1)}, bf16[640,1024]{1,0:T(8,128)(2,1)}, u32[]{:S(2)}, u32[]{:S(2)}) collective-permute-start(bf16[640,1024]{1,0:T(8,128)(2,1)} %add.245), channel_id=1, source_target_pairs={{0,8},{8,16},{16,24},{1,9},{9,17},{17,25},{2,10},{10,18},{18,26},{... | collective-permute-start | bytes 3932168 | tf_op jit(solution)/shard_map/ppermute | solution.py:327
  412.2 27.7 %all-to-all-start.2 = ((bf16[8,96,1024]{2,1,0:T(8,128)(2,1)}), bf16[8,96,1024]{2,1,0:T(8,128)(2,1)}, u32[]{:S(2)}, u32[]{:S(2)}) async-start(bf16[8,96,1024]{2,1,0:T(8,128)(2,1)} %fusion.16), calls=%async_computation.2 | async-start | bytes 3145728 | tf_op jit(solution)/shard_map/all_to_all | solution.py:504
  416.5 279.9 %reduce-scatter.11.cloned.1.call-start = ((), (), s32[]{:S(2)}) async-start(), calls=%async_computation.15 | async-start | bytes 2359296 | tf_op jit(solution)/shard_map/reduce_scatter | solution.py:476
  418.8 87.6 %collective-permute-start.22 = (bf16[640,1024]{1,0:T(8,128)(2,1)}, bf16[640,1024]{1,0:T(8,128)(2,1)}, u32[]{:S(2)}, u32[]{:S(2)}) collective-permute-start(bf16[640,1024]{1,0:T(8,128)(2,1)} %get-tuple-element.147), channel_id=1, source_target_pairs={{16,0},{24,8},{0,16},{8,24},{17,1},{25,9},{1,17},{9,25},{18,2},{26... | collective-permute-start | bytes 3932168 | tf_op jit(solution)/shard_map/ppermute | solution.py:344
  418.8 60.0 %collective-permute-start.21 = (bf16[640,1024]{1,0:T(8,128)(2,1)}, bf16[640,1024]{1,0:T(8,128)(2,1)}, u32[]{:S(2)}, u32[]{:S(2)}) collective-permute-start(bf16[640,1024]{1,0:T(8,128)(2,1)} %get-tuple-element.143), channel_id=1, source_target_pairs={{24,0},{0,8},{8,16},{16,24},{25,1},{1,9},{9,17},{17,25},{26,2},{2,... | collective-permute-start | bytes 3932168 | tf_op jit(solution)/shard_map/ppermute | solution.py:344
  418.9 95.9 %collective-permute-start.23 = (bf16[640,1024]{1,0:T(8,128)(2,1)}, bf16[640,1024]{1,0:T(8,128)(2,1)}, u32[]{:S(2)}, u32[]{:S(2)}) collective-permute-start(bf16[640,1024]{1,0:T(8,128)(2,1)} %get-tuple-element.154), channel_id=1, source_target_pairs={{8,0},{16,8},{24,16},{0,24},{9,1},{17,9},{25,17},{1,25},{10,2},{18... | collective-permute-start | bytes 3932168 | tf_op jit(solution)/shard_map/ppermute | solution.py:344
  453.6 267.6 %reduce-scatter.9.cloned.1.call-start = ((), (), s32[]{:S(2)}) async-start(), calls=%async_computation.14 | async-start | bytes 7077888 | tf_op jit(solution)/shard_map/reduce_scatter | solution.py:476
  515.7 120.8 %collective-permute-start.47 = (bf16[128,1024]{1,0:T(8,128)(2,1)}, bf16[128,1024]{1,0:T(8,128)(2,1)}, u32[]{:S(2)}, u32[]{:S(2)}) collective-permute-start(bf16[128,1024]{1,0:T(8,128)(2,1)} %get-tuple-element.185), channel_id=1, source_target_pairs={{24,0},{0,8},{8,16},{16,24},{25,1},{1,9},{9,17},{17,25},{26,2},{2,... | collective-permute-start | bytes 786440 | tf_op jit(solution)/shard_map/ppermute | solution.py:344
  574.3 55.8 %collective-permute-start.41 = (bf16[32,4096]{1,0:T(8,128)(2,1)}, bf16[32,4096]{1,0:T(8,128)(2,1)}, u32[]{:S(2)}, u32[]{:S(2)}) collective-permute-start(bf16[32,4096]{1,0:T(8,128)(2,1)} %get-tuple-element.188), channel_id=1, source_target_pairs={{24,0},{0,8},{8,16},{16,24},{25,1},{1,9},{9,17},{17,25},{26,2},{2,... | collective-permute-start | bytes 786440 | tf_op jit(solution)/shard_map/ppermute | solution.py:344
  574.4 56.1 %collective-permute-start.42 = (bf16[32,4096]{1,0:T(8,128)(2,1)}, bf16[32,4096]{1,0:T(8,128)(2,1)}, u32[]{:S(2)}, u32[]{:S(2)}) collective-permute-start(bf16[32,4096]{1,0:T(8,128)(2,1)} %get-tuple-element.190), channel_id=1, source_target_pairs={{16,0},{24,8},{0,16},{8,24},{17,1},{25,9},{1,17},{9,25},{18,2},{26... | collective-permute-start | bytes 786440 | tf_op jit(solution)/shard_map/ppermute | solution.py:344
  576.1 54.4 %collective-permute-start.43 = (bf16[32,4096]{1,0:T(8,128)(2,1)}, bf16[32,4096]{1,0:T(8,128)(2,1)}, u32[]{:S(2)}, u32[]{:S(2)}) collective-permute-start(bf16[32,4096]{1,0:T(8,128)(2,1)} %get-tuple-element.189), channel_id=1, source_target_pairs={{8,0},{16,8},{24,16},{0,24},{9,1},{17,9},{25,17},{1,25},{10,2},{18... | collective-permute-start | bytes 786440 | tf_op jit(solution)/shard_map/ppermute | solution.py:344
  603.3 107.7 %all-to-all-start.3 = ((bf16[8,80,1024]{2,1,0:T(8,128)(2,1)}), bf16[8,80,1024]{2,1,0:T(8,128)(2,1)}, u32[]{:S(2)}, u32[]{:S(2)}) async-start(bf16[8,80,1024]{2,1,0:T(8,128)(2,1)} %bitcast.152), calls=%async_computation.5 | async-start | bytes 2621440 | tf_op jit(solution)/shard_map/all_to_all | solution.py:534
  631.8 27.8 %collective-permute-start.44 = (bf16[32,4096]{1,0:T(8,128)(2,1)S(1)}, bf16[32,4096]{1,0:T(8,128)(2,1)S(1)}, u32[]{:S(2)}, u32[]{:S(2)}) collective-permute-start(bf16[32,4096]{1,0:T(8,128)(2,1)S(1)} %get-tuple-element.174), channel_id=1, source_target_pairs={{8,0},{16,8},{24,16},{0,24},{9,1},{17,9},{25,17},{1,25},{10,2},{18... | collective-permute-start | bytes 786440 | tf_op jit(solution)/shard_map/ppermute | solution.py:344
  656.7 33.6 %collective-permute-start.51 = (bf16[128,1024]{1,0:T(8,128)(2,1)S(1)}, bf16[128,1024]{1,0:T(8,128)(2,1)S(1)}, u32[]{:S(2)}, u32[]{:S(2)}) collective-permute-start(bf16[128,1024]{1,0:T(8,128)(2,1)S(1)} %get-tuple-element.172), channel_id=1, source_target_pairs={{16,0},{24,8},{0,16},{8,24},{17,1},{25,9},{1,17},{9,25},{18,2},{26... | collective-permute-start | bytes 786440 | tf_op jit(solution)/shard_map/ppermute | solution.py:344
  656.7 33.6 %collective-permute-start.52 = (bf16[128,1024]{1,0:T(8,128)(2,1)S(1)}, bf16[128,1024]{1,0:T(8,128)(2,1)S(1)}, u32[]{:S(2)}, u32[]{:S(2)}) collective-permute-start(bf16[128,1024]{1,0:T(8,128)(2,1)S(1)} %get-tuple-element.172), channel_id=1, source_target_pairs={{24,0},{0,8},{8,16},{16,24},{25,1},{1,9},{9,17},{17,25},{26,2},{2,... | collective-permute-start | bytes 786440 | tf_op jit(solution)/shard_map/ppermute | solution.py:344
  657.3 37.0 %collective-permute-start.45 = (bf16[32,4096]{1,0:T(8,128)(2,1)S(1)}, bf16[32,4096]{1,0:T(8,128)(2,1)S(1)}, u32[]{:S(2)}, u32[]{:S(2)}) collective-permute-start(bf16[32,4096]{1,0:T(8,128)(2,1)S(1)} %get-tuple-element.174), channel_id=1, source_target_pairs={{16,0},{24,8},{0,16},{8,24},{17,1},{25,9},{1,17},{9,25},{18,2},{26... | collective-permute-start | bytes 786440 | tf_op jit(solution)/shard_map/ppermute | solution.py:344
  659.6 34.8 %collective-permute-start.46 = (bf16[32,4096]{1,0:T(8,128)(2,1)S(1)}, bf16[32,4096]{1,0:T(8,128)(2,1)S(1)}, u32[]{:S(2)}, u32[]{:S(2)}) collective-permute-start(bf16[32,4096]{1,0:T(8,128)(2,1)S(1)} %get-tuple-element.174), channel_id=1, source_target_pairs={{24,0},{0,8},{8,16},{16,24},{25,1},{1,9},{9,17},{17,25},{26,2},{2,... | collective-permute-start | bytes 786440 | tf_op jit(solution)/shard_map/ppermute | solution.py:344
  (88 other events, 1341.4 us)
Sparse Core Ops, SparseCore 0:
  9.9 60.4 all-gather.4
  72.3 27.8 all-gather.6
  102.1 66.0 all-gather.10
  170.0 54.3 all-gather.8
  272.0 92.2 reduce-scatter.4
  367.9 82.1 reduce-scatter.6
  453.7 38.1 reduce-scatter.10
  578.3 75.7 reduce-scatter.8

commit v3 on v2

--- a/solution.py
+++ b/solution.py
@@ -290,6 +290,313 @@
     )(*mids, *pgs, *acts, *egs)
 
 
+def exchange_kernel(
+    waves, layers, groups, slots_ref, *refs
+):
+    g_refs = refs[:layers]
+    mix_ref, up_ref, down_ref, back_ref, slab_ref = refs[layers : layers + 5]
+    po_refs = refs[layers + 5 : 2 * layers + 5]
+    (
+        du_ref, dd_ref, buf, part, got, act_s, pg_s, eg_s, home, home_slab,
+        a_send, a_recv, z_send, z_recv, r_send, r_recv, b_send, b_recv,
+    ) = refs[2 * layers + 5 :]
+    each = groups // waves
+    capacity, width = slots_ref.shape[1:]
+    rows = each * capacity
+    last = layers - 1
+    here, me = lax.axis_index("dp"), lax.axis_index("ep")
+    up_id, down_id = lax.rem(here + 1, layers), lax.rem(here + last, layers)
+    peer = lambda j: lax.rem(me + j, groups)
+    source = lambda j: lax.rem(me + groups - j, groups)
+    mesh_id = pl.DeviceIdType.MESH
+
+    def a_copy(j):
+        return pltpu.make_async_remote_copy(
+            slots_ref.at[peer(j)], buf.at[j // each, 0, lax.rem(j, each)],
+            a_send.at[j], a_recv.at[j], device_id={"ep": peer(j)}, device_id_type=mesh_id,
+        )
+
+    def z_copy(w, way, s):
+        src, dst = ((layers - s + 1) % layers, layers - s) if way == 0 else (s - 1, s)
+        return pltpu.make_async_remote_copy(
+            buf.at[w, src], buf.at[w, dst], z_send.at[w, way, s - 1], z_recv.at[w, way, s - 1],
+            device_id={"dp": up_id if way == 0 else down_id}, device_id_type=mesh_id,
+        )
+
+    def r_copy(w, way, s):
+        return pltpu.make_async_remote_copy(
+            part.at[w, layers - s if way == 0 else s], got.at[w, way, s - 1],
+            r_send.at[w, way, s - 1], r_recv.at[w, way, s - 1],
+            device_id={"dp": up_id if way == 0 else down_id}, device_id_type=mesh_id,
+        )
+
+    def b_copies(j):
+        w, i = j // each, lax.rem(j, each)
+        start = pl.multiple_of(i * capacity, 16)
+        return [
+            pltpu.make_async_remote_copy(
+                src, dst, b_send.at[j, n], b_recv.at[j, n],
+                device_id={"ep": source(j)}, device_id_type=mesh_id,
+            )
+            for n, (src, dst) in enumerate(
+                (
+                    (part.at[w, 0, pl.ds(start, capacity)], home.at[j]),
+                    (part.at[w, 0, pl.ds(rows, 16)], home_slab.at[j]),
+                )
+            )
+        ]
+
+    def z_sends(way, s):
+        if way == 0:
+            return jnp.logical_and(here <= last - 1, here >= s - 1)
+        return jnp.logical_and(here >= 1, here <= layers - s)
+
+    def z_gets(way, s):
+        return here >= s if way == 0 else here <= last - s
+
+    def r_sends(way, s):
+        return here <= s - 1 if way == 0 else here >= layers - s
+
+    def r_gets(way, s):
+        if way == 0:
+            return jnp.logical_and(here >= 1, here <= s)
+        return jnp.logical_and(here >= last - s, here <= last - 1)
+
+    part[...] = jnp.zeros_like(part)
+    got[:, :, last - 1] = jnp.zeros_like(got[:, :, last - 1])
+    du_ref[...] = jnp.zeros_like(du_ref)
+    dd_ref[...] = jnp.zeros_like(dd_ref)
+
+    barrier = pltpu.get_barrier_semaphore()
+
+    def greet(j, carry):
+        pl.semaphore_signal(barrier, inc=1, device_id={"ep": peer(j)}, device_id_type=mesh_id)
+        return carry
+
+    lax.fori_loop(1, groups, greet, 0)
+
+    @pl.when(here < last)
+    def _():
+        pl.semaphore_signal(barrier, inc=1, device_id={"dp": up_id}, device_id_type=mesh_id)
+
+    @pl.when(here > 0)
+    def _():
+        pl.semaphore_signal(barrier, inc=1, device_id={"dp": down_id}, device_id_type=mesh_id)
+
+    pl.semaphore_wait(barrier, groups - 1 + jnp.where(here < last, 1, 0) + jnp.where(here > 0, 1, 0))
+
+    def over(first, count, act):
+        lax.fori_loop(first, count, lambda j, c: (act(j), c)[1], 0)
+
+    over(1, groups, lambda j: a_copy(j).start())
+    buf[0, 0, 0] = slots_ref[me]
+
+    def slab_of(row):
+        high = row.astype(BF16).astype(F32)
+        line = lax.broadcasted_iota(jnp.int32, (16, rows), 0)
+        return jnp.where(line == 0, high, jnp.where(line == 1, row - high, 0.0)).astype(BF16)
+
+    def piece(w, ks):
+        mid = jnp.concatenate([buf[w, k].reshape(rows, width) for k in ks], axis=0)
+        g = jnp.concatenate(
+            [g_refs[k][source(w * each + i)] for k in ks for i in range(each)], axis=0
+        ).astype(F32)
+        logits = dot_nn(mid, mix_ref[...])
+        share = 1.0 / (1.0 + jnp.exp(logits[:, 0:1] - logits[:, 1:2]))
+        eg = (share * g).astype(BF16)
+        act, slope = gelu_pair(dot_nn(mid, up_ref[...]))
+        act = act.astype(BF16)
+        pg = (dot_nt(eg, down_ref[...]) * slope).astype(BF16)
+        pi = dot_nt(pg, up_ref[...]).astype(BF16)
+        po = dot_nn(act, down_ref[...])
+        sums = jnp.sum(po * g, axis=-1, keepdims=True)
+        po = po.astype(BF16)
+        diag = lax.broadcasted_iota(jnp.int32, (rows, rows), 0) == lax.broadcasted_iota(
+            jnp.int32, (rows, rows), 1
+        )
+        for n, k in enumerate(ks):
+            mine = slice(n * rows, (n + 1) * rows)
+            spot = slice(k * rows, (k + 1) * rows)
+            eg_s[spot] = eg[mine]
+            act_s[spot] = act[mine]
+            pg_s[spot] = pg[mine]
+            part[w, k, 0:rows] = pi[mine]
+            line = jnp.sum(jnp.where(diag, sums[mine], 0.0), axis=0, keepdims=True)
+            part[w, k, rows : rows + 16, 0:rows] = slab_of(line)
+            for i in range(each):
+                at = n * rows + i * capacity
+                po_refs[k][source(w * each + i)] = po[at : at + capacity]
+
+    def weight_grads(w):
+        mid = buf[w].reshape(layers * rows, width)
+        du_ref[...] += dot_tn(mid, pg_s[...])
+        dd_ref[...] += dot_tn(act_s[...], eg_s[...])
+
+    def add_to(w, k, pieces):
+        total = part[w, k, 0:rows].astype(F32)
+        extra = part[w, k, rows : rows + 16, 0:rows].astype(F32)
+        for way, s in pieces:
+            total = total + got[w, way, s - 1, 0:rows].astype(F32)
+            extra = extra + got[w, way, s - 1, rows : rows + 16, 0:rows].astype(F32)
+        part[w, k, 0:rows] = total.astype(BF16)
+        part[w, k, rows : rows + 16, 0:rows] = slab_of(jnp.sum(extra, axis=0, keepdims=True))
+
+    def start_hop(copy, sends, w, s):
+        for way in range(2):
+            pl.when(sends(way, s))(lambda way=way: copy(w, way, s).start())
+
+    def get_hop(copy, gets, w, s):
+        for way in range(2):
+            pl.when(gets(way, s))(lambda way=way: copy(w, way, s).wait_recv())
+
+    def pass_on(w, s):
+        for way in range(2):
+
+            @pl.when(r_gets(way, s))
+            def _():
+                r_copy(w, way, s).wait_recv()
+                add_to(w, layers - s - 1 if way == 0 else s + 1, [(way, s)])
+
+        start_hop(r_copy, r_sends, w, s + 1)
+
+    def finish(w):
+        get_hop(r_copy, r_gets, w, last)
+        add_to(w, 0, [(0, last), (1, last)])
+        for i in range(each):
+            j = w * each + i
+            start = i * capacity
+
+            @pl.when(j > 0)
+            def _():
+                for copy in b_copies(j):
+                    copy.start()
+
+            @pl.when(j == 0)
+            def _():
+                home[0] = part[0, 0, start : start + capacity]
+                home_slab[0] = part[0, 0, rows : rows + 16]
+
+    far = [1, last]
+    near = [k for k in range(layers) if k not in far]
+
+    def body(i, carry):
+        w = i - 1
+        gathers = i < waves
+        works = jnp.logical_and(i >= 1, i <= waves)
+
+        @pl.when(gathers)
+        def _():
+            for n in range(each):
+                pl.when(i * each + n > 0)(lambda n=n: a_copy(i * each + n).wait_recv())
+            start_hop(z_copy, z_sends, i, 1)
+
+        @pl.when(works)
+        def _():
+            piece(w, far)
+            start_hop(r_copy, r_sends, w, 1)
+
+        @pl.when(i >= 2)
+        def _():
+            finish(i - 2)
+
+        for s in range(1, last):
+
+            @pl.when(gathers)
+            def _():
+                get_hop(z_copy, z_gets, i, s)
+                start_hop(z_copy, z_sends, i, s + 1)
+
+            @pl.when(works)
+            def _():
+                if s == 1:
+                    piece(w, near)
+                if s == last - 1:
+                    weight_grads(w)
+                pass_on(w, s)
+
+        @pl.when(gathers)
+        def _():
+            get_hop(z_copy, z_gets, i, last)
+
+        return carry
+
+    lax.fori_loop(0, waves + 2, body, 0)
+
+    def land(j, carry):
+        for copy in b_copies(j):
+            copy.wait_recv()
+            copy.wait_send()
+        a_copy(j).wait_send()
+        return carry
+
+    lax.fori_loop(1, groups, land, 0)
+
+    def sent(w, carry):
+        for way in range(2):
+            for s in range(1, layers):
+                pl.when(z_sends(way, s))(lambda: z_copy(w, way, s).wait_send())
+                pl.when(r_sends(way, s))(lambda: r_copy(w, way, s).wait_send())
+        return carry
+
+    lax.fori_loop(0, waves, sent, 0)
+
+    def arrange(j, carry):
+        back_ref[peer(j)] = home[j]
+        slab_ref[peer(j)] = home_slab[j]
+        return carry
+
+    lax.fori_loop(0, groups, arrange, 0)
+
+
+def exchange_waves(groups):
+    return 4 if groups % 4 == 0 else 1
+
+
+def expert_exchange(slots, gs, mix_pad, up, down):
+    layers, groups = lax.axis_size("dp"), lax.axis_size("ep")
+    waves = exchange_waves(groups)
+    each = groups // waves
+    _, capacity, width = slots.shape
+    hidden = up.shape[1]
+    rows = each * capacity
+    sem = pltpu.SemaphoreType.DMA
+    block = jax.ShapeDtypeStruct((groups, capacity, width), BF16)
+    vmem = pl.BlockSpec(memory_space=pltpu.VMEM)
+    total_rows = layers * groups * capacity
+    outs = pl.pallas_call(
+        functools.partial(exchange_kernel, waves, layers, groups),
+        in_specs=[vmem] * (4 + layers),
+        out_specs=[vmem] * (4 + layers),
+        out_shape=[block, jax.ShapeDtypeStruct((groups, 16, width), BF16)]
+        + [block] * layers
+        + [jax.ShapeDtypeStruct((width, hidden), F32), jax.ShapeDtypeStruct((hidden, width), F32)],
+        scratch_shapes=[
+            pltpu.VMEM((waves, layers, each, capacity, width), BF16),
+            pltpu.VMEM((waves, layers, rows + 16, width), BF16),
+            pltpu.VMEM((waves, 2, layers - 1, rows + 16, width), BF16),
+            pltpu.VMEM((layers * rows, hidden), BF16),
+            pltpu.VMEM((layers * rows, hidden), BF16),
+            pltpu.VMEM((layers * rows, width), BF16),
+            pltpu.VMEM((groups, capacity, width), BF16),
+            pltpu.VMEM((groups, 16, width), BF16),
+            sem((groups,)),
+            sem((groups,)),
+            sem((waves, 2, layers - 1)),
+            sem((waves, 2, layers - 1)),
+            sem((waves, 2, layers - 1)),
+            sem((waves, 2, layers - 1)),
+            sem((groups, 2)),
+            sem((groups, 2)),
+        ],
+        compiler_params=pltpu.CompilerParams(
+            collective_id=0, has_side_effects=True, vmem_limit_bytes=62 << 20
+        ),
+        cost_estimate=cost(12 * total_rows * width * hidden, 20 * total_rows * width),
+        name="expert_exchange",
+    )(slots, *gs, mix_pad, up, down)
+    return outs[0], outs[1], outs[2 : 2 + layers], outs[2 + layers], outs[3 + layers]
+
+
 def normalise(values_in):
     centred = values_in - jnp.mean(values_in, axis=-1, keepdims=True)
     inverse = lax.rsqrt(jnp.mean(centred * centred, axis=-1, keepdims=True) + 1e-05)
@@ -327,13 +634,11 @@
     return lax.ppermute(rows, "dp", pairs)
 
 
-def line_reduce(parts, work):
+def line_reduce(parts):
     size = lax.axis_size("dp")
     up = send_hop(parts[size - 1], 1, 1)
     down = send_hop(parts[1], -1, 1)
     for stage in range(2, size):
-        if stage - 2 < len(work):
-            up, down = after((up, down), work[stage - 2])
         up = send_hop(up + parts[size - stage], 1, stage)
         down = send_hop(down + parts[stage], -1, stage)
     return parts[0].astype(F32) + up.astype(F32) + down.astype(F32)
@@ -396,12 +701,6 @@
     slots = experts * capacity
     gather = lambda w: lax.all_gather(w, "ep", axis=0, tiled=True)
     exchange_out = lambda a: lax.all_to_all(a, "ep", split_axis=0, concat_axis=1, tiled=True)
-    qkv_full, out_full, up_full, down_full = (
-        gather(qkv_weight),
-        gather(out_weight),
-        gather(up_weight),
-        gather(down_weight),
-    )
     expert_up2 = expert_up[0]
     expert_down2 = expert_down[0]
     mix_pad = jnp.pad(mix_weight, ((0, 0), (0, 126)))
@@ -422,9 +721,14 @@
     unit1, inverse1 = normalise(token_rows)
     normed_in = (unit1 * ln1_gain).astype(BF16)
     g_own = exchange_out(pick(cotangent)).reshape(slots, width)
-    normed_in, g_own = lax.optimization_barrier((normed_in, g_own))
+    normed_in, g_own, qkv_weight = lax.optimization_barrier((normed_in, g_own, qkv_weight))
+    qkv_full, out_full, up_full, down_full = (
+        gather(qkv_weight),
+        gather(out_weight),
+        gather(up_weight),
+        gather(down_weight),
+    )
     g_low, g_high = [g_own], [g_own]
-    mid_low_hops, mid_high_hops = [], []
 
     def step(lows, highs, *others):
         stage = len(lows)
@@ -445,68 +749,64 @@
     mid_low = (unit2 * ln2_gain).astype(BF16)
     mid_slots = pick(mid_low)
     (mid_slots,) = step(g_low, g_high, mid_slots)
-    mid_own = exchange_out(mid_slots).reshape(slots, width)
-    (mid_own,) = step(g_low, g_high, mid_own)
+    step(g_low, g_high)
     gs = [g_own] + join(g_low, g_high)
-    m_low, m_high = [mid_own], [mid_own]
-    step(m_low, m_high)
-
-    chunk = lambda mid, g: expert_chunk(mid, g, mix_pad, expert_up2, expert_down2)
-    chunks = {0: chunk(mid_own, g_own)}
-    step(m_low, m_high, chunks[0][0])
 
     grad_out = cotangent.astype(F32)
     logits = dot_nn(mid_low, mix_weight)
     mix1 = 1.0 / (1.0 + jnp.exp(logits[:, 0:1] - logits[:, 1:2]))
     mix0 = 1.0 / (1.0 + jnp.exp(logits[:, 1:2] - logits[:, 0:1]))
     dense_grad = (mix0 * grad_out).astype(BF16)
-    while len(m_low) < layers:
-        dense_grad, = step(m_low, m_high, dense_grad)
-    mids = {0: mid_own}
-    middle = layers // 2
-    mids[middle] = m_high[middle] + m_low[layers - middle]
-    chunks[middle] = chunk(mids[middle], gs[middle])
-    for k in [layers - 1] + list(range(1, layers - 1)):
-        if k != middle:
-            mids[k] = m_high[k] + m_low[layers - k]
-            chunks[k] = chunk(mids[k], gs[k])
-    mids = [mids[k] for k in range(layers)]
-    chunks = [chunks[k] for k in range(layers)]
+    scatter = lambda a: lax.psum_scatter(a.astype(BF16), "ep", scatter_dimension=0, tiled=True)
     back = lambda k, a: shifted(a, layers - k) if k else a
-    scatter = lambda a: lax.psum_scatter(a.astype(BF16), "ep", scatter_dimension=0, tiled=True)
-    dense_out, mid_grad_dense, up_grad, down_grad = dense_branch(
-        mid_low, after(dense_grad, chunks[1][0]), up_full, down_full
-    )
-    up_shard = scatter(up_grad)
-    down_shard = scatter(after(down_grad, chunks[1][0]))
-    expert_up_grad, expert_down_grad = expert_weight_grads(
-        mids,
-        [c[3] for c in chunks],
-        [c[2] for c in chunks],
-        [after(chunks[0][4], dense_out)] + [c[4] for c in chunks[1:]],
-    )
-    in_total = line_reduce([c[1] for c in chunks], [dense_out, expert_up_grad])
-    dots = [back(k, chunks[k][5].reshape(groups, capacity)) for k in range(layers)]
-    outs = [chunks[0][0]] + [back(k, after(chunks[k][0], in_total)) for k in range(1, layers)]
+
     def total(parts):
         acc = parts[0].astype(F32)
         for part in parts[1:]:
             acc = acc + part.astype(F32)
         return acc
 
-    dot_sum = total(dots)
-    dot_high = lax.reduce_precision(dot_sum, 8, 7)
-    dot_low = dot_sum - dot_high
-    extra = jnp.stack([dot_high, dot_low], axis=1)
-    extra = jnp.pad(extra, ((0, 0), (0, 14), (0, width - capacity)))
-    in_sum = in_total.reshape(groups, capacity, width)
-    packed = jnp.concatenate([in_sum, extra], axis=1).astype(BF16)
-    returned = lax.all_to_all(packed, "ep", split_axis=0, concat_axis=0, tiled=True)
-    returned, up_shard = lax.optimization_barrier((returned, up_shard))
-    in_rows = returned[:, :capacity].reshape(slots, width)
-    dot_back = (
-        returned[:, capacity, :capacity].astype(F32) + returned[:, capacity + 1, :capacity].astype(F32)
-    ).reshape(1, slots)
+    if capacity % 16 == 0:
+        blocks = [g.reshape(groups, capacity, width) for g in gs]
+        returned, slab, partial_outs, expert_up_grad, expert_down_grad = expert_exchange(
+            mid_slots, blocks, mix_pad, expert_up2, expert_down2
+        )
+        each = groups // exchange_waves(groups)
+        offset = lax.rem(
+            jnp.arange(groups, dtype=jnp.int32) + groups - lax.axis_index("ep"), groups
+        )
+        spot = lax.rem(offset, each)[:, None] == jnp.arange(each, dtype=jnp.int32)[None, :]
+        lines = slab[:, 0, : each * capacity].astype(F32) + slab[:, 1, : each * capacity].astype(F32)
+        dot_back = jnp.sum(
+            jnp.where(spot[:, :, None], lines.reshape(groups, each, capacity), 0.0), axis=1
+        ).reshape(1, slots)
+        dense_grad, returned = lax.optimization_barrier((dense_grad, returned))
+        outs = [a.reshape(slots, width) for a in partial_outs]
+    else:
+        mid_own = exchange_out(mid_slots).reshape(slots, width)
+        mids = [mid_own] + [shifted(mid_own, k) for k in range(1, layers)]
+        chunks = [expert_chunk(mids[k], gs[k], mix_pad, expert_up2, expert_down2) for k in range(layers)]
+        in_total = line_reduce([c[1] for c in chunks])
+        dot_sum = total([back(k, chunks[k][5].reshape(groups, capacity)) for k in range(layers)])
+        dot_high = lax.reduce_precision(dot_sum, 8, 7)
+        extra = jnp.stack([dot_high, dot_sum - dot_high], axis=1)
+        extra = jnp.pad(extra, ((0, 0), (0, 14), (0, width - capacity)))
+        packed = jnp.concatenate([in_total.reshape(groups, capacity, width), extra], axis=1)
+        both = lax.all_to_all(packed.astype(BF16), "ep", split_axis=0, concat_axis=0, tiled=True)
+        returned = both[:, :capacity]
+        dot_back = (
+            both[:, capacity, :capacity].astype(F32) + both[:, capacity + 1, :capacity].astype(F32)
+        ).reshape(1, slots)
+        outs = [c[0] for c in chunks]
+        expert_up_grad, expert_down_grad = expert_weight_grads(
+            mids, [c[3] for c in chunks], [c[2] for c in chunks], [c[4] for c in chunks]
+        )
+
+    dense_out, mid_grad_dense, up_grad, down_grad = dense_branch(mid_low, dense_grad, up_full, down_full)
+    up_shard = scatter(up_grad)
+    down_shard = scatter(after(down_grad, up_shard))
+    outs = [back(k, outs[k]) for k in range(layers)]
+    in_rows = returned.reshape(slots, width)
     mix_dot1 = jnp.sum(table.astype(F32) * dot_back, axis=1, keepdims=True)
     mix_dot0 = jnp.sum(grad_out * dense_out, axis=-1, keepdims=True)
     mean_dot = mix0 * mix_dot0 + mix1 * mix_dot1
@@ -520,16 +820,17 @@
     attn_out_grad = res_grad.astype(BF16)
     out_weight_grad = dot_tn(attended, attn_out_grad)
     attended_grad = dot_nt(attn_out_grad, out_full).astype(BF16)
-    attended_grad, outs[1] = lax.optimization_barrier((attended_grad, outs[1]))
     qkv_grad = attention_backward(qkv_rows, bucket, attended_grad, lse)
-    out_shard = scatter(after(out_weight_grad, up_shard))
-    qkv_grad, outs[2], down_shard = lax.optimization_barrier((qkv_grad, outs[2], down_shard))
+    out_shard = scatter(after(out_weight_grad, down_shard))
+    qkv_grad, up_shard, outs[1] = lax.optimization_barrier((qkv_grad, up_shard, outs[1]))
     qkv_weight_grad = dot_tn(normed_in, qkv_grad)
     normed_grad = dot_nt(qkv_grad, qkv_full)
     ln1_gain_grad = jnp.sum(normed_grad * unit1, axis=0)
     tokens_grad = res_grad + norm_backward(normed_grad, ln1_gain, unit1, inverse1)
 
-    up_shard, down_shard, *outs = after((up_shard, down_shard, *outs), qkv_weight_grad)
+    up_shard, down_shard, out_shard, *outs = after(
+        (up_shard, down_shard, out_shard, *outs), normed_grad
+    )
     out_sum = total(outs).astype(BF16).reshape(groups, capacity, width)
     out_back = lax.all_to_all(out_sum, "ep", split_axis=0, concat_axis=0, tiled=True)
     expert_out = dot_nn(table, out_back.reshape(slots, width))
@@ -537,8 +838,8 @@
 
     up_final = sum_layers(up_shard)
     down_final = sum_layers(down_shard)
-    out_final = sum_layers(after(out_shard, qkv_weight_grad))
-    qkv_final = sum_layers(scatter(qkv_weight_grad))
+    out_final = sum_layers(out_shard)
+    qkv_final = sum_layers(scatter(after(qkv_weight_grad, out_shard)))
     small_sums = sum_everywhere(
         jnp.concatenate([ln1_gain_grad[None], ln2_gain_grad[None], mix_weight_grad.T], axis=0)
     )

time: 779 us -> 811 us (1.041)
  Pallas kernels: 132 us -> 233 us
  starting transfers between devices: 158 us -> 87.1 us
  waiting for transfers between devices: 308 us -> 352 us
  blocking collectives: 22.9 us -> 0 us
  other arithmetic: 56.7 us -> 39.3 us
    reduce_scatter x4, waiting for transfers between devices: 0.04 us -> 108 us  [on_device(): lax.psum_scatter(a.astype(BF16), 'ep', scatter_dimension=0, tiled=True)]
    pallas_call x5 -> x1, Pallas kernels: 61.2 us -> 162 us  [expert_exchange(): pl.pallas_call(functools.partial(exchange_kernel, waves, layers, groups),...]
    ppermute x12 -> x6, waiting for transfers between devices: 87 us -> 32.2 us  [hop(): return lax.ppermute(rows, 'dp', pairs)]
    ppermute x5, waiting for transfers between devices: 32.4 us -> 80.1 us  [sum_everywhere(): lax.ppermute(values, axis, [(i, i ^ step) for i in range(size)])]
    ppermute x30 -> x27, waiting for transfers between devices: 117 us -> 74.2 us  [shifted(): lax.ppermute(rows, 'dp', [((i + step) % size, i) for i in range(size)])]
    ppermute x30 -> x27, starting transfers between devices: 99 us -> 59.3 us  [shifted(): lax.ppermute(rows, 'dp', [((i + step) % size, i) for i in range(size)])]
    all_to_all x1 -> x0, blocking collectives: 22.9 us -> none  [on_device(): lax.all_to_all(a, 'ep', split_axis=0, concat_axis=1, tiled=True)]
    all_gather x4, waiting for transfers between devices: 19.5 us -> 38 us  [on_device(): gather = lambda w: lax.all_gather(w, 'ep', axis=0, tiled=True)]
  transfers between devices with their start and end apart: 64 -> 48, of which waited for: 32 -> 22; matrix products, arithmetic and copies ran while one was open for 14% -> 11% of each run, Pallas kernels for 12% -> 24%
where the time goes in v3:
time: 811 us; the launch traced here: 803 us
  waiting for transfers between devices  352 us (43%)
  Pallas kernels  233 us (29%)
  starting transfers between devices  87.1 us (11%)
  matrix products  44.5 us (5%)
  other arithmetic  39.3 us (5%)
  local copies, waits for them, and re-layouts  31.6 us (4%)
  between operations  15.7 us (2%)
    pallas_call x1, Pallas kernels, expert_exchange(): pl.pallas_call(functools.partial(exchange_kernel, waves, layers, groups),...  162 us
    reduce_scatter x4, waiting for transfers between devices, on_device(): lax.psum_scatter(a.astype(BF16), 'ep', scatter_dimension=0, tiled=True)  108 us
    ppermute x5, waiting for transfers between devices, sum_everywhere(): lax.ppermute(values, axis, [(i, i ^ step) for i in range(size)])  80.1 us
    ppermute x27, waiting for transfers between devices, shifted(): lax.ppermute(rows, 'dp', [((i + step) % size, i) for i in range(size)])  74.2 us
    ppermute x27, starting transfers between devices, shifted(): lax.ppermute(rows, 'dp', [((i + step) % size, i) for i in range(size)])  59.3 us
    all_gather x4, waiting for transfers between devices, on_device(): gather = lambda w: lax.all_gather(w, 'ep', axis=0, tiled=True)  38 us
    pallas_call x1, Pallas kernels, dense_branch(): pl.pallas_call(dense_kernel, grid=(ff // tile,), in_specs=[whole, whole,...  36.8 us
    ppermute x6, waiting for transfers between devices, hop(): return lax.ppermute(rows, 'dp', pairs)  32.2 us
  transfers between devices with their start and end apart: 48, of which 22 were waited for; matrix products, arithmetic and copies ran while one was open for 11% of the time, Pallas kernels for 24%

profile of v3, /device:TPU:0, one launch (start us, length us, event | category | flops | bytes accessed | tf_op | source)
XLA Modules:
  0.0 803.3 jit_solution(11330641323767364349)
XLA Ops:
  12.1 5.3 all-to-all-start
  18.6 17.1 %all-to-all-done = bf16[8,80,1024]{2,1,0:T(8,128)(2,1)S(1)} async-done(((bf16[8,80,1024]{2,1,0:T(8,128)(2,1)}), bf16[8,80,1024]{2,1,0:T(8,128)(2,1)S(1)}, u32[]{:S(2)}, u32[]{:S(2)}) %all-to-all-start) | async-done | bytes 1310752 | tf_op jit(solution)/shard_map/all_to_all | solution.py:703
  37.8 4.6 collective-permute-start
  44.3 36.5 %all-gather.5.cloned.1.call-done = bf16[1024,3072]{1,0:T(8,128)(2,1)} async-done(((bf16[128,3072]{1,0:T(8,128)(2,1)}), bf16[1024,3072]{1,0:T(8,128)(2,1)}) %all-gather.5.cloned.1.call-update) | async-done | bytes 6291472 | tf_op jit(solution)/shard_map/all_gather | solution.py:702
  80.8 6.4 convolution_convert_fusion.q_ref.k_ref.v_ref
  90.3 15.8 %attn_fwd.1 = (bf16[512,1024]{1,0:T(8,128)(2,1)S(1)}, f32[512,1024]{1,0:T(8,128)S(1)}) custom-call(s32[1]{0:T(128)S(6)} %copy.56.flag_ref, bf16[512,3072]{1,0:T(8,128)(2,1)S(1)} %convolution_convert_fusion.q_ref.k_ref.v_ref, bf16[512,3072]{1,0:T(8,128)(2,1)S(1)} %convolution_convert_fusion.q_ref.k_ref.v_ref, ...), custom_call_target="tpu_custom_call" | custom-call | flops 2147483648 | bytes 5242880 | tf_op jit(solution)/shard_map/attn_fwd/pallas_call | solution.py:85
  116.9 7.4 collective-permute-done.3
  133.6 24.8 %collective-permute-done.5 = bf16[640,1024]{1,0:T(8,128)(2,1)} collective-permute-done((bf16[640,1024]{1,0:T(8,128)(2,1)}, bf16[640,1024]{1,0:T(8,128)(2,1)}, u32[]{:S(2)}, u32[]{:S(2)}) %collective-permute-start.5) | collective-permute-done | bytes 1310752 | tf_op jit(solution)/shard_map/ppermute | solution.py:621
  165.0 161.9 %expert_exchange.1 = (bf16[8,80,1024]{2,1,0:T(8,128)(2,1)}, bf16[8,16,1024]{2,1,0:T(8,128)(2,1)}, bf16[8,80,1024]{2,1,0:T(8,128)(2,1)}, bf16[8,80,1024]{2,1,0:T(...) custom-call(bf16[8,80,1024]{2,1,0:T(8,128)(2,1)} %bitcast.197, ...), custom_call_target="tpu_custom_call" | custom-call | flops 32212254720 | bytes 52428800 | tf_op jit(solution)/shard_map/expert_exchange/pallas_call | solution.py:566
  328.2 36.8 %dense_branch.1 = (f32[512,1024]{1,0:T(8,128)S(1)}, f32[512,1024]{1,0:T(8,128)}, bf16[1024,4096]{1,0:T(8,128)(2,1)}, bf16[4096,1024]{1,0:T(8,128)(2,1)}) custom-call(bf16[512,1024]{1,0:T(8,128)(2,1)S(1)} %multiply_convert_fusion.mid_ref, bf16[512,1024]{1,0:T(8,128)(2,1)S(1)} %copy-done.4, bf16[1024,4096]{1,0:T(8,128)(2,1)} %all-gather.9.cloned.1.call-done.up_ref, ...), custom_call_target="tpu_custom_call" | custom-call | flops 25769803776 | bytes 39845888 | tf_op jit(solution)/shard_map/dense_branch/pallas_call | solution.py:197
  366.4 70.4 %reduce-scatter.5.cloned.1.call-done = bf16[128,4096]{1,0:T(8,128)(2,1)} async-done(((bf16[1024,4096]{1,0:T(8,128)(2,1)}), bf16[128,4096]{1,0:T(8,128)(2,1)}) %reduce-scatter.5.cloned.1.call-update) | async-done | bytes 1048592 | tf_op jit(solution)/shard_map/reduce_scatter | solution.py:760
  455.2 18.9 %attn_bwd.1 = bf16[512,3072]{1,0:T(8,128)(2,1)S(1)} custom-call(s32[1]{0:T(128)S(6)} %copy.56.flag_ref, bf16[512,3072]{1,0:T(8,128)(2,1)S(1)} %copy-done.1, bf16[512,3072]{1,0:T(8,128)(2,1)S(1)} %copy-done.1, bf16[512,3072]{1,0:T(8,128)(2,1)S(1)} %copy-done.1, bf16[512,1024]{1,0:T(8,128)(2,1)S(1)} %convolution_convert_fusion.3.g_ref, f32[512,1024]{1,0:T(8,128)S(1)} %copy-done.6), custom_call_target="tpu_custom_call" | custom-call | flops 5368709120 | bytes 10485760 | tf_op jit(solution)/shard_map/attn_bwd/pallas_call | solution.py:148
  474.1 37.7 %reduce-scatter.7.cloned.1.call-done = bf16[512,1024]{1,0:T(8,128)(2,1)} async-done(((bf16[4096,1024]{1,0:T(8,128)(2,1)}), bf16[512,1024]{1,0:T(8,128)(2,1)}) %reduce-scatter.7.cloned.1.call-update) | async-done | bytes 1048592 | tf_op jit(solution)/shard_map/reduce_scatter | solution.py:760
  511.8 8.1 %fusion.11 = (f32[1024]{0:T(1024)S(1)}, f32[512]{0:T(512)S(1)}, f32[512]{0:T(512)S(1)}, f32[512,1024]{1,0:T(8,128)}) fusion(bf16[512,1024]{1,0:T(8,128)(2,1)} %param.13, f32[512]{0:T(512)S(1)} %add_rsqrt_fusion.1, f32[512]{0:T(512)S(1)} %broadcast_multiply_fusion.5, f32[1024]{0:T(1024)S(1)} %copy-done.26, bf16[512,3072]{1,0:T(8,128)(2,1)S(1)} %attn_bwd.1, ...), kind=kOutput, calls=%fused_computation.19 | convolution fusion | flops 3225942016 | bytes 12599296 | tf_op jit(solution)/shard_map/dot_general | solution.py:25
  526.4 6.8 fusion.49
  533.2 76.6 %collective-permute-done.10 = f32[4,1024]{1,0:T(4,128)S(1)} collective-permute-done((f32[4,1024]{1,0:T(4,128)S(1)}, f32[4,1024]{1,0:T(4,128)S(1)}, u32[]{:S(2)}, u32[]{:S(2)}) %collective-permute-start.10) | collective-permute-done | bytes 16416 | tf_op jit(solution)/shard_map/ppermute | solution.py:676
  616.1 4.7 fusion.10
  622.0 4.3 add_convert_fusion
  631.1 3.8 collective-permute-start.22
  639.6 7.5 collective-permute-done.21
  653.4 4.5 collective-permute-done.23
  658.5 9.1 %collective-permute-done.24 = bf16[32,1024]{1,0:T(8,128)(2,1)S(1)} collective-permute-done((bf16[32,1024]{1,0:T(8,128)(2,1)S(1)}, bf16[32,1024]{1,0:T(8,128)(2,1)S(1)}, u32[]{:S(2)}, u32[]{:S(2)}) %collective-permute-start.24) | collective-permute-done | bytes 65568 | tf_op jit(solution)/shard_map/ppermute | solution.py:649
  668.3 5.4 collective-permute-done.25
  681.7 9.0 %collective-permute-done.33 = bf16[128,1024]{1,0:T(8,128)(2,1)S(1)} collective-permute-done((bf16[128,1024]{1,0:T(8,128)(2,1)}, bf16[128,1024]{1,0:T(8,128)(2,1)S(1)}, u32[]{:S(2)}, u32[]{:S(2)}) %collective-permute-start.33) | collective-permute-done | bytes 262176 | tf_op jit(solution)/shard_map/ppermute | solution.py:649
  695.6 5.7 collective-permute-done.27
  702.6 6.8 collective-permute-start.31
  712.7 11.8 %collective-permute-start.37 = (bf16[128,1024]{1,0:T(8,128)(2,1)S(1)}, bf16[128,1024]{1,0:T(8,128)(2,1)S(1)}, u32[]{:S(2)}, u32[]{:S(2)}) collective-permute-start(bf16[128,1024]{1,0:T(8,128)(2,1)S(1)} %get-tuple-element.102), channel_id=1, source_target_pairs={{24,0},{0,8},{8,16},{16,24},{25,1},{1,9},{9,17},{17,25},{26,2},{2,... | collective-permute-start | bytes 786440 | tf_op jit(solution)/shard_map/ppermute | solution.py:649
  724.5 8.8 %collective-permute-done.37 = bf16[128,1024]{1,0:T(8,128)(2,1)S(1)} collective-permute-done((bf16[128,1024]{1,0:T(8,128)(2,1)S(1)}, bf16[128,1024]{1,0:T(8,128)(2,1)S(1)}, u32[]{:S(2)}, u32[]{:S(2)}) %collective-permute-start.37) | collective-permute-done | bytes 262176 | tf_op jit(solution)/shard_map/ppermute | solution.py:649
  739.8 6.2 collective-permute-start.14
  755.5 5.5 collective-permute-done.15
  762.8 5.2 collective-permute-start.17
  773.7 12.1 %collective-permute-done.18 = bf16[32,3072]{1,0:T(8,128)(2,1)S(1)} collective-permute-done((bf16[32,3072]{1,0:T(8,128)(2,1)}, bf16[32,3072]{1,0:T(8,128)(2,1)S(1)}, u32[]{:S(2)}, u32[]{:S(2)}) %collective-permute-start.18) | collective-permute-done | bytes 196640 | tf_op jit(solution)/shard_map/ppermute | solution.py:649
  (234 shorter events, 142.2 us)
Async XLA Ops:
  12.1 23.5 %all-to-all-start = ((bf16[8,80,1024]{2,1,0:T(8,128)(2,1)}), bf16[8,80,1024]{2,1,0:T(8,128)(2,1)S(1)}, u32[]{:S(2)}, u32[]{:S(2)}) async-start(bf16[8,80,1024]{2,1,0:T(8,128)(2,1)} %bitcast.158), calls=%async_computation | async-start | bytes 2621440 | tf_op jit(solution)/shard_map/all_to_all | solution.py:703
  17.4 63.3 %all-gather.5.cloned.1.call-start = ((), (), s32[]{:S(2)}) async-start(), calls=%async_computation.6 | async-start | bytes 7077888 | tf_op jit(solution)/shard_map/all_gather | solution.py:702
  35.7 74.9 %all-gather.7.cloned.1.call-start = ((), (), s32[]{:S(2)}) async-start(), calls=%async_computation.7 | async-start | bytes 2359296 | tf_op jit(solution)/shard_map/all_gather | solution.py:702
  36.4 290.5 %all-gather.9.cloned.1.call-start = ((), (), s32[]{:S(2)}) async-start(), calls=%async_computation.8 | async-start | bytes 9437184 | tf_op jit(solution)/shard_map/all_gather | solution.py:702
  37.2 289.8 %all-gather.11.cloned.1.call-start = ((), (), s32[]{:S(2)}) async-start(), calls=%async_computation.9 | async-start | bytes 9437184 | tf_op jit(solution)/shard_map/all_gather | solution.py:702
  37.8 399.0 %reduce-scatter.5.cloned.1.call-start = ((), (), s32[]{:S(2)}) async-start(), calls=%async_computation.10 | async-start | bytes 9437184 | tf_op jit(solution)/shard_map/reduce_scatter | solution.py:760
  37.8 49.4 %collective-permute-start = (bf16[640,1024]{1,0:T(8,128)(2,1)S(1)}, bf16[640,1024]{1,0:T(8,128)(2,1)}, u32[]{:S(2)}, u32[]{:S(2)}) collective-permute-start(bf16[640,1024]{1,0:T(8,128)(2,1)S(1)} %bitcast.156), channel_id=1, source_target_pairs={{0,8},{8,16},{16,24},{1,9},{9,17},{17,25},{2,10},{10,18},{18,26},{... | collective-permute-start | bytes 3932168 | tf_op jit(solution)/shard_map/ppermute | solution.py:621
  42.4 44.8 %collective-permute-start.1 = (bf16[640,1024]{1,0:T(8,128)(2,1)S(1)}, bf16[640,1024]{1,0:T(8,128)(2,1)}, u32[]{:S(2)}, u32[]{:S(2)}) collective-permute-start(bf16[640,1024]{1,0:T(8,128)(2,1)S(1)} %bitcast.157), channel_id=1, source_target_pairs={{8,0},{16,8},{24,16},{9,1},{17,9},{25,17},{10,2},{18,10},{26,18},{... | collective-permute-start | bytes 3932168 | tf_op jit(solution)/shard_map/ppermute | solution.py:621
  87.2 29.7 %collective-permute-start.2 = (bf16[640,1024]{1,0:T(8,128)(2,1)}, bf16[640,1024]{1,0:T(8,128)(2,1)}, u32[]{:S(2)}, u32[]{:S(2)}) collective-permute-start(bf16[640,1024]{1,0:T(8,128)(2,1)} %collective-permute-done), channel_id=1, source_target_pairs={{8,16},{16,24},{9,17},{17,25},{10,18},{18,26},{11,19},{19,27},{12,... | collective-permute-start | bytes 3932168 | tf_op jit(solution)/shard_map/ppermute | solution.py:621
  89.0 35.3 %collective-permute-start.3 = (bf16[640,1024]{1,0:T(8,128)(2,1)}, bf16[640,1024]{1,0:T(8,128)(2,1)}, u32[]{:S(2)}, u32[]{:S(2)}) collective-permute-start(bf16[640,1024]{1,0:T(8,128)(2,1)} %collective-permute-done.1), channel_id=1, source_target_pairs={{8,0},{16,8},{9,1},{17,9},{10,2},{18,10},{11,3},{19,11},{12,4},{20... | collective-permute-start | bytes 3932168 | tf_op jit(solution)/shard_map/ppermute | solution.py:621
  126.0 32.3 %collective-permute-start.5 = (bf16[640,1024]{1,0:T(8,128)(2,1)}, bf16[640,1024]{1,0:T(8,128)(2,1)}, u32[]{:S(2)}, u32[]{:S(2)}) collective-permute-start(bf16[640,1024]{1,0:T(8,128)(2,1)} %collective-permute-done.3), channel_id=1, source_target_pairs={{8,0},{9,1},{10,2},{11,3},{12,4},{13,5},{14,6},{15,7}} | collective-permute-start | bytes 3932168 | tf_op jit(solution)/shard_map/ppermute | solution.py:621
  366.4 145.4 %reduce-scatter.7.cloned.1.call-start = ((), (), s32[]{:S(2)}) async-start(), calls=%async_computation.11 | async-start | bytes 9437184 | tf_op jit(solution)/shard_map/reduce_scatter | solution.py:760
  436.8 185.1 %reduce-scatter.9.cloned.1.call-start = ((), (), s32[]{:S(2)}) async-start(), calls=%async_computation.12 | async-start | bytes 2359296 | tf_op jit(solution)/shard_map/reduce_scatter | solution.py:760
  438.1 36.0 %collective-permute-start.6 = (bf16[640,1024]{1,0:T(8,128)(2,1)}, bf16[640,1024]{1,0:T(8,128)(2,1)}, u32[]{:S(2)}, u32[]{:S(2)}) collective-permute-start(bf16[640,1024]{1,0:T(8,128)(2,1)} %bitcast.196), channel_id=1, source_target_pairs={{24,0},{0,8},{8,16},{16,24},{25,1},{1,9},{9,17},{17,25},{26,2},{2,... | collective-permute-start | bytes 3932168 | tf_op jit(solution)/shard_map/ppermute | solution.py:649
  521.5 100.5 %collective-permute-start.7 = (bf16[640,1024]{1,0:T(8,128)(2,1)}, bf16[640,1024]{1,0:T(8,128)(2,1)}, u32[]{:S(2)}, u32[]{:S(2)}) collective-permute-start(bf16[640,1024]{1,0:T(8,128)(2,1)} %bitcast.195), channel_id=1, source_target_pairs={{16,0},{24,8},{0,16},{8,24},{17,1},{25,9},{1,17},{9,25},{18,2},{26... | collective-permute-start | bytes 3932168 | tf_op jit(solution)/shard_map/ppermute | solution.py:649
  523.9 98.0 %collective-permute-start.8 = (bf16[640,1024]{1,0:T(8,128)(2,1)}, bf16[640,1024]{1,0:T(8,128)(2,1)}, u32[]{:S(2)}, u32[]{:S(2)}) collective-permute-start(bf16[640,1024]{1,0:T(8,128)(2,1)} %bitcast.194), channel_id=1, source_target_pairs={{8,0},{16,8},{24,16},{0,24},{9,1},{17,9},{25,17},{1,25},{10,2},{18... | collective-permute-start | bytes 3932168 | tf_op jit(solution)/shard_map/ppermute | solution.py:649
  524.4 85.3 %collective-permute-start.10 = (f32[4,1024]{1,0:T(4,128)S(1)}, f32[4,1024]{1,0:T(4,128)S(1)}, u32[]{:S(2)}, u32[]{:S(2)}) collective-permute-start(f32[4,1024]{1,0:T(4,128)S(1)} %fusion.41), channel_id=1, source_target_pairs={{0,16},{8,24},{16,0},{24,8},{1,17},{9,25},{17,1},{25,9},{2,18},{10... | collective-permute-start | bytes 49160 | tf_op jit(solution)/shard_map/ppermute | solution.py:676
  626.3 141.7 %all-to-all-start.1 = ((bf16[8,80,1024]{2,1,0:T(8,128)(2,1)}), bf16[8,80,1024]{2,1,0:T(8,128)(2,1)S(1)}, u32[]{:S(2)}, u32[]{:S(2)}) async-start(bf16[8,80,1024]{2,1,0:T(8,128)(2,1)} %bitcast.21), calls=%async_computation.4 | async-start | bytes 2621440 | tf_op jit(solution)/shard_map/all_to_all | solution.py:835
  630.0 108.6 %reduce-scatter.11.cloned.1.call-start = ((), (), s32[]{:S(2)}) async-start(), calls=%async_computation.13 | async-start | bytes 7077888 | tf_op jit(solution)/shard_map/reduce_scatter | solution.py:760
  635.8 59.8 %collective-permute-start.26 = (bf16[32,4096]{1,0:T(8,128)(2,1)}, bf16[32,4096]{1,0:T(8,128)(2,1)}, u32[]{:S(2)}, u32[]{:S(2)}) collective-permute-start(bf16[32,4096]{1,0:T(8,128)(2,1)} %get-tuple-element.114), channel_id=1, source_target_pairs={{24,0},{0,8},{8,16},{16,24},{25,1},{1,9},{9,17},{17,25},{26,2},{2,... | collective-permute-start | bytes 786440 | tf_op jit(solution)/shard_map/ppermute | solution.py:649
  636.9 58.7 %collective-permute-start.28 = (bf16[32,4096]{1,0:T(8,128)(2,1)}, bf16[32,4096]{1,0:T(8,128)(2,1)}, u32[]{:S(2)}, u32[]{:S(2)}) collective-permute-start(bf16[32,4096]{1,0:T(8,128)(2,1)} %get-tuple-element.115), channel_id=1, source_target_pairs={{8,0},{16,8},{24,16},{0,24},{9,1},{17,9},{25,17},{1,25},{10,2},{18... | collective-permute-start | bytes 786440 | tf_op jit(solution)/shard_map/ppermute | solution.py:649
  649.5 28.4 %collective-permute-start.32 = (bf16[128,1024]{1,0:T(8,128)(2,1)}, bf16[128,1024]{1,0:T(8,128)(2,1)}, u32[]{:S(2)}, u32[]{:S(2)}) collective-permute-start(bf16[128,1024]{1,0:T(8,128)(2,1)} %get-tuple-element.111), channel_id=1, source_target_pairs={{24,0},{0,8},{8,16},{16,24},{25,1},{1,9},{9,17},{17,25},{26,2},{2,... | collective-permute-start | bytes 786440 | tf_op jit(solution)/shard_map/ppermute | solution.py:649
  651.5 30.2 %collective-permute-start.34 = (bf16[128,1024]{1,0:T(8,128)(2,1)}, bf16[128,1024]{1,0:T(8,128)(2,1)}, u32[]{:S(2)}, u32[]{:S(2)}) collective-permute-start(bf16[128,1024]{1,0:T(8,128)(2,1)} %get-tuple-element.112), channel_id=1, source_target_pairs={{8,0},{16,8},{24,16},{0,24},{9,1},{17,9},{25,17},{1,25},{10,2},{18... | collective-permute-start | bytes 786440 | tf_op jit(solution)/shard_map/ppermute | solution.py:649
  673.7 17.0 %collective-permute-start.33 = (bf16[128,1024]{1,0:T(8,128)(2,1)}, bf16[128,1024]{1,0:T(8,128)(2,1)S(1)}, u32[]{:S(2)}, u32[]{:S(2)}) collective-permute-start(bf16[128,1024]{1,0:T(8,128)(2,1)} %get-tuple-element.113), channel_id=1, source_target_pairs={{16,0},{24,8},{0,16},{8,24},{17,1},{25,9},{1,17},{9,25},{18,2},{26... | collective-permute-start | bytes 786440 | tf_op jit(solution)/shard_map/ppermute | solution.py:649
  677.9 23.5 %collective-permute-start.27 = (bf16[32,4096]{1,0:T(8,128)(2,1)}, bf16[32,4096]{1,0:T(8,128)(2,1)S(1)}, u32[]{:S(2)}, u32[]{:S(2)}) collective-permute-start(bf16[32,4096]{1,0:T(8,128)(2,1)} %get-tuple-element.116), channel_id=1, source_target_pairs={{16,0},{24,8},{0,16},{8,24},{17,1},{25,9},{1,17},{9,25},{18,2},{26... | collective-permute-start | bytes 786440 | tf_op jit(solution)/shard_map/ppermute | solution.py:649
  691.9 32.5 %collective-permute-start.36 = (bf16[128,1024]{1,0:T(8,128)(2,1)S(1)}, bf16[128,1024]{1,0:T(8,128)(2,1)S(1)}, u32[]{:S(2)}, u32[]{:S(2)}) collective-permute-start(bf16[128,1024]{1,0:T(8,128)(2,1)S(1)} %get-tuple-element.102), channel_id=1, source_target_pairs={{16,0},{24,8},{0,16},{8,24},{17,1},{25,9},{1,17},{9,25},{18,2},{26... | collective-permute-start | bytes 786440 | tf_op jit(solution)/shard_map/ppermute | solution.py:649
  692.0 20.7 %collective-permute-start.35 = (bf16[128,1024]{1,0:T(8,128)(2,1)S(1)}, bf16[128,1024]{1,0:T(8,128)(2,1)S(1)}, u32[]{:S(2)}, u32[]{:S(2)}) collective-permute-start(bf16[128,1024]{1,0:T(8,128)(2,1)S(1)} %get-tuple-element.102), channel_id=1, source_target_pairs={{8,0},{16,8},{24,16},{0,24},{9,1},{17,9},{25,17},{1,25},{10,2},{18... | collective-permute-start | bytes 786440 | tf_op jit(solution)/shard_map/ppermute | solution.py:649
  702.6 34.2 %collective-permute-start.31 = (bf16[32,4096]{1,0:T(8,128)(2,1)S(1)}, bf16[32,4096]{1,0:T(8,128)(2,1)S(1)}, u32[]{:S(2)}, u32[]{:S(2)}) collective-permute-start(bf16[32,4096]{1,0:T(8,128)(2,1)S(1)} %get-tuple-element.104), channel_id=1, source_target_pairs={{24,0},{0,8},{8,16},{16,24},{25,1},{1,9},{9,17},{17,25},{26,2},{2,... | collective-permute-start | bytes 786440 | tf_op jit(solution)/shard_map/ppermute | solution.py:649
  709.4 26.2 %collective-permute-start.30 = (bf16[32,4096]{1,0:T(8,128)(2,1)S(1)}, bf16[32,4096]{1,0:T(8,128)(2,1)S(1)}, u32[]{:S(2)}, u32[]{:S(2)}) collective-permute-start(bf16[32,4096]{1,0:T(8,128)(2,1)S(1)} %get-tuple-element.104), channel_id=1, source_target_pairs={{16,0},{24,8},{0,16},{8,24},{17,1},{25,9},{1,17},{9,25},{18,2},{26... | collective-permute-start | bytes 786440 | tf_op jit(solution)/shard_map/ppermute | solution.py:649
  712.7 20.6 %collective-permute-start.29 = (bf16[32,4096]{1,0:T(8,128)(2,1)S(1)}, bf16[32,4096]{1,0:T(8,128)(2,1)S(1)}, u32[]{:S(2)}, u32[]{:S(2)}) collective-permute-start(bf16[32,4096]{1,0:T(8,128)(2,1)S(1)} %get-tuple-element.104), channel_id=1, source_target_pairs={{8,0},{16,8},{24,16},{0,24},{9,1},{17,9},{25,17},{1,25},{10,2},{18... | collective-permute-start | bytes 786440 | tf_op jit(solution)/shard_map/ppermute | solution.py:649
  712.7 20.6 %collective-permute-start.37 = (bf16[128,1024]{1,0:T(8,128)(2,1)S(1)}, bf16[128,1024]{1,0:T(8,128)(2,1)S(1)}, u32[]{:S(2)}, u32[]{:S(2)}) collective-permute-start(bf16[128,1024]{1,0:T(8,128)(2,1)S(1)} %get-tuple-element.102), channel_id=1, source_target_pairs={{24,0},{0,8},{8,16},{16,24},{25,1},{1,9},{9,17},{17,25},{26,2},{2,... | collective-permute-start | bytes 786440 | tf_op jit(solution)/shard_map/ppermute | solution.py:649
  746.0 15.1 %collective-permute-start.15 = (bf16[32,3072]{1,0:T(8,128)(2,1)S(1)}, bf16[32,3072]{1,0:T(8,128)(2,1)S(1)}, u32[]{:S(2)}, u32[]{:S(2)}) collective-permute-start(bf16[32,3072]{1,0:T(8,128)(2,1)S(1)} %get-tuple-element.119), channel_id=1, source_target_pairs={{16,0},{24,8},{0,16},{8,24},{17,1},{25,9},{1,17},{9,25},{18,2},{26... | collective-permute-start | bytes 589832 | tf_op jit(solution)/shard_map/ppermute | solution.py:649
  (44 other events, 402.1 us)
Sparse Core Ops, SparseCore 0:
  35.8 44.9 all-gather.4
  82.7 27.8 all-gather.6
  112.5 54.3 all-gather.8
  168.7 60.3 all-gather.10
  366.5 70.2 reduce-scatter.4
  440.5 71.2 reduce-scatter.6
  515.1 41.2 reduce-scatter.8
  653.5 59.9 reduce-scatter.10

commit v4 on v3

--- a/solution.py
+++ b/solution.py
@@ -206,7 +206,7 @@
             jax.ShapeDtypeStruct((ff, width), BF16),
         ],
         compiler_params=params(48),
-        cost_estimate=cost(12 * length * width * ff, 8 * width * ff + 12 * length * width),
+        cost_estimate=cost(length, length),
         name="dense_branch",
     )(mid, dg, up, down)
 
@@ -293,13 +293,15 @@
 def exchange_kernel(
     waves, layers, groups, slots_ref, *refs
 ):
-    g_refs = refs[:layers]
-    mix_ref, up_ref, down_ref, back_ref, slab_ref = refs[layers : layers + 5]
-    po_refs = refs[layers + 5 : 2 * layers + 5]
+    gathered = 2 * layers - 1
+    g_low = [refs[0], *refs[1:layers]]
+    g_high = [refs[0], *refs[layers:gathered]]
+    mix_ref, up_ref, down_ref, back_ref, slab_ref = refs[gathered : gathered + 5]
+    po_refs = refs[gathered + 5 : gathered + layers + 5]
     (
-        du_ref, dd_ref, buf, part, got, act_s, pg_s, eg_s, home, home_slab,
-        a_send, a_recv, z_send, z_recv, r_send, r_recv, b_send, b_recv,
-    ) = refs[2 * layers + 5 :]
+        du_ref, dd_ref, g_refs, buf, part, got, act_s, pg_s, eg_s, home, home_slab,
+        g_sem, a_send, a_recv, z_send, z_recv, r_send, r_recv, b_send, b_recv,
+    ) = refs[gathered + layers + 5 :]
     each = groups // waves
     capacity, width = slots_ref.shape[1:]
     rows = each * capacity
@@ -362,6 +364,14 @@
             return jnp.logical_and(here >= 1, here <= s)
         return jnp.logical_and(here >= last - s, here <= last - 1)
 
+    def g_copy(ref, k):
+        return pltpu.make_async_copy(ref, g_refs.at[k], g_sem.at[k])
+
+    for k in range(layers):
+        pl.when(here + k <= last)(lambda k=k: g_copy(g_high[k], k).start())
+        if k:
+            pl.when(here + k > last)(lambda k=k: g_copy(g_low[layers - k], k).start())
+
     part[...] = jnp.zeros_like(part)
     got[:, :, last - 1] = jnp.zeros_like(got[:, :, last - 1])
     du_ref[...] = jnp.zeros_like(du_ref)
@@ -390,6 +400,8 @@
 
     over(1, groups, lambda j: a_copy(j).start())
     buf[0, 0, 0] = slots_ref[me]
+    for k in range(layers):
+        g_copy(g_high[k], k).wait()
 
     def slab_of(row):
         high = row.astype(BF16).astype(F32)
@@ -399,7 +411,7 @@
     def piece(w, ks):
         mid = jnp.concatenate([buf[w, k].reshape(rows, width) for k in ks], axis=0)
         g = jnp.concatenate(
-            [g_refs[k][source(w * each + i)] for k in ks for i in range(each)], axis=0
+            [g_refs[k, source(w * each + i)] for k in ks for i in range(each)], axis=0
         ).astype(F32)
         logits = dot_nn(mid, mix_ref[...])
         share = 1.0 / (1.0 + jnp.exp(logits[:, 0:1] - logits[:, 1:2]))
@@ -552,7 +564,7 @@
     return 4 if groups % 4 == 0 else 1
 
 
-def expert_exchange(slots, gs, mix_pad, up, down):
+def expert_exchange(slots, g_low, g_high, mix_pad, up, down):
     layers, groups = lax.axis_size("dp"), lax.axis_size("ep")
     waves = exchange_waves(groups)
     each = groups // waves
@@ -565,12 +577,13 @@
     total_rows = layers * groups * capacity
     outs = pl.pallas_call(
         functools.partial(exchange_kernel, waves, layers, groups),
-        in_specs=[vmem] * (4 + layers),
+        in_specs=[vmem] + [pl.BlockSpec(memory_space=pl.ANY)] * (2 * layers - 1) + [vmem] * 3,
         out_specs=[vmem] * (4 + layers),
         out_shape=[block, jax.ShapeDtypeStruct((groups, 16, width), BF16)]
         + [block] * layers
         + [jax.ShapeDtypeStruct((width, hidden), F32), jax.ShapeDtypeStruct((hidden, width), F32)],
         scratch_shapes=[
+            pltpu.VMEM((layers, groups, capacity, width), BF16),
             pltpu.VMEM((waves, layers, each, capacity, width), BF16),
             pltpu.VMEM((waves, layers, rows + 16, width), BF16),
             pltpu.VMEM((waves, 2, layers - 1, rows + 16, width), BF16),
@@ -579,6 +592,7 @@
             pltpu.VMEM((layers * rows, width), BF16),
             pltpu.VMEM((groups, capacity, width), BF16),
             pltpu.VMEM((groups, 16, width), BF16),
+            sem((layers,)),
             sem((groups,)),
             sem((groups,)),
             sem((waves, 2, layers - 1)),
@@ -593,8 +607,251 @@
         ),
         cost_estimate=cost(12 * total_rows * width * hidden, 20 * total_rows * width),
         name="expert_exchange",
-    )(slots, *gs, mix_pad, up, down)
+    )(slots, *g_low, *g_high[1:], mix_pad, up, down)
     return outs[0], outs[1], outs[2 : 2 + layers], outs[2 + layers], outs[3 + layers]
+
+
+def sums_kernel(plan, layers, groups, small_ref, *refs):
+    count = len(plan)
+    mats, outs = refs[:count], refs[count : 2 * count]
+    (
+        small_out, own, sib, got, held, inner, final, wide, small_two, small_chip, small_layer,
+        own_sem, s_send, s_recv, x_send, x_recv, z_send, z_recv, t_send, t_recv, o_sem,
+    ) = refs[2 * count :]
+    chips = groups // 2
+    width = held.shape[-1]
+    total = held.shape[0]
+    last = layers - 1
+    here, me = lax.axis_index("dp"), lax.axis_index("ep")
+    core, chip = lax.rem(me, 2), me // 2
+    sibling = me + 1 - 2 * core
+    mesh_id = pl.DeviceIdType.MESH
+    chip_at = lambda j: lax.rem(chip + j, chips)
+    pieces = [(m, i) for m in range(count) for i in range(plan[m])]
+    at_end = jnp.logical_or(here == 0, here == last)
+    inside = jnp.logical_and(here > 0, here < last)
+    inward = 1 + (here // last) * (last - 2)
+    outward = lax.rem((here - 1) * last + layers * last, layers)
+    across = last - here
+
+    def source(m, i, half):
+        if len(mats[m].shape) == 5:
+            return mats[m].at[:, half, i]
+        return mats[m].at[:, half, :, pl.ds(i * width, width)]
+
+    def remote(src, dst, send, recv, where):
+        return pltpu.make_async_remote_copy(
+            src, dst, send, recv, device_id=where, device_id_type=mesh_id
+        )
+
+    def s_copy(c):
+        return remote(source(*pieces[c], 1 - core), sib.at[c], s_send.at[c], s_recv.at[c], {"ep": sibling})
+
+    def x_copy(c, j):
+        return remote(
+            own.at[c, chip_at(j)], got.at[c, j - 1], x_send.at[c, j - 1], x_recv.at[c, j - 1],
+            {"ep": 2 * chip_at(j) + core},
+        )
+
+    def z_copy(c, n):
+        src = (held, held, inner)[n]
+        dst = (inner, final, final)[n]
+        where = (inward, across, outward)[n]
+        return remote(src.at[c], dst.at[c], z_send.at[c, n], z_recv.at[c, n], {"dp": where})
+
+    def t_copy(n, j):
+        if n == 0:
+            return remote(small_ref, small_two, t_send.at[0, 0], t_recv.at[0, 0], {"ep": sibling})
+        if n == 1:
+            spot = small_chip.at[chip]
+            return remote(spot, spot, t_send.at[1, j], t_recv.at[1, j], {"ep": 2 * chip_at(j) + core})
+        spot = small_layer.at[here]
+        return remote(
+            spot, spot, t_send.at[2, j], t_recv.at[2, j], {"dp": lax.rem(here + j, layers)}
+        )
+
+    for c in range(total):
+        pltpu.make_async_copy(source(*pieces[c], core), own.at[c], own_sem.at[c]).start()
+
+    barrier = pltpu.get_barrier_semaphore()
+    pl.semaphore_signal(barrier, inc=1, device_id={"ep": sibling}, device_id_type=mesh_id)
+
+    def over(first, end, act):
+        def step(j, carry):
+            act(j)
+            return carry
+
+        lax.fori_loop(first, end, step, 0)
+
+    over(
+        1,
+        chips,
+        lambda j: pl.semaphore_signal(
+            barrier, inc=1, device_id={"ep": 2 * chip_at(j) + core}, device_id_type=mesh_id
+        ),
+    )
+    over(
+        1,
+        layers,
+        lambda j: pl.semaphore_signal(
+            barrier, inc=1, device_id={"dp": lax.rem(here + j, layers)}, device_id_type=mesh_id
+        ),
+    )
+    pl.semaphore_wait(barrier, chips + last)
+
+    t_copy(0, 0).start()
+    for c in range(total):
+        s_copy(c).start()
+
+    def body(t, carry):
+        @pl.when(t < total)
+        def _():
+            pltpu.make_async_copy(sib.at[t], own.at[t], own_sem.at[t]).wait()
+            remote(own.at[t], sib.at[t], s_send.at[t], s_recv.at[t], {"ep": sibling}).wait_recv()
+
+            def add(p):
+                own[t, p] = own[t, p] + sib[t, p]
+
+            over(0, chips, add)
+            over(1, chips, lambda j: x_copy(t, j).start())
+
+        @pl.when(jnp.logical_and(t >= 1, t <= total))
+        def _():
+            c = t - 1
+            over(1, chips, lambda j: x_copy(c, j).wait_recv())
+            wide[c] = own[c, chip].astype(F32)
+
+            def add(j):
+                wide[c] += got[c, j - 1].astype(F32)
+
+            over(1, chips, add)
+            held[c] = wide[c].astype(BF16)
+            pl.when(at_end)(lambda: z_copy(c, 0).start())
+
+        @pl.when(jnp.logical_and(inside, jnp.logical_and(t >= 2, t <= total + 1)))
+        def _():
+            c = t - 2
+            z_copy(c, 0).wait_recv()
+            held[c] = held[c] + inner[c]
+            z_copy(c, 1).start()
+
+        @pl.when(jnp.logical_and(inside, jnp.logical_and(t >= 3, t <= total + 2)))
+        def _():
+            c = t - 3
+            z_copy(c, 1).wait_recv()
+            both = held[c] + final[c]
+            inner[c] = both
+            wide[c] = both.astype(F32)
+            z_copy(c, 2).start()
+
+        @pl.when(jnp.logical_and(at_end, t >= 4))
+        def _():
+            c = t - 4
+            z_copy(c, 2).wait_recv()
+            wide[c] = final[c].astype(F32)
+
+        @pl.when(t == 1)
+        def _():
+            t_copy(0, 0).wait_recv()
+            small_chip[chip] = small_ref[...] + small_two[...]
+            over(1, chips, lambda j: t_copy(1, j).start())
+
+        @pl.when(t == 3)
+        def _():
+            over(1, chips, lambda j: t_copy(1, j).wait_recv())
+            acc = small_chip[0]
+            for n in range(1, chips):
+                acc = acc + small_chip[n]
+            small_layer[here] = acc
+            over(1, layers, lambda j: t_copy(2, j).start())
+
+        return carry
+
+    lax.fori_loop(0, total + 4, body, 0)
+
+    copies = []
+    for c, (m, i) in enumerate(pieces):
+        spot = outs[m].at[i] if len(outs[m].shape) == 3 else outs[m].at[:, pl.ds(i * width, width)]
+        copies.append(pltpu.make_async_copy(wide.at[c], spot, o_sem.at[c]))
+        copies[-1].start()
+
+    over(1, layers, lambda j: t_copy(2, j).wait_recv())
+    acc = small_layer[0]
+    for n in range(1, layers):
+        acc = acc + small_layer[n]
+    small_out[...] = acc
+
+    t_copy(0, 0).wait_send()
+    over(1, chips, lambda j: t_copy(1, j).wait_send())
+    over(1, layers, lambda j: t_copy(2, j).wait_send())
+
+    def sent(c):
+        remote(own.at[c], sib.at[c], s_send.at[c], s_recv.at[c], {"ep": sibling}).wait_send()
+        over(1, chips, lambda j: x_copy(c, j).wait_send())
+        pl.when(at_end)(lambda: z_copy(c, 0).wait_send())
+
+        @pl.when(inside)
+        def _():
+            z_copy(c, 1).wait_send()
+            z_copy(c, 2).wait_send()
+
+    over(0, total, sent)
+    for copy in copies:
+        copy.wait()
+
+
+def gradient_sums(small, columns, rows_split):
+    layers, groups = lax.axis_size("dp"), lax.axis_size("ep")
+    chips = groups // 2
+    width = small.shape[1]
+    plan = [a.shape[1] // width for a in columns] + [a.shape[0] // width for a in rows_split]
+    high = columns[0].shape[0] // groups
+    total = sum(plan)
+    views = [a.reshape(chips, 2, high, a.shape[1]) for a in columns] + [
+        a.reshape(chips, 2, n, high, width) for a, n in zip(rows_split, plan[len(columns) :])
+    ]
+    shapes = [jax.ShapeDtypeStruct((high, a.shape[1]), F32) for a in columns] + [
+        jax.ShapeDtypeStruct((n, high, width), F32) for n in plan[len(columns) :]
+    ]
+    sem = pltpu.SemaphoreType.DMA
+    vmem = pl.BlockSpec(memory_space=pltpu.VMEM)
+    anywhere = pl.BlockSpec(memory_space=pl.ANY)
+    buffers = lambda *lead: pltpu.VMEM((total, *lead, high, width), BF16)
+    outs = pl.pallas_call(
+        functools.partial(sums_kernel, plan, layers, groups),
+        in_specs=[vmem] + [anywhere] * len(views),
+        out_specs=[anywhere] * len(views) + [vmem],
+        out_shape=shapes + [jax.ShapeDtypeStruct(small.shape, F32)],
+        scratch_shapes=[
+            buffers(chips),
+            buffers(chips),
+            buffers(chips - 1),
+            buffers(),
+            buffers(),
+            buffers(),
+            pltpu.VMEM((total, high, width), F32),
+            pltpu.VMEM(small.shape, F32),
+            pltpu.VMEM((chips, *small.shape), F32),
+            pltpu.VMEM((layers, *small.shape), F32),
+            sem((total,)),
+            sem((total,)),
+            sem((total,)),
+            sem((total, chips - 1)),
+            sem((total, chips - 1)),
+            sem((total, 3)),
+            sem((total, 3)),
+            sem((3, max(chips, layers))),
+            sem((3, max(chips, layers))),
+            sem((total,)),
+        ],
+        compiler_params=pltpu.CompilerParams(
+            collective_id=1, has_side_effects=True, vmem_limit_bytes=62 << 20
+        ),
+        cost_estimate=cost(10 * total * chips * high * width, 8 * total * chips * high * width),
+        name="gradient_sums",
+    )(small, *views)
+    rows_out = [a.reshape(-1, width) for a in outs[len(columns) : -1]]
+    return (*outs[: len(columns)], *rows_out, outs[-1])
 
 
 def normalise(values_in):
@@ -741,6 +998,7 @@
         return held[2:]
 
     step(g_low, g_high)
+    (normed_in,) = step(g_low, g_high, normed_in)
     qkv_rows = dot_nn(normed_in, qkv_full).astype(BF16)
     (qkv_rows,) = step(g_low, g_high, qkv_rows)
     attended, lse = attention_forward(qkv_rows, bucket)
@@ -749,8 +1007,6 @@
     mid_low = (unit2 * ln2_gain).astype(BF16)
     mid_slots = pick(mid_low)
     (mid_slots,) = step(g_low, g_high, mid_slots)
-    step(g_low, g_high)
-    gs = [g_own] + join(g_low, g_high)
 
     grad_out = cotangent.astype(F32)
     logits = dot_nn(mid_low, mix_weight)
@@ -767,9 +1023,9 @@
         return acc
 
     if capacity % 16 == 0:
-        blocks = [g.reshape(groups, capacity, width) for g in gs]
+        blocks = lambda many: [g.reshape(groups, capacity, width) for g in many]
         returned, slab, partial_outs, expert_up_grad, expert_down_grad = expert_exchange(
-            mid_slots, blocks, mix_pad, expert_up2, expert_down2
+            mid_slots, blocks(g_low), blocks(g_high), mix_pad, expert_up2, expert_down2
         )
         each = groups // exchange_waves(groups)
         offset = lax.rem(
@@ -783,6 +1039,7 @@
         dense_grad, returned = lax.optimization_barrier((dense_grad, returned))
         outs = [a.reshape(slots, width) for a in partial_outs]
     else:
+        gs = [g_own] + join(g_low, g_high)
         mid_own = exchange_out(mid_slots).reshape(slots, width)
         mids = [mid_own] + [shifted(mid_own, k) for k in range(1, layers)]
         chunks = [expert_chunk(mids[k], gs[k], mix_pad, expert_up2, expert_down2) for k in range(layers)]
@@ -802,10 +1059,19 @@
             mids, [c[3] for c in chunks], [c[2] for c in chunks], [c[4] for c in chunks]
         )
 
+    last = layers - 1
+    out_up, out_down = send_hop(outs[last], 1, 1), send_hop(outs[1], -1, 1)
     dense_out, mid_grad_dense, up_grad, down_grad = dense_branch(mid_low, dense_grad, up_full, down_full)
-    up_shard = scatter(up_grad)
-    down_shard = scatter(after(down_grad, up_shard))
-    outs = [back(k, outs[k]) for k in range(layers)]
+
+    def out_step(stage, *others):
+        held = lax.optimization_barrier((out_up, out_down, *others))
+        return (
+            send_hop(held[0] + outs[layers - stage], 1, stage),
+            send_hop(held[1] + outs[stage], -1, stage),
+            *held[2:],
+        )
+
+    out_up, out_down, dense_out = out_step(2, dense_out)
     in_rows = returned.reshape(slots, width)
     mix_dot1 = jnp.sum(table.astype(F32) * dot_back, axis=1, keepdims=True)
     mix_dot0 = jnp.sum(grad_out * dense_out, axis=-1, keepdims=True)
@@ -820,29 +1086,33 @@
     attn_out_grad = res_grad.astype(BF16)
     out_weight_grad = dot_tn(attended, attn_out_grad)
     attended_grad = dot_nt(attn_out_grad, out_full).astype(BF16)
+    for stage in range(3, layers):
+        out_up, out_down, attended_grad = out_step(stage, attended_grad)
     qkv_grad = attention_backward(qkv_rows, bucket, attended_grad, lse)
-    out_shard = scatter(after(out_weight_grad, down_shard))
-    qkv_grad, up_shard, outs[1] = lax.optimization_barrier((qkv_grad, up_shard, outs[1]))
+    out_up, out_down, qkv_grad = lax.optimization_barrier((out_up, out_down, qkv_grad))
     qkv_weight_grad = dot_tn(normed_in, qkv_grad)
     normed_grad = dot_nt(qkv_grad, qkv_full)
     ln1_gain_grad = jnp.sum(normed_grad * unit1, axis=0)
     tokens_grad = res_grad + norm_backward(normed_grad, ln1_gain, unit1, inverse1)
 
-    up_shard, down_shard, out_shard, *outs = after(
-        (up_shard, down_shard, out_shard, *outs), normed_grad
-    )
-    out_sum = total(outs).astype(BF16).reshape(groups, capacity, width)
+    out_sum = total([outs[0], out_up, out_down]).astype(BF16).reshape(groups, capacity, width)
     out_back = lax.all_to_all(out_sum, "ep", split_axis=0, concat_axis=0, tiled=True)
     expert_out = dot_nn(table, out_back.reshape(slots, width))
     result = (hidden_res + mix0 * dense_out + mix1 * expert_out).astype(BF16)
 
-    up_final = sum_layers(up_shard)
-    down_final = sum_layers(down_shard)
-    out_final = sum_layers(out_shard)
-    qkv_final = sum_layers(scatter(after(qkv_weight_grad, out_shard)))
-    small_sums = sum_everywhere(
-        jnp.concatenate([ln1_gain_grad[None], ln2_gain_grad[None], mix_weight_grad.T], axis=0)
-    )
+    ln1_gain_grad, result = lax.optimization_barrier((ln1_gain_grad, result))
+    small = jnp.concatenate([ln1_gain_grad[None], ln2_gain_grad[None], mix_weight_grad.T], axis=0)
+    small = jnp.pad(small, ((0, 4), (0, 0)))
+    if layers == 4 and length // groups >= 16:
+        qkv_final, out_final, up_final, down_final, small_sums = gradient_sums(
+            small,
+            [a.astype(BF16) for a in (qkv_weight_grad, out_weight_grad, up_grad)],
+            [down_grad],
+        )
+    else:
+        sums = [sum_layers(scatter(a)) for a in (qkv_weight_grad, out_weight_grad, up_grad, down_grad)]
+        qkv_final, out_final, up_final, down_final = sums
+        small_sums = sum_everywhere(small)
     return (
         result,
         tokens_grad,
@@ -852,7 +1122,7 @@
         small_sums[1],
         up_final,
         down_final,
-        small_sums[2:].T,
+        small_sums[2:4].T,
         expert_up_grad[None],
         expert_down_grad[None],
     )

time: 811 us -> 650 us (0.80)
  waiting for transfers between devices: 352 us -> 85.8 us
  Pallas kernels: 233 us -> 417 us
  starting transfers between devices: 87.1 us -> 42.8 us
  other arithmetic: 39.3 us -> 16.6 us
    pallas_call x0 -> x1, Pallas kernels: none -> 172 us  [gradient_sums(): pl.pallas_call(functools.partial(sums_kernel, plan, layers, groups), in_s...]
    ppermute x32 -> x6, waiting for transfers between devices: 154 us -> 15.1 us  [send_hop(): return lax.ppermute(rows, 'dp', pairs)]
    reduce_scatter x4 -> x0, waiting for transfers between devices: 108 us -> none  [on_device(): lax.psum_scatter(a.astype(BF16), 'ep', scatter_dimension=0, tiled=True)]
    ppermute x32 -> x6, starting transfers between devices: 65.6 us -> 20.1 us  [send_hop(): return lax.ppermute(rows, 'dp', pairs)]
    all_gather x4, waiting for transfers between devices: 38 us -> 4.41 us  [on_device(): gather = lambda w: lax.all_gather(w, 'ep', axis=0, tiled=True)]
    ppermute x6, waiting for transfers between devices: 32.2 us -> 45.4 us  [hop(): return lax.ppermute(rows, 'dp', pairs)]
    pallas_call x1, Pallas kernels: 162 us -> 174 us  [expert_exchange(): pl.pallas_call(functools.partial(exchange_kernel, waves, layers, groups),...]
    convert_element_type x5 -> x1, other arithmetic: 10.9 us -> 2.05 us  [on_device(): total([outs[0], out_up, out_down]).astype(BF16)]
  transfers between devices with their start and end apart: 48 -> 18, of which waited for: 22 -> 8; matrix products, arithmetic and copies ran while one was open for 11% -> 6% of each run, Pallas kernels for 24% -> 38%
where the time goes in v4:
time: 650 us; the launch traced here: 641 us
  Pallas kernels  417 us (64%)
  waiting for transfers between devices  85.8 us (13%)
  starting transfers between devices  42.8 us (7%)
  matrix products  39.6 us (6%)
  local copies, waits for them, and re-layouts  24.4 us (4%)
  other arithmetic  16.6 us (3%)
  between operations  15.4 us (2%)
    pallas_call x1, Pallas kernels, expert_exchange(): pl.pallas_call(functools.partial(exchange_kernel, waves, layers, groups),...  174 us
    pallas_call x1, Pallas kernels, gradient_sums(): pl.pallas_call(functools.partial(sums_kernel, plan, layers, groups), in_s...  172 us
    ppermute x6, waiting for transfers between devices, hop(): return lax.ppermute(rows, 'dp', pairs)  45.4 us
    pallas_call x1, Pallas kernels, dense_branch(): pl.pallas_call(dense_kernel, grid=(ff // tile,), in_specs=[whole, whole,...  36.2 us
    unnamed x75, local copies, waits for them, and re-layouts  20.7 us
    ppermute x6, starting transfers between devices, send_hop(): return lax.ppermute(rows, 'dp', pairs)  20.1 us
    pallas_call x1, Pallas kernels, attention_backward(): pl.pallas_call(functools.partial(attn_bwd_kernel, tile), grid=(pairs,), i...  18.8 us
    dot_general x6, matrix products, dot_nn(): lax.dot_general(a, b, (((1,), (0,)), ((), ())), preferred_element_type=F32)  17 us
  transfers between devices with their start and end apart: 18, of which 8 were waited for; matrix products, arithmetic and copies ran while one was open for 6% of the time, Pallas kernels for 38%

profile of v4, /device:TPU:0, one launch (start us, length us, event | category | flops | bytes accessed | tf_op | source)
XLA Modules:
  0.0 641.2 jit_solution(5566725341918384314)
XLA Ops:
  8.9 3.2 convolution_convert_fusion.4
  12.1 5.3 all-to-all-start
  19.5 16.2 %all-to-all-done = bf16[8,80,1024]{2,1,0:T(8,128)(2,1)S(1)} async-done(((bf16[8,80,1024]{2,1,0:T(8,128)(2,1)}), bf16[8,80,1024]{2,1,0:T(8,128)(2,1)S(1)}, u32[]{:S(2)}, u32[]{:S(2)}) %all-to-all-start) | async-done | bytes 1310752 | tf_op jit(solution)/shard_map/all_to_all | solution.py:960
  37.8 4.6 collective-permute-start
  43.6 22.9 %collective-permute-done = bf16[640,1024]{1,0:T(8,128)(2,1)} collective-permute-done((bf16[640,1024]{1,0:T(8,128)(2,1)S(1)}, bf16[640,1024]{1,0:T(8,128)(2,1)}, u32[]{:S(2)}, u32[]{:S(2)}) %collective-permute-start) | collective-permute-done | bytes 1310752 | tf_op jit(solution)/shard_map/ppermute | solution.py:878
  66.5 5.3 collective-permute-done.1
  76.4 4.4 all-gather.5.cloned.1.call-done
  80.8 6.5 %convolution_convert_fusion.1.q_ref.k_ref.v_ref = bf16[512,3072]{1,0:T(8,128)(2,1)S(1)} fusion(bf16[512,1024]{1,0:T(8,128)(2,1)} %fusion.8, bf16[1024,3072]{1,0:T(8,128)(2,1)} %all-gather.5.cloned.1.call-done), kind=kOutput, calls=%fused_computation.1 | convolution fusion | flops 3222798336 | bytes 10485760 | tf_op jit(solution)/shard_map/dot_general | solution.py:21
  87.4 16.2 %collective-permute-done.3 = bf16[640,1024]{1,0:T(8,128)(2,1)} collective-permute-done((bf16[640,1024]{1,0:T(8,128)(2,1)}, bf16[640,1024]{1,0:T(8,128)(2,1)}, u32[]{:S(2)}, u32[]{:S(2)}) %collective-permute-start.3) | collective-permute-done | bytes 1310752 | tf_op jit(solution)/shard_map/ppermute | solution.py:878
  106.6 15.8 %attn_fwd.1 = (bf16[512,1024]{1,0:T(8,128)(2,1)S(1)}, f32[512,1024]{1,0:T(8,128)S(1)}) custom-call(s32[1]{0:T(128)S(6)} %copy.32.flag_ref, bf16[512,3072]{1,0:T(8,128)(2,1)S(1)} %convolution_convert_fusion.1.q_ref.k_ref.v_ref, bf16[512,3072]{1,0:T(8,128)(2,1)S(1)} %convolution_convert_fusion.1.q_ref.k_ref.v_ref, ...), custom_call_target="tpu_custom_call" | custom-call | flops 2147483648 | bytes 5242880 | tf_op jit(solution)/shard_map/attn_fwd/pallas_call | solution.py:85
  125.4 3.3 fusion.31
  130.0 2.0 convolution_convert_fusion.3
  133.1 174.1 %expert_exchange.1 = (bf16[8,80,1024]{2,1,0:T(8,128)(2,1)}, bf16[8,16,1024]{2,1,0:T(8,128)(2,1)}, bf16[8,80,1024]{2,1,0:T(8,128)(2,1)}, bf16[8,80,1024]{2,1,0:T(...) custom-call(bf16[8,80,1024]{2,1,0:T(8,128)(2,1)} %bitcast.97, ...), custom_call_target="tpu_custom_call" | custom-call | flops 32212254720 | bytes 52428800 | tf_op jit(solution)/shard_map/expert_exchange/pallas_call | solution.py:578
  307.1 5.4 collective-permute-start.6
  317.9 36.2 %dense_branch.1 = (f32[512,1024]{1,0:T(8,128)S(1)}, f32[512,1024]{1,0:T(8,128)}, bf16[1024,4096]{1,0:T(8,128)(2,1)}, bf16[4096,1024]{1,0:T(8,128)(2,1)}) custom-call(bf16[512,1024]{1,0:T(8,128)(2,1)S(1)} %multiply_convert_fusion.mid_ref, bf16[512,1024]{1,0:T(8,128)(2,1)S(1)} %fusion.15.dg_ref, bf16[1024,4096]{1,0:T(8,128)(2,1)} %all-gather.9.cloned.1.call-done.up_ref, ...), custom_call_target="tpu_custom_call" | custom-call | flops 512 | bytes 512 | tf_op jit(solution)/shard_map/dense_branch/pallas_call | solution.py:197
  354.2 2.3 fusion.16
  356.5 2.1 bitcast_add_fusion
  366.1 15.1 %collective-permute-done.8 = bf16[640,1024]{1,0:T(8,128)(2,1)S(1)} collective-permute-done((bf16[640,1024]{1,0:T(8,128)(2,1)S(1)}, bf16[640,1024]{1,0:T(8,128)(2,1)S(1)}, u32[]{:S(2)}, u32[]{:S(2)}) %collective-permute-start.8) | collective-permute-done | bytes 1310752 | tf_op jit(solution)/shard_map/ppermute | solution.py:891
  383.2 9.2 %collective-permute-start.10 = (bf16[640,1024]{1,0:T(8,128)(2,1)S(1)}, bf16[640,1024]{1,0:T(8,128)(2,1)S(1)}, u32[]{:S(2)}, u32[]{:S(2)}) collective-permute-start(bf16[640,1024]{1,0:T(8,128)(2,1)S(1)} %bitcast_add_fusion.2), channel_id=1, source_target_pairs={{0,8},{8,16},{16,24},{1,9},{9,17},{17,25},{2,10},{10,18},{18,26},{... | collective-permute-start | bytes 3932168 | tf_op jit(solution)/shard_map/ppermute | solution.py:891
  392.7 2.7 convolution_convert_fusion.2
  395.8 18.8 %attn_bwd.1 = bf16[512,3072]{1,0:T(8,128)(2,1)S(1)} custom-call(s32[1]{0:T(128)S(6)} %copy.32.flag_ref, bf16[512,3072]{1,0:T(8,128)(2,1)S(1)} %copy-done.1, bf16[512,3072]{1,0:T(8,128)(2,1)S(1)} %copy-done.1, bf16[512,3072]{1,0:T(8,128)(2,1)S(1)} %copy-done.1, bf16[512,1024]{1,0:T(8,128)(2,1)S(1)} %convolution_convert_fusion.5.g_ref, f32[512,1024]{1,0:T(8,128)S(1)} %copy-done.5), custom_call_target="tpu_custom_call" | custom-call | flops 5368709120 | bytes 10485760 | tf_op jit(solution)/shard_map/attn_bwd/pallas_call | solution.py:148
  414.6 2.1 fusion.1
  416.6 5.3 all-to-all-start.1
  422.0 7.1 %fusion.10 = (f32[512]{0:T(512)S(1)}, f32[1024]{0:T(1024)S(1)}, f32[512]{0:T(512)S(1)}, f32[512,1024]{1,0:T(8,128)S(1)}) fusion(bf16[512,1024]{1,0:T(8,128)(2,1)} %param.13, f32[1024]{0:T(1024)S(1)} %copy-done.32, f32[512]{0:T(512)S(1)} %add_rsqrt_fusion.1, f32[512]{0:T(512)S(1)} %broadcast_multiply_fusion.5, bf16[512,3072]{1,0:T(8,128)(2,1)S(1)} %attn_bwd.1, ...), kind=kOutput, calls=%fused_computation.19 | convolution fusion | flops 3225942016 | bytes 12599296 | tf_op jit(solution)/shard_map/dot_general | solution.py:25
  429.1 2.0 fusion.13
  432.0 5.5 convolution_convert_fusion
  437.5 2.8 all-to-all-done.1
  440.3 4.0 add_convert_fusion
  444.9 171.8 %gradient_sums.1 = (f32[128,3072]{1,0:T(8,128)}, f32[128,1024]{1,0:T(8,128)}, f32[128,4096]{1,0:T(8,128)}, f32[4,128,1024]{2,1,0:T(8,128)}, f32[8,1024]{1,0:T(8,128)}) custom-call(f32[8,1024]{1,0:T(8,128)} %select_maximum_fusion.small_ref, bf16[4,2,128,3072]{3,2,1,0:T(8,128)(2,1)} %bitcast.65, bf16[4,2,128,1024]{3,2,1,0:T(8,128)(2,1)} %bitcast.69, ...), custom_call_target="tpu_custom_call" | custom-call | flops 62914560 | bytes 50331648 | tf_op jit(solution)/shard_map/gradient_sums/pallas_call | solution.py:820
  619.6 2.9 copy.33
  628.5 2.1 copy.37
  632.2 2.0 copy.38
  (138 shorter events, 46.7 us)
Async XLA Ops:
  12.1 5.4 copy-start.12
  12.1 6.0 copy-start.32
  12.1 23.5 %all-to-all-start = ((bf16[8,80,1024]{2,1,0:T(8,128)(2,1)}), bf16[8,80,1024]{2,1,0:T(8,128)(2,1)S(1)}, u32[]{:S(2)}, u32[]{:S(2)}) async-start(bf16[8,80,1024]{2,1,0:T(8,128)(2,1)} %bitcast.73), calls=%async_computation | async-start | bytes 2621440 | tf_op jit(solution)/shard_map/all_to_all | solution.py:960
  17.4 63.3 %all-gather.5.cloned.1.call-start = ((), (), s32[]{:S(2)}) async-start(), calls=%async_computation.2 | async-start | bytes 7077888 | tf_op jit(solution)/shard_map/all_gather | solution.py:959
  19.5 55.9 %copy-start.30 = (bf16[1024,2]{0,1:T(2,128)(2,1)S(1)}, bf16[1024,2]{0,1:T(2,128)(2,1)}, u32[]{:S(2)}) copy-start(bf16[1024,2]{0,1:T(2,128)(2,1)} %param.22) | copy-start | bytes 12292
  35.7 51.7 %copy-start.23 = (bf16[8,80,1024]{2,1,0:T(8,128)(2,1)}, bf16[8,80,1024]{2,1,0:T(8,128)(2,1)S(1)}, u32[]{:S(2)}) copy-start(bf16[8,80,1024]{2,1,0:T(8,128)(2,1)S(1)} %all-to-all-done) | copy-start | bytes 3932164
  35.7 89.7 %all-gather.7.cloned.1.call-start = ((), (), s32[]{:S(2)}) async-start(), calls=%async_computation.3 | async-start | bytes 2359296 | tf_op jit(solution)/shard_map/all_gather | solution.py:959
  36.4 281.4 %all-gather.11.cloned.1.call-start = ((), (), s32[]{:S(2)}) async-start(), calls=%async_computation.5 | async-start | bytes 9437184 | tf_op jit(solution)/shard_map/all_gather | solution.py:959
  37.2 280.7 %all-gather.9.cloned.1.call-start = ((), (), s32[]{:S(2)}) async-start(), calls=%async_computation.4 | async-start | bytes 9437184 | tf_op jit(solution)/shard_map/all_gather | solution.py:959
  37.8 28.7 %collective-permute-start = (bf16[640,1024]{1,0:T(8,128)(2,1)S(1)}, bf16[640,1024]{1,0:T(8,128)(2,1)}, u32[]{:S(2)}, u32[]{:S(2)}) collective-permute-start(bf16[640,1024]{1,0:T(8,128)(2,1)S(1)} %bitcast.71), channel_id=1, source_target_pairs={{0,8},{8,16},{16,24},{1,9},{9,17},{17,25},{2,10},{10,18},{18,26},{... | collective-permute-start | bytes 3932168 | tf_op jit(solution)/shard_map/ppermute | solution.py:878
  42.3 29.4 %collective-permute-start.1 = (bf16[640,1024]{1,0:T(8,128)(2,1)S(1)}, bf16[640,1024]{1,0:T(8,128)(2,1)}, u32[]{:S(2)}, u32[]{:S(2)}) collective-permute-start(bf16[640,1024]{1,0:T(8,128)(2,1)S(1)} %bitcast.72), channel_id=1, source_target_pairs={{8,0},{16,8},{24,16},{9,1},{17,9},{25,17},{10,2},{18,10},{26,18},{... | collective-permute-start | bytes 3932168 | tf_op jit(solution)/shard_map/ppermute | solution.py:878
  71.8 15.6 %collective-permute-start.2 = (bf16[640,1024]{1,0:T(8,128)(2,1)}, bf16[640,1024]{1,0:T(8,128)(2,1)}, u32[]{:S(2)}, u32[]{:S(2)}) collective-permute-start(bf16[640,1024]{1,0:T(8,128)(2,1)} %collective-permute-done), channel_id=1, source_target_pairs={{8,16},{16,24},{9,17},{17,25},{10,18},{18,26},{11,19},{19,27},{12,... | collective-permute-start | bytes 3932168 | tf_op jit(solution)/shard_map/ppermute | solution.py:878
  73.5 30.1 %collective-permute-start.3 = (bf16[640,1024]{1,0:T(8,128)(2,1)}, bf16[640,1024]{1,0:T(8,128)(2,1)}, u32[]{:S(2)}, u32[]{:S(2)}) collective-permute-start(bf16[640,1024]{1,0:T(8,128)(2,1)} %collective-permute-done.1), channel_id=1, source_target_pairs={{8,0},{16,8},{9,1},{17,9},{10,2},{18,10},{11,3},{19,11},{12,4},{20... | collective-permute-start | bytes 3932168 | tf_op jit(solution)/shard_map/ppermute | solution.py:878
  103.5 28.5 %collective-permute-start.4 = (bf16[640,1024]{1,0:T(8,128)(2,1)}, bf16[640,1024]{1,0:T(8,128)(2,1)}, u32[]{:S(2)}, u32[]{:S(2)}) collective-permute-start(bf16[640,1024]{1,0:T(8,128)(2,1)} %collective-permute-done.2), channel_id=1, source_target_pairs={{16,24},{17,25},{18,26},{19,27},{20,28},{21,29},{22,30},{23,31}} | collective-permute-start | bytes 3932168 | tf_op jit(solution)/shard_map/ppermute | solution.py:878
  105.3 27.8 %collective-permute-start.5 = (bf16[640,1024]{1,0:T(8,128)(2,1)}, bf16[640,1024]{1,0:T(8,128)(2,1)}, u32[]{:S(2)}, u32[]{:S(2)}) collective-permute-start(bf16[640,1024]{1,0:T(8,128)(2,1)} %collective-permute-done.3), channel_id=1, source_target_pairs={{8,0},{9,1},{10,2},{11,3},{12,4},{13,5},{14,6},{15,7}} | collective-permute-start | bytes 3932168 | tf_op jit(solution)/shard_map/ppermute | solution.py:878
  307.1 47.0 %collective-permute-start.6 = (bf16[640,1024]{1,0:T(8,128)(2,1)}, bf16[640,1024]{1,0:T(8,128)(2,1)}, u32[]{:S(2)}, u32[]{:S(2)}) collective-permute-start(bf16[640,1024]{1,0:T(8,128)(2,1)} %bitcast.75), channel_id=1, source_target_pairs={{0,8},{1,9},{2,10},{3,11},{4,12},{5,13},{6,14},{7,15}} | collective-permute-start | bytes 3932168 | tf_op jit(solution)/shard_map/ppermute | solution.py:891
  312.5 41.6 %collective-permute-start.7 = (bf16[640,1024]{1,0:T(8,128)(2,1)}, bf16[640,1024]{1,0:T(8,128)(2,1)}, u32[]{:S(2)}, u32[]{:S(2)}) collective-permute-start(bf16[640,1024]{1,0:T(8,128)(2,1)} %bitcast.74), channel_id=1, source_target_pairs={{24,16},{25,17},{26,18},{27,19},{28,20},{29,21},{30,22},{31,23}} | collective-permute-start | bytes 3932168 | tf_op jit(solution)/shard_map/ppermute | solution.py:891
  358.6 22.6 %collective-permute-start.8 = (bf16[640,1024]{1,0:T(8,128)(2,1)S(1)}, bf16[640,1024]{1,0:T(8,128)(2,1)S(1)}, u32[]{:S(2)}, u32[]{:S(2)}) collective-permute-start(bf16[640,1024]{1,0:T(8,128)(2,1)S(1)} %get-tuple-element.112), channel_id=1, source_target_pairs={{0,8},{8,16},{1,9},{9,17},{2,10},{10,18},{3,11},{11,19},{4,12},{12... | collective-permute-start | bytes 3932168 | tf_op jit(solution)/shard_map/ppermute | solution.py:891
  360.2 21.1 %collective-permute-start.9 = (bf16[640,1024]{1,0:T(8,128)(2,1)S(1)}, bf16[640,1024]{1,0:T(8,128)(2,1)S(1)}, u32[]{:S(2)}, u32[]{:S(2)}) collective-permute-start(bf16[640,1024]{1,0:T(8,128)(2,1)S(1)} %get-tuple-element.111), channel_id=1, source_target_pairs={{16,8},{24,16},{17,9},{25,17},{18,10},{26,18},{19,11},{27,19},{20,... | collective-permute-start | bytes 3932168 | tf_op jit(solution)/shard_map/ppermute | solution.py:891
  364.8 27.8 %copy-start.15 = (f32[512,1024]{1,0:T(8,128)}, f32[512,1024]{1,0:T(8,128)S(1)}, u32[]{:S(2)}) copy-start(f32[512,1024]{1,0:T(8,128)S(1)} %convert_add_fusion) | copy-start | bytes 6291460
  364.8 16.5 %copy-start.25 = (bf16[8,80,1024]{2,1,0:T(8,128)(2,1)S(1)}, bf16[8,80,1024]{2,1,0:T(8,128)(2,1)}, u32[]{:S(2)}) copy-start(bf16[8,80,1024]{2,1,0:T(8,128)(2,1)} %get-tuple-element.72) | copy-start | bytes 3932164
  366.1 16.8 %copy-start.24 = (bf16[8,80,1024]{2,1,0:T(8,128)(2,1)S(1)}, bf16[8,80,1024]{2,1,0:T(8,128)(2,1)}, u32[]{:S(2)}) copy-start(bf16[8,80,1024]{2,1,0:T(8,128)(2,1)} %get-tuple-element.73) | copy-start | bytes 3932164
  381.5 11.1 %copy-start.7 = (bf16[512,1024]{1,0:T(8,128)(2,1)S(1)}, bf16[512,1024]{1,0:T(8,128)(2,1)}, u32[]{:S(2)}) copy-start(bf16[512,1024]{1,0:T(8,128)(2,1)} %copy-done.6) | copy-start | bytes 3145732
  381.5 33.1 %collective-permute-start.11 = (bf16[640,1024]{1,0:T(8,128)(2,1)S(1)}, bf16[640,1024]{1,0:T(8,128)(2,1)S(1)}, u32[]{:S(2)}, u32[]{:S(2)}) collective-permute-start(bf16[640,1024]{1,0:T(8,128)(2,1)S(1)} %bitcast_add_fusion.3), channel_id=1, source_target_pairs={{8,0},{16,8},{24,16},{9,1},{17,9},{25,17},{10,2},{18,10},{26,18},{... | collective-permute-start | bytes 3932168 | tf_op jit(solution)/shard_map/ppermute | solution.py:891
  383.2 31.4 %collective-permute-start.10 = (bf16[640,1024]{1,0:T(8,128)(2,1)S(1)}, bf16[640,1024]{1,0:T(8,128)(2,1)S(1)}, u32[]{:S(2)}, u32[]{:S(2)}) collective-permute-start(bf16[640,1024]{1,0:T(8,128)(2,1)S(1)} %bitcast_add_fusion.2), channel_id=1, source_target_pairs={{0,8},{8,16},{16,24},{1,9},{9,17},{17,25},{2,10},{10,18},{18,26},{... | collective-permute-start | bytes 3932168 | tf_op jit(solution)/shard_map/ppermute | solution.py:891
  395.8 18.8 %copy-start.22 = (bf16[8,80,1024]{2,1,0:T(8,128)(2,1)S(1)}, bf16[8,80,1024]{2,1,0:T(8,128)(2,1)}, u32[]{:S(2)}) copy-start(bf16[8,80,1024]{2,1,0:T(8,128)(2,1)} %get-tuple-element.89) | copy-start | bytes 3932164
  414.6 7.4 %copy-start.8 = (bf16[512,3072]{1,0:T(8,128)(2,1)}, bf16[512,3072]{1,0:T(8,128)(2,1)S(1)}, u32[]{:S(2)}) copy-start(bf16[512,3072]{1,0:T(8,128)(2,1)S(1)} %attn_bwd.1) | copy-start | bytes 9437188
  416.6 23.6 %all-to-all-start.1 = ((bf16[8,80,1024]{2,1,0:T(8,128)(2,1)}), bf16[8,80,1024]{2,1,0:T(8,128)(2,1)}, u32[]{:S(2)}, u32[]{:S(2)}) async-start(bf16[8,80,1024]{2,1,0:T(8,128)(2,1)} %bitcast.66), calls=%async_computation.1 | async-start | bytes 2621440 | tf_op jit(solution)/shard_map/all_to_all | solution.py:1099
  422.0 7.1 %copy-start.13 = (bf16[512,1024]{1,0:T(8,128)(2,1)S(1)}, bf16[512,1024]{1,0:T(8,128)(2,1)}, u32[]{:S(2)}) copy-start(bf16[512,1024]{1,0:T(8,128)(2,1)} %param.13) | copy-start | bytes 3145732
  422.0 7.1 %copy-start.16 = (f32[512,1024]{1,0:T(8,128)S(1)}, f32[512,1024]{1,0:T(8,128)}, u32[]{:S(2)}) copy-start(f32[512,1024]{1,0:T(8,128)} %copy-done.15) | copy-start | bytes 6291460
  432.0 8.3 %copy-start.3 = (f32[512,1024]{1,0:T(8,128)S(1)}, f32[512,1024]{1,0:T(8,128)}, u32[]{:S(2)}) copy-start(f32[512,1024]{1,0:T(8,128)} %copy-done.2) | copy-start | bytes 6291460
  616.7 5.7 copy-start.29
  (20 other events, 54.9 us)
Sparse Core Ops, SparseCore 0:
  35.8 44.9 all-gather.4
  82.7 27.8 all-gather.6
  112.5 68.4 all-gather.10
  182.7 59.4 all-gather.8

commit v5 on v4

--- a/solution.py
+++ b/solution.py
@@ -11,6 +11,8 @@
 SHORT_SEQS = 4
 PAIR = 2 * HEAD
 NEG = -1e30
+SPLIT = 2
+LAG = 2
 ROOT = 0.7978845608028654
 CUBE = 0.044715
 F32 = jnp.float32
@@ -159,7 +161,7 @@
         out_specs=pl.BlockSpec((length, 3 * width), lambda j: (0, 0)),
         out_shape=jax.ShapeDtypeStruct((length, 3 * width), BF16),
         compiler_params=params(40),
-        cost_estimate=cost(20 * length * length * width, 20 * length * width),
+        cost_estimate=cost(length, length),
         name="attn_bwd",
     )(flag, qkv, qkv, qkv, grad, lse)
 
@@ -488,6 +490,11 @@
                 home[0] = part[0, 0, start : start + capacity]
                 home_slab[0] = part[0, 0, rows : rows + 16]
 
+    def first_hop(w):
+        for n in range(each):
+            pl.when(w * each + n > 0)(lambda n=n: a_copy(w * each + n).wait_recv())
+        start_hop(z_copy, z_sends, w, 1)
+
     far = [1, last]
     near = [k for k in range(layers) if k not in far]
 
@@ -496,11 +503,7 @@
         gathers = i < waves
         works = jnp.logical_and(i >= 1, i <= waves)
 
-        @pl.when(gathers)
-        def _():
-            for n in range(each):
-                pl.when(i * each + n > 0)(lambda n=n: a_copy(i * each + n).wait_recv())
-            start_hop(z_copy, z_sends, i, 1)
+        pl.when(i == 0)(lambda: first_hop(0))
 
         @pl.when(works)
         def _():
@@ -517,6 +520,8 @@
             def _():
                 get_hop(z_copy, z_gets, i, s)
                 start_hop(z_copy, z_sends, i, s + 1)
+                if s == last - 1:
+                    pl.when(i + 1 < waves)(lambda: first_hop(i + 1))
 
             @pl.when(works)
             def _():
@@ -611,7 +616,7 @@
     return outs[0], outs[1], outs[2 : 2 + layers], outs[2 + layers], outs[3 + layers]
 
 
-def sums_kernel(plan, layers, groups, small_ref, *refs):
+def sums_kernel(plan, split, layers, groups, small_ref, *refs):
     count = len(plan)
     mats, outs = refs[:count], refs[count : 2 * count]
     (
@@ -627,17 +632,22 @@
     sibling = me + 1 - 2 * core
     mesh_id = pl.DeviceIdType.MESH
     chip_at = lambda j: lax.rem(chip + j, chips)
-    pieces = [(m, i) for m in range(count) for i in range(plan[m])]
+    pieces = [(m, i, n) for m in range(count) for i in range(plan[m]) for n in range(split)]
+    lines = held.shape[1]
+    square = chips == 4
+    by_one = chip + 1 - 2 * lax.rem(chip, 2)
+    by_two = chip + 2 - 4 * (chip // 2)
     at_end = jnp.logical_or(here == 0, here == last)
     inside = jnp.logical_and(here > 0, here < last)
     inward = 1 + (here // last) * (last - 2)
     outward = lax.rem((here - 1) * last + layers * last, layers)
     across = last - here
 
-    def source(m, i, half):
+    def source(m, i, n, half):
+        span = pl.ds(n * lines, lines)
         if len(mats[m].shape) == 5:
-            return mats[m].at[:, half, i]
-        return mats[m].at[:, half, :, pl.ds(i * width, width)]
+            return mats[m].at[:, half, i, span]
+        return mats[m].at[:, half, span, pl.ds(i * width, width)]
 
     def remote(src, dst, send, recv, where):
         return pltpu.make_async_remote_copy(
@@ -652,6 +662,24 @@
             own.at[c, chip_at(j)], got.at[c, j - 1], x_send.at[c, j - 1], x_recv.at[c, j - 1],
             {"ep": 2 * chip_at(j) + core},
         )
+
+    def near_chip(c):
+        return by_one + lax.rem(c, 2) * (by_two - by_one)
+
+    def next_chip(c):
+        return by_two + lax.rem(c, 2) * (by_one - by_two)
+
+    def y_copy(c, n):
+        block = (near_chip(c), 3 - chip, next_chip(c))[n]
+        where = next_chip(c) if n == 2 else near_chip(c)
+        return remote(
+            own.at[c, block], got.at[c, n], x_send.at[c, n], x_recv.at[c, n], {"ep": 2 * where + core}
+        )
+
+    lags = [LAG * n for n in range(1, 6)] if square else [0] + [LAG * n for n in range(1, 5)]
+
+    def due(t, n):
+        return jnp.logical_and(t >= lags[n], t < total + lags[n])
 
     def z_copy(c, n):
         src = (held, held, inner)[n]
@@ -713,40 +741,59 @@
                 own[t, p] = own[t, p] + sib[t, p]
 
             over(0, chips, add)
-            over(1, chips, lambda j: x_copy(t, j).start())
-
-        @pl.when(jnp.logical_and(t >= 1, t <= total))
+            if square:
+                y_copy(t, 1).start()
+                y_copy(t, 0).start()
+            else:
+                over(1, chips, lambda j: x_copy(t, j).start())
+
+        if square:
+
+            @pl.when(due(t, 0))
+            def _():
+                c = t - lags[0]
+                y_copy(c, 1).wait_recv()
+                own[c, next_chip(c)] = own[c, next_chip(c)] + got[c, 1]
+                y_copy(c, 2).start()
+                y_copy(c, 0).wait_recv()
+                own[c, chip] = own[c, chip] + got[c, 0]
+
+        @pl.when(due(t, 1))
         def _():
-            c = t - 1
-            over(1, chips, lambda j: x_copy(c, j).wait_recv())
-            wide[c] = own[c, chip].astype(F32)
-
-            def add(j):
-                wide[c] += got[c, j - 1].astype(F32)
-
-            over(1, chips, add)
-            held[c] = wide[c].astype(BF16)
+            c = t - lags[1]
+            if square:
+                y_copy(c, 2).wait_recv()
+                held[c] = own[c, chip] + got[c, 2]
+            else:
+                over(1, chips, lambda j: x_copy(c, j).wait_recv())
+                wide[c] = own[c, chip].astype(F32)
+
+                def add(j):
+                    wide[c] += got[c, j - 1].astype(F32)
+
+                over(1, chips, add)
+                held[c] = wide[c].astype(BF16)
             pl.when(at_end)(lambda: z_copy(c, 0).start())
 
-        @pl.when(jnp.logical_and(inside, jnp.logical_and(t >= 2, t <= total + 1)))
+        @pl.when(jnp.logical_and(inside, due(t, 2)))
         def _():
-            c = t - 2
+            c = t - lags[2]
             z_copy(c, 0).wait_recv()
             held[c] = held[c] + inner[c]
             z_copy(c, 1).start()
 
-        @pl.when(jnp.logical_and(inside, jnp.logical_and(t >= 3, t <= total + 2)))
+        @pl.when(jnp.logical_and(inside, due(t, 3)))
         def _():
-            c = t - 3
+            c = t - lags[3]
             z_copy(c, 1).wait_recv()
             both = held[c] + final[c]
             inner[c] = both
             wide[c] = both.astype(F32)
             z_copy(c, 2).start()
 
-        @pl.when(jnp.logical_and(at_end, t >= 4))
+        @pl.when(jnp.logical_and(at_end, due(t, 4)))
         def _():
-            c = t - 4
+            c = t - lags[4]
             z_copy(c, 2).wait_recv()
             wide[c] = final[c].astype(F32)
 
@@ -767,11 +814,15 @@
 
         return carry
 
-    lax.fori_loop(0, total + 4, body, 0)
+    lax.fori_loop(0, total + lags[4], body, 0)
 
     copies = []
-    for c, (m, i) in enumerate(pieces):
-        spot = outs[m].at[i] if len(outs[m].shape) == 3 else outs[m].at[:, pl.ds(i * width, width)]
+    for c, (m, i, n) in enumerate(pieces):
+        span = pl.ds(n * lines, lines)
+        if len(outs[m].shape) == 3:
+            spot = outs[m].at[i, span]
+        else:
+            spot = outs[m].at[span, pl.ds(i * width, width)]
         copies.append(pltpu.make_async_copy(wide.at[c], spot, o_sem.at[c]))
         copies[-1].start()
 
@@ -787,7 +838,11 @@
 
     def sent(c):
         remote(own.at[c], sib.at[c], s_send.at[c], s_recv.at[c], {"ep": sibling}).wait_send()
-        over(1, chips, lambda j: x_copy(c, j).wait_send())
+        if square:
+            for n in range(3):
+                y_copy(c, n).wait_send()
+        else:
+            over(1, chips, lambda j: x_copy(c, j).wait_send())
         pl.when(at_end)(lambda: z_copy(c, 0).wait_send())
 
         @pl.when(inside)
@@ -806,7 +861,8 @@
     width = small.shape[1]
     plan = [a.shape[1] // width for a in columns] + [a.shape[0] // width for a in rows_split]
     high = columns[0].shape[0] // groups
-    total = sum(plan)
+    split = SPLIT if high % (16 * SPLIT) == 0 else 1
+    total, lines = sum(plan) * split, high // split
     views = [a.reshape(chips, 2, high, a.shape[1]) for a in columns] + [
         a.reshape(chips, 2, n, high, width) for a, n in zip(rows_split, plan[len(columns) :])
     ]
@@ -816,9 +872,9 @@
     sem = pltpu.SemaphoreType.DMA
     vmem = pl.BlockSpec(memory_space=pltpu.VMEM)
     anywhere = pl.BlockSpec(memory_space=pl.ANY)
-    buffers = lambda *lead: pltpu.VMEM((total, *lead, high, width), BF16)
+    buffers = lambda *lead: pltpu.VMEM((total, *lead, lines, width), BF16)
     outs = pl.pallas_call(
-        functools.partial(sums_kernel, plan, layers, groups),
+        functools.partial(sums_kernel, plan, split, layers, groups),
         in_specs=[vmem] + [anywhere] * len(views),
         out_specs=[anywhere] * len(views) + [vmem],
         out_shape=shapes + [jax.ShapeDtypeStruct(small.shape, F32)],
@@ -829,7 +885,7 @@
             buffers(),
             buffers(),
             buffers(),
-            pltpu.VMEM((total, high, width), F32),
+            pltpu.VMEM((total, lines, width), F32),
             pltpu.VMEM(small.shape, F32),
             pltpu.VMEM((chips, *small.shape), F32),
             pltpu.VMEM((layers, *small.shape), F32),
@@ -847,7 +903,7 @@
         compiler_params=pltpu.CompilerParams(
             collective_id=1, has_side_effects=True, vmem_limit_bytes=62 << 20
         ),
-        cost_estimate=cost(10 * total * chips * high * width, 8 * total * chips * high * width),
+        cost_estimate=cost(10 * total * chips * lines * width, 8 * total * chips * lines * width),
         name="gradient_sums",
     )(small, *views)
     rows_out = [a.reshape(-1, width) for a in outs[len(columns) : -1]]
@@ -1059,19 +1115,8 @@
             mids, [c[3] for c in chunks], [c[2] for c in chunks], [c[4] for c in chunks]
         )
 
-    last = layers - 1
-    out_up, out_down = send_hop(outs[last], 1, 1), send_hop(outs[1], -1, 1)
+    outs = [back(k, outs[k]) for k in range(layers)]
     dense_out, mid_grad_dense, up_grad, down_grad = dense_branch(mid_low, dense_grad, up_full, down_full)
-
-    def out_step(stage, *others):
-        held = lax.optimization_barrier((out_up, out_down, *others))
-        return (
-            send_hop(held[0] + outs[layers - stage], 1, stage),
-            send_hop(held[1] + outs[stage], -1, stage),
-            *held[2:],
-        )
-
-    out_up, out_down, dense_out = out_step(2, dense_out)
     in_rows = returned.reshape(slots, width)
     mix_dot1 = jnp.sum(table.astype(F32) * dot_back, axis=1, keepdims=True)
     mix_dot0 = jnp.sum(grad_out * dense_out, axis=-1, keepdims=True)
@@ -1086,21 +1131,12 @@
     attn_out_grad = res_grad.astype(BF16)
     out_weight_grad = dot_tn(attended, attn_out_grad)
     attended_grad = dot_nt(attn_out_grad, out_full).astype(BF16)
-    for stage in range(3, layers):
-        out_up, out_down, attended_grad = out_step(stage, attended_grad)
     qkv_grad = attention_backward(qkv_rows, bucket, attended_grad, lse)
-    out_up, out_down, qkv_grad = lax.optimization_barrier((out_up, out_down, qkv_grad))
     qkv_weight_grad = dot_tn(normed_in, qkv_grad)
     normed_grad = dot_nt(qkv_grad, qkv_full)
     ln1_gain_grad = jnp.sum(normed_grad * unit1, axis=0)
     tokens_grad = res_grad + norm_backward(normed_grad, ln1_gain, unit1, inverse1)
 
-    out_sum = total([outs[0], out_up, out_down]).astype(BF16).reshape(groups, capacity, width)
-    out_back = lax.all_to_all(out_sum, "ep", split_axis=0, concat_axis=0, tiled=True)
-    expert_out = dot_nn(table, out_back.reshape(slots, width))
-    result = (hidden_res + mix0 * dense_out + mix1 * expert_out).astype(BF16)
-
-    ln1_gain_grad, result = lax.optimization_barrier((ln1_gain_grad, result))
     small = jnp.concatenate([ln1_gain_grad[None], ln2_gain_grad[None], mix_weight_grad.T], axis=0)
     small = jnp.pad(small, ((0, 4), (0, 0)))
     if layers == 4 and length // groups >= 16:
@@ -1113,6 +1149,12 @@
         sums = [sum_layers(scatter(a)) for a in (qkv_weight_grad, out_weight_grad, up_grad, down_grad)]
         qkv_final, out_final, up_final, down_final = sums
         small_sums = sum_everywhere(small)
+    outs = list(after(tuple(outs), small_sums))
+    out_sum = total(outs).astype(BF16).reshape(groups, capacity, width)
+    out_back = lax.all_to_all(out_sum, "ep", split_axis=0, concat_axis=0, tiled=True)
+    expert_out = dot_nn(table, out_back.reshape(slots, width))
+    result = (hidden_res + mix0 * dense_out + mix1 * expert_out).astype(BF16)
+
     return (
         result,
         tokens_grad,

time: 650 us -> 582 us (0.90)
  Pallas kernels: 417 us -> 373 us
  starting transfers between devices: 42.8 us -> 28.1 us
  waiting for transfers between devices: 85.8 us -> 77.2 us
    pallas_call x1, Pallas kernels: 172 us -> 134 us  [gradient_sums(): pl.pallas_call(functools.partial(sums_kernel, plan, split, layers, groups...]
    ppermute x6 -> x3, waiting for transfers between devices: 15.1 us -> 0.01 us  [shifted(): lax.ppermute(rows, 'dp', [((i + step) % size, i) for i in range(size)])]
    ppermute x6 -> x3, starting transfers between devices: 20.1 us -> 5.35 us  [shifted(): lax.ppermute(rows, 'dp', [((i + step) % size, i) for i in range(size)])]
    all_to_all x1, waiting for transfers between devices: 2.79 us -> 12.6 us  [on_device(): lax.all_to_all(out_sum, 'ep', split_axis=0, concat_axis=0, tiled=True)]
    unnamed x75 -> x77, local copies, waits for them, and re-layouts: 20.7 us -> 23.6 us
  transfers between devices with their start and end apart: 18 -> 15, of which waited for: 8 -> 6; matrix products, arithmetic and copies ran while one was open for 6% -> 7% of each run, Pallas kernels for 38% -> 65%
where the time goes in v5:
time: 582 us; the launch traced here: 573 us
  Pallas kernels  373 us (64%)
  waiting for transfers between devices  77.2 us (13%)
  matrix products  37.5 us (6%)
  starting transfers between devices  28.1 us (5%)
  local copies, waits for them, and re-layouts  25.7 us (4%)
  other arithmetic  16.5 us (3%)
  between operations  15.3 us (3%)
    pallas_call x1, Pallas kernels, expert_exchange(): pl.pallas_call(functools.partial(exchange_kernel, waves, layers, groups),...  168 us
    pallas_call x1, Pallas kernels, gradient_sums(): pl.pallas_call(functools.partial(sums_kernel, plan, split, layers, groups...  134 us
    ppermute x6, waiting for transfers between devices, hop(): return lax.ppermute(rows, 'dp', pairs)  39 us
    pallas_call x1, Pallas kernels, dense_branch(): pl.pallas_call(dense_kernel, grid=(ff // tile,), in_specs=[whole, whole,...  36.4 us
    unnamed x77, local copies, waits for them, and re-layouts  23.6 us
    pallas_call x1, Pallas kernels, attention_backward(): pl.pallas_call(functools.partial(attn_bwd_kernel, tile), grid=(pairs,), i...  19 us
    dot_general x6, matrix products, dot_nn(): lax.dot_general(a, b, (((1,), (0,)), ((), ())), preferred_element_type=F32)  17 us
    all_to_all x1, waiting for transfers between devices, on_device(): lax.all_to_all(a, 'ep', split_axis=0, concat_axis=1, tiled=True)  16.2 us
  transfers between devices with their start and end apart: 15, of which 6 were waited for; matrix products, arithmetic and copies ran while one was open for 7% of the time, Pallas kernels for 65%

profile of v5, /device:TPU:0, one launch (start us, length us, event | category | flops | bytes accessed | tf_op | source)
XLA Modules:
  0.0 573.3 jit_solution(2643037195217459632)
XLA Ops:
  8.9 3.2 convolution_convert_fusion.4
  12.1 5.3 all-to-all-start
  19.5 16.2 %all-to-all-done = bf16[8,80,1024]{2,1,0:T(8,128)(2,1)S(1)} async-done(((bf16[8,80,1024]{2,1,0:T(8,128)(2,1)}), bf16[8,80,1024]{2,1,0:T(8,128)(2,1)S(1)}, u32[]{:S(2)}, u32[]{:S(2)}) %all-to-all-start) | async-done | bytes 1310752 | tf_op jit(solution)/shard_map/all_to_all | solution.py:1016
  39.1 5.6 collective-permute-start
  44.7 22.8 %collective-permute-done.1 = bf16[640,1024]{1,0:T(8,128)(2,1)} collective-permute-done((bf16[640,1024]{1,0:T(8,128)(2,1)S(1)}, bf16[640,1024]{1,0:T(8,128)(2,1)}, u32[]{:S(2)}, u32[]{:S(2)}) %collective-permute-start.1) | collective-permute-done | bytes 1310752 | tf_op jit(solution)/shard_map/ppermute | solution.py:934
  68.6 1.7 collective-permute-start.2
  73.3 7.5 %all-gather.5.cloned.1.call-done = bf16[1024,3072]{1,0:T(8,128)(2,1)} async-done(((bf16[128,3072]{1,0:T(8,128)(2,1)}), bf16[1024,3072]{1,0:T(8,128)(2,1)}) %all-gather.5.cloned.1.call-update) | async-done | bytes 6291472 | tf_op jit(solution)/shard_map/all_gather | solution.py:1015
  80.8 6.5 %convolution_convert_fusion.1.q_ref.k_ref.v_ref = bf16[512,3072]{1,0:T(8,128)(2,1)S(1)} fusion(bf16[512,1024]{1,0:T(8,128)(2,1)} %fusion.6, bf16[1024,3072]{1,0:T(8,128)(2,1)} %all-gather.5.cloned.1.call-done), kind=kOutput, calls=%fused_computation.1 | convolution fusion | flops 3222798336 | bytes 10485760 | tf_op jit(solution)/shard_map/dot_general | solution.py:23
  87.4 15.1 %collective-permute-done.3 = bf16[640,1024]{1,0:T(8,128)(2,1)} collective-permute-done((bf16[640,1024]{1,0:T(8,128)(2,1)}, bf16[640,1024]{1,0:T(8,128)(2,1)}, u32[]{:S(2)}, u32[]{:S(2)}) %collective-permute-start.3) | collective-permute-done | bytes 1310752 | tf_op jit(solution)/shard_map/ppermute | solution.py:934
  102.4 1.7 collective-permute-start.4
  105.5 15.8 %attn_fwd.1 = (bf16[512,1024]{1,0:T(8,128)(2,1)S(1)}, f32[512,1024]{1,0:T(8,128)S(1)}) custom-call(s32[1]{0:T(128)S(6)} %copy.32.flag_ref, bf16[512,3072]{1,0:T(8,128)(2,1)S(1)} %convolution_convert_fusion.1.q_ref.k_ref.v_ref, bf16[512,3072]{1,0:T(8,128)(2,1)S(1)} %convolution_convert_fusion.1.q_ref.k_ref.v_ref, ...), custom_call_target="tpu_custom_call" | custom-call | flops 2147483648 | bytes 5242880 | tf_op jit(solution)/shard_map/attn_fwd/pallas_call | solution.py:87
  121.3 1.7 copy-done
  124.3 3.3 fusion.29
  130.7 2.0 convolution_convert_fusion.3
  132.8 168.1 %expert_exchange.1 = (bf16[8,80,1024]{2,1,0:T(8,128)(2,1)}, bf16[8,16,1024]{2,1,0:T(8,128)(2,1)}, bf16[8,80,1024]{2,1,0:T(8,128)(2,1)}, bf16[8,80,1024]{2,1,0:T(...) custom-call(bf16[8,80,1024]{2,1,0:T(8,128)(2,1)} %bitcast.94, ...), custom_call_target="tpu_custom_call" | custom-call | flops 32212254720 | bytes 52428800 | tf_op jit(solution)/shard_map/expert_exchange/pallas_call | solution.py:583
  302.0 2.7 collective-permute-start.6
  309.0 36.4 %dense_branch.1 = (f32[512,1024]{1,0:T(8,128)S(1)}, f32[512,1024]{1,0:T(8,128)}, bf16[1024,4096]{1,0:T(8,128)(2,1)}, bf16[4096,1024]{1,0:T(8,128)(2,1)}) custom-call(bf16[512,1024]{1,0:T(8,128)(2,1)S(1)} %multiply_convert_fusion.mid_ref, bf16[512,1024]{1,0:T(8,128)(2,1)S(1)} %copy-done.4, bf16[1024,4096]{1,0:T(8,128)(2,1)} %all-gather.9.cloned.1.call-done.up_ref, ...), custom_call_target="tpu_custom_call" | custom-call | flops 512 | bytes 512 | tf_op jit(solution)/shard_map/dense_branch/pallas_call | solution.py:199
  348.3 1.6 multiply_reduce_fusion.1
  354.9 19.0 %attn_bwd.1 = bf16[512,3072]{1,0:T(8,128)(2,1)S(1)} custom-call(s32[1]{0:T(128)S(6)} %copy.32.flag_ref, bf16[512,3072]{1,0:T(8,128)(2,1)S(1)} %copy-done.1, bf16[512,3072]{1,0:T(8,128)(2,1)S(1)} %copy-done.1, bf16[512,3072]{1,0:T(8,128)(2,1)S(1)} %copy-done.1, bf16[512,1024]{1,0:T(8,128)(2,1)S(1)} %convolution_convert_fusion.5.g_ref, f32[512,1024]{1,0:T(8,128)S(1)} %copy-done.6), custom_call_target="tpu_custom_call" | custom-call | flops 512 | bytes 512 | tf_op jit(solution)/shard_map/attn_bwd/pallas_call | solution.py:150
  373.9 5.1 fusion.8
  379.9 2.6 convolution_convert_fusion.2
  382.6 5.5 convolution_convert_fusion
  388.1 133.7 %gradient_sums.1 = (f32[128,3072]{1,0:T(8,128)}, f32[128,1024]{1,0:T(8,128)}, f32[128,4096]{1,0:T(8,128)}, f32[4,128,1024]{2,1,0:T(8,128)}, f32[8,1024]{1,0:T(8,128)}) custom-call(f32[8,1024]{1,0:T(8,128)} %select_maximum_fusion.small_ref, bf16[4,2,128,3072]{3,2,1,0:T(8,128)(2,1)} %bitcast.59, bf16[4,2,128,1024]{3,2,1,0:T(8,128)(2,1)} %bitcast.62, ...), custom_call_target="tpu_custom_call" | custom-call | flops 62914560 | bytes 50331648 | tf_op jit(solution)/shard_map/gradient_sums/pallas_call | solution.py:876
  521.9 4.3 add_convert_fusion
  526.2 4.4 all-to-all-start.1
  531.9 4.4 fusion.11
  536.3 12.6 %all-to-all-done.1 = bf16[8,80,1024]{2,1,0:T(8,128)(2,1)} async-done(((bf16[8,80,1024]{2,1,0:T(8,128)(2,1)}), bf16[8,80,1024]{2,1,0:T(8,128)(2,1)}, u32[]{:S(2)}, u32[]{:S(2)}) %all-to-all-start.1) | async-done | bytes 1310752 | tf_op jit(solution)/shard_map/all_to_all | solution.py:1154
  548.9 4.2 add_convert_fusion.1
  559.0 1.6 copy-done.18
  560.7 2.1 copy.37
  562.8 1.6 copy-done.17
  564.4 2.0 copy.38
  (132 shorter events, 37.5 us)
Async XLA Ops:
  12.1 5.4 copy-start.11
  12.1 6.0 %copy-start.30 = (f32[1024]{0:T(1024)S(1)}, f32[1024]{0:T(1024)}, u32[]{:S(2)}) copy-start(f32[1024]{0:T(1024)} %param.16) | copy-start | bytes 12292
  12.1 23.5 %all-to-all-start = ((bf16[8,80,1024]{2,1,0:T(8,128)(2,1)}), bf16[8,80,1024]{2,1,0:T(8,128)(2,1)S(1)}, u32[]{:S(2)}, u32[]{:S(2)}) async-start(bf16[8,80,1024]{2,1,0:T(8,128)(2,1)} %bitcast.66), calls=%async_computation | async-start | bytes 2621440 | tf_op jit(solution)/shard_map/all_to_all | solution.py:1016
  17.4 63.3 %all-gather.5.cloned.1.call-start = ((), (), s32[]{:S(2)}) async-start(), calls=%async_computation.2 | async-start | bytes 7077888 | tf_op jit(solution)/shard_map/all_gather | solution.py:1015
  19.5 52.7 %copy-start.28 = (bf16[1024,2]{0,1:T(2,128)(2,1)S(1)}, bf16[1024,2]{0,1:T(2,128)(2,1)}, u32[]{:S(2)}) copy-start(bf16[1024,2]{0,1:T(2,128)(2,1)} %param.22) | copy-start | bytes 12292
  35.7 51.7 %copy-start.23 = (bf16[8,80,1024]{2,1,0:T(8,128)(2,1)}, bf16[8,80,1024]{2,1,0:T(8,128)(2,1)S(1)}, u32[]{:S(2)}) copy-start(bf16[8,80,1024]{2,1,0:T(8,128)(2,1)S(1)} %all-to-all-done) | copy-start | bytes 3932164
  35.7 88.6 %all-gather.7.cloned.1.call-start = ((), (), s32[]{:S(2)}) async-start(), calls=%async_computation.3 | async-start | bytes 2359296 | tf_op jit(solution)/shard_map/all_gather | solution.py:1015
  36.4 271.2 %all-gather.9.cloned.1.call-start = ((), (), s32[]{:S(2)}) async-start(), calls=%async_computation.4 | async-start | bytes 9437184 | tf_op jit(solution)/shard_map/all_gather | solution.py:1015
  37.2 270.5 %all-gather.11.cloned.1.call-start = ((), (), s32[]{:S(2)}) async-start(), calls=%async_computation.5 | async-start | bytes 9437184 | tf_op jit(solution)/shard_map/all_gather | solution.py:1015
  37.8 29.7 %collective-permute-start.1 = (bf16[640,1024]{1,0:T(8,128)(2,1)S(1)}, bf16[640,1024]{1,0:T(8,128)(2,1)}, u32[]{:S(2)}, u32[]{:S(2)}) collective-permute-start(bf16[640,1024]{1,0:T(8,128)(2,1)S(1)} %bitcast.64), channel_id=1, source_target_pairs={{8,0},{16,8},{24,16},{9,1},{17,9},{25,17},{10,2},{18,10},{26,18},{... | collective-permute-start | bytes 3932168 | tf_op jit(solution)/shard_map/ppermute | solution.py:934
  39.1 29.5 %collective-permute-start = (bf16[640,1024]{1,0:T(8,128)(2,1)S(1)}, bf16[640,1024]{1,0:T(8,128)(2,1)}, u32[]{:S(2)}, u32[]{:S(2)}) collective-permute-start(bf16[640,1024]{1,0:T(8,128)(2,1)S(1)} %bitcast.65), channel_id=1, source_target_pairs={{0,8},{8,16},{16,24},{1,9},{9,17},{17,25},{2,10},{10,18},{18,26},{... | collective-permute-start | bytes 3932168 | tf_op jit(solution)/shard_map/ppermute | solution.py:934
  68.6 18.8 %collective-permute-start.2 = (bf16[640,1024]{1,0:T(8,128)(2,1)}, bf16[640,1024]{1,0:T(8,128)(2,1)}, u32[]{:S(2)}, u32[]{:S(2)}) collective-permute-start(bf16[640,1024]{1,0:T(8,128)(2,1)} %collective-permute-done), channel_id=1, source_target_pairs={{8,16},{16,24},{9,17},{17,25},{10,18},{18,26},{11,19},{19,27},{12,... | collective-permute-start | bytes 3932168 | tf_op jit(solution)/shard_map/ppermute | solution.py:934
  70.3 32.2 %collective-permute-start.3 = (bf16[640,1024]{1,0:T(8,128)(2,1)}, bf16[640,1024]{1,0:T(8,128)(2,1)}, u32[]{:S(2)}, u32[]{:S(2)}) collective-permute-start(bf16[640,1024]{1,0:T(8,128)(2,1)} %collective-permute-done.1), channel_id=1, source_target_pairs={{8,0},{16,8},{9,1},{17,9},{10,2},{18,10},{11,3},{19,11},{12,4},{20... | collective-permute-start | bytes 3932168 | tf_op jit(solution)/shard_map/ppermute | solution.py:934
  102.4 30.3 %collective-permute-start.4 = (bf16[640,1024]{1,0:T(8,128)(2,1)}, bf16[640,1024]{1,0:T(8,128)(2,1)}, u32[]{:S(2)}, u32[]{:S(2)}) collective-permute-start(bf16[640,1024]{1,0:T(8,128)(2,1)} %collective-permute-done.2), channel_id=1, source_target_pairs={{16,24},{17,25},{18,26},{19,27},{20,28},{21,29},{22,30},{23,31}} | collective-permute-start | bytes 3932168 | tf_op jit(solution)/shard_map/ppermute | solution.py:934
  104.2 28.6 %collective-permute-start.5 = (bf16[640,1024]{1,0:T(8,128)(2,1)}, bf16[640,1024]{1,0:T(8,128)(2,1)}, u32[]{:S(2)}, u32[]{:S(2)}) collective-permute-start(bf16[640,1024]{1,0:T(8,128)(2,1)} %collective-permute-done.3), channel_id=1, source_target_pairs={{8,0},{9,1},{10,2},{11,3},{12,4},{13,5},{14,6},{15,7}} | collective-permute-start | bytes 3932168 | tf_op jit(solution)/shard_map/ppermute | solution.py:934
  302.0 219.9 %collective-permute-start.6 = (bf16[640,1024]{1,0:T(8,128)(2,1)}, bf16[640,1024]{1,0:T(8,128)(2,1)}, u32[]{:S(2)}, u32[]{:S(2)}) collective-permute-start(bf16[640,1024]{1,0:T(8,128)(2,1)} %bitcast.93), channel_id=1, source_target_pairs={{24,0},{0,8},{8,16},{16,24},{25,1},{1,9},{9,17},{17,25},{26,2},{2,... | collective-permute-start | bytes 3932168 | tf_op jit(solution)/shard_map/ppermute | solution.py:962
  304.7 217.2 %collective-permute-start.7 = (bf16[640,1024]{1,0:T(8,128)(2,1)}, bf16[640,1024]{1,0:T(8,128)(2,1)}, u32[]{:S(2)}, u32[]{:S(2)}) collective-permute-start(bf16[640,1024]{1,0:T(8,128)(2,1)} %bitcast.92), channel_id=1, source_target_pairs={{16,0},{24,8},{0,16},{8,24},{17,1},{25,9},{1,17},{9,25},{18,2},{26... | collective-permute-start | bytes 3932168 | tf_op jit(solution)/shard_map/ppermute | solution.py:962
  306.1 215.7 %collective-permute-start.8 = (bf16[640,1024]{1,0:T(8,128)(2,1)}, bf16[640,1024]{1,0:T(8,128)(2,1)}, u32[]{:S(2)}, u32[]{:S(2)}) collective-permute-start(bf16[640,1024]{1,0:T(8,128)(2,1)} %bitcast.91), channel_id=1, source_target_pairs={{8,0},{16,8},{24,16},{0,24},{9,1},{17,9},{25,17},{1,25},{10,2},{18... | collective-permute-start | bytes 3932168 | tf_op jit(solution)/shard_map/ppermute | solution.py:962
  308.9 36.4 %copy-start.15 = (bf16[512,1024]{1,0:T(8,128)(2,1)S(1)}, bf16[512,1024]{1,0:T(8,128)(2,1)}, u32[]{:S(2)}) copy-start(bf16[512,1024]{1,0:T(8,128)(2,1)} %param.25) | copy-start | bytes 3145732
  309.0 37.7 %copy-start.25 = (bf16[8,80,1024]{2,1,0:T(8,128)(2,1)S(1)}, bf16[8,80,1024]{2,1,0:T(8,128)(2,1)}, u32[]{:S(2)}) copy-start(bf16[8,80,1024]{2,1,0:T(8,128)(2,1)} %get-tuple-element.74) | copy-start | bytes 3932164
  351.6 28.4 %copy-start.16 = (f32[512,1024]{1,0:T(8,128)}, f32[512,1024]{1,0:T(8,128)S(1)}, u32[]{:S(2)}) copy-start(f32[512,1024]{1,0:T(8,128)S(1)} %convert_add_fusion) | copy-start | bytes 6291460
  351.6 22.3 %slice-start = ((s8[6291456]{0:T(1024)(128)(4,1)}), s8[4194304]{0:T(1024)(128)(4,1)S(1)}, s32[]{:S(2)}) async-start(s8[6291456]{0:T(1024)(128)(4,1)} %bitcast.87), calls=%async_computation.6 | async-start | bytes 8388608
  354.9 19.1 %copy-start.12 = (bf16[512,1024]{1,0:T(8,128)(2,1)S(1)}, bf16[512,1024]{1,0:T(8,128)(2,1)}, u32[]{:S(2)}) copy-start(bf16[512,1024]{1,0:T(8,128)(2,1)} %param.13) | copy-start | bytes 3145732
  354.9 19.1 %slice-start.1 = ((s8[6291456]{0:T(1024)(128)(4,1)}), s8[2097152]{0:T(1024)(128)(4,1)S(1)}, s32[]{:S(2)}) async-start(s8[6291456]{0:T(1024)(128)(4,1)} %bitcast.87), calls=%async_computation.7 | async-start | bytes 4194304
  373.9 6.0 %copy-start.8 = (bf16[512,1024]{1,0:T(8,128)(2,1)S(1)}, bf16[512,1024]{1,0:T(8,128)(2,1)}, u32[]{:S(2)}) copy-start(bf16[512,1024]{1,0:T(8,128)(2,1)} %copy-done.7) | copy-start | bytes 3145732
  388.1 133.8 %copy-start.24 = (bf16[8,80,1024]{2,1,0:T(8,128)(2,1)S(1)}, bf16[8,80,1024]{2,1,0:T(8,128)(2,1)}, u32[]{:S(2)}) copy-start(bf16[8,80,1024]{2,1,0:T(8,128)(2,1)} %get-tuple-element.68) | copy-start | bytes 3932164
  526.2 4.4 copy-start.31
  526.2 5.7 copy-start.13
  526.2 22.6 %all-to-all-start.1 = ((bf16[8,80,1024]{2,1,0:T(8,128)(2,1)}), bf16[8,80,1024]{2,1,0:T(8,128)(2,1)}, u32[]{:S(2)}, u32[]{:S(2)}) async-start(bf16[8,80,1024]{2,1,0:T(8,128)(2,1)} %bitcast.30), calls=%async_computation.1 | async-start | bytes 2621440 | tf_op jit(solution)/shard_map/all_to_all | solution.py:1154
  531.9 17.0 %copy-start.3 = (f32[512,1024]{1,0:T(8,128)S(1)}, f32[512,1024]{1,0:T(8,128)}, u32[]{:S(2)}) copy-start(f32[512,1024]{1,0:T(8,128)} %copy-done.2) | copy-start | bytes 6291460
  548.9 4.2 copy-start.22
  560.6 3.7 copy-start.17
  (18 other events, 36.6 us)
Sparse Core Ops, SparseCore 0:
  35.8 44.9 all-gather.4
  82.7 27.8 all-gather.6
  112.5 68.4 all-gather.8
  182.8 58.7 all-gather.10

commit v6 on v5

--- a/solution.py
+++ b/solution.py
@@ -190,7 +190,7 @@
         mg_ref[...] += mg
 
 
-def dense_branch(mid, dg, up, down, tile=512):
+def dense_branch(mid, dg, up, down, tile=1024):
     length, width = mid.shape
     ff = up.shape[1]
     whole = pl.BlockSpec((length, width), lambda j: (0, 0))
@@ -322,17 +322,33 @@
 
     def z_copy(w, way, s):
         src, dst = ((layers - s + 1) % layers, layers - s) if way == 0 else (s - 1, s)
-        return pltpu.make_async_remote_copy(
-            buf.at[w, src], buf.at[w, dst], z_send.at[w, way, s - 1], z_recv.at[w, way, s - 1],
-            device_id={"dp": up_id if way == 0 else down_id}, device_id_type=mesh_id,
-        )
+        return [
+            pltpu.make_async_remote_copy(
+                buf.at[w, src], buf.at[w, dst], z_send.at[w, way, s - 1], z_recv.at[w, way, s - 1],
+                device_id={"dp": up_id if way == 0 else down_id}, device_id_type=mesh_id,
+            )
+        ]
+
+    lanes = -(-rows // 128) * 128
+    main, extra_rows = pl.ds(0, rows), pl.ds(rows, 16)
 
     def r_copy(w, way, s):
-        return pltpu.make_async_remote_copy(
-            part.at[w, layers - s if way == 0 else s], got.at[w, way, s - 1],
-            r_send.at[w, way, s - 1], r_recv.at[w, way, s - 1],
-            device_id={"dp": up_id if way == 0 else down_id}, device_id_type=mesh_id,
-        )
+        k = layers - s if way == 0 else s
+        return [
+            pltpu.make_async_remote_copy(
+                src, dst, r_send.at[w, way, s - 1, n], r_recv.at[w, way, s - 1, n],
+                device_id={"dp": up_id if way == 0 else down_id}, device_id_type=mesh_id,
+            )
+            for n, (src, dst) in enumerate(
+                (
+                    (part.at[w, k, main], got.at[w, way, s - 1, main]),
+                    (
+                        part.at[w, k, extra_rows, pl.ds(0, lanes)],
+                        got.at[w, way, s - 1, extra_rows, pl.ds(0, lanes)],
+                    ),
+                )
+            )
+        ]
 
     def b_copies(j):
         w, i = j // each, lax.rem(j, each)
@@ -345,7 +361,7 @@
             for n, (src, dst) in enumerate(
                 (
                     (part.at[w, 0, pl.ds(start, capacity)], home.at[j]),
-                    (part.at[w, 0, pl.ds(rows, 16)], home_slab.at[j]),
+                    (part.at[w, 0, extra_rows, pl.ds(0, lanes)], home_slab.at[j]),
                 )
             )
         ]
@@ -457,18 +473,19 @@
 
     def start_hop(copy, sends, w, s):
         for way in range(2):
-            pl.when(sends(way, s))(lambda way=way: copy(w, way, s).start())
+            pl.when(sends(way, s))(lambda way=way: [c.start() for c in copy(w, way, s)][:0] or None)
 
     def get_hop(copy, gets, w, s):
         for way in range(2):
-            pl.when(gets(way, s))(lambda way=way: copy(w, way, s).wait_recv())
+            pl.when(gets(way, s))(lambda way=way: [c.wait_recv() for c in copy(w, way, s)][:0] or None)
 
     def pass_on(w, s):
         for way in range(2):
 
             @pl.when(r_gets(way, s))
             def _():
-                r_copy(w, way, s).wait_recv()
+                for copy in r_copy(w, way, s):
+                    copy.wait_recv()
                 add_to(w, layers - s - 1 if way == 0 else s + 1, [(way, s)])
 
         start_hop(r_copy, r_sends, w, s + 1)
@@ -488,7 +505,7 @@
             @pl.when(j == 0)
             def _():
                 home[0] = part[0, 0, start : start + capacity]
-                home_slab[0] = part[0, 0, rows : rows + 16]
+                home_slab[0] = part[0, 0, rows : rows + 16, 0:lanes]
 
     def first_hop(w):
         for n in range(each):
@@ -498,46 +515,35 @@
     far = [1, last]
     near = [k for k in range(layers) if k not in far]
 
-    def body(i, carry):
-        w = i - 1
-        gathers = i < waves
-        works = jnp.logical_and(i >= 1, i <= waves)
-
-        pl.when(i == 0)(lambda: first_hop(0))
-
-        @pl.when(works)
+    def valid(w):
+        return jnp.logical_and(w >= 0, w < waves)
+
+    def body(t, carry):
+        for s in range(1, layers):
+            pl.when(valid(t - s))(lambda s=s: get_hop(z_copy, z_gets, t - s, s))
+        for s in range(2, layers):
+            pl.when(valid(t + 1 - s))(lambda s=s: start_hop(z_copy, z_sends, t + 1 - s, s))
+        pl.when(t + 1 < waves)(lambda: first_hop(t + 1))
+        w = t - last
+
+        @pl.when(valid(w))
         def _():
             piece(w, far)
             start_hop(r_copy, r_sends, w, 1)
 
-        @pl.when(i >= 2)
+        for s in range(1, last):
+            pl.when(valid(w - s))(lambda s=s: pass_on(w - s, s))
+        pl.when(valid(w - last))(lambda: finish(w - last))
+
+        @pl.when(valid(w))
         def _():
-            finish(i - 2)
-
-        for s in range(1, last):
-
-            @pl.when(gathers)
-            def _():
-                get_hop(z_copy, z_gets, i, s)
-                start_hop(z_copy, z_sends, i, s + 1)
-                if s == last - 1:
-                    pl.when(i + 1 < waves)(lambda: first_hop(i + 1))
-
-            @pl.when(works)
-            def _():
-                if s == 1:
-                    piece(w, near)
-                if s == last - 1:
-                    weight_grads(w)
-                pass_on(w, s)
-
-        @pl.when(gathers)
-        def _():
-            get_hop(z_copy, z_gets, i, last)
+            piece(w, near)
+            weight_grads(w)
 
         return carry
 
-    lax.fori_loop(0, waves + 2, body, 0)
+    first_hop(0)
+    lax.fori_loop(0, waves + 2 * last, body, 0)
 
     def land(j, carry):
         for copy in b_copies(j):
@@ -551,8 +557,13 @@
     def sent(w, carry):
         for way in range(2):
             for s in range(1, layers):
-                pl.when(z_sends(way, s))(lambda: z_copy(w, way, s).wait_send())
-                pl.when(r_sends(way, s))(lambda: r_copy(w, way, s).wait_send())
+                for copy, sends in ((z_copy, z_sends), (r_copy, r_sends)):
+
+                    @pl.when(sends(way, s))
+                    def _():
+                        for one in copy(w, way, s):
+                            one.wait_send()
+
         return carry
 
     lax.fori_loop(0, waves, sent, 0)
@@ -566,7 +577,7 @@
 
 
 def exchange_waves(groups):
-    return 4 if groups % 4 == 0 else 1
+    return 8 if groups % 8 == 0 else 1
 
 
 def expert_exchange(slots, g_low, g_high, mix_pad, up, down):
@@ -576,6 +587,7 @@
     _, capacity, width = slots.shape
     hidden = up.shape[1]
     rows = each * capacity
+    lanes = -(-rows // 128) * 128
     sem = pltpu.SemaphoreType.DMA
     block = jax.ShapeDtypeStruct((groups, capacity, width), BF16)
     vmem = pl.BlockSpec(memory_space=pltpu.VMEM)
@@ -584,7 +596,7 @@
         functools.partial(exchange_kernel, waves, layers, groups),
         in_specs=[vmem] + [pl.BlockSpec(memory_space=pl.ANY)] * (2 * layers - 1) + [vmem] * 3,
         out_specs=[vmem] * (4 + layers),
-        out_shape=[block, jax.ShapeDtypeStruct((groups, 16, width), BF16)]
+        out_shape=[block, jax.ShapeDtypeStruct((groups, 16, lanes), BF16)]
         + [block] * layers
         + [jax.ShapeDtypeStruct((width, hidden), F32), jax.ShapeDtypeStruct((hidden, width), F32)],
         scratch_shapes=[
@@ -596,14 +608,14 @@
             pltpu.VMEM((layers * rows, hidden), BF16),
             pltpu.VMEM((layers * rows, width), BF16),
             pltpu.VMEM((groups, capacity, width), BF16),
-            pltpu.VMEM((groups, 16, width), BF16),
+            pltpu.VMEM((groups, 16, lanes), BF16),
             sem((layers,)),
             sem((groups,)),
             sem((groups,)),
             sem((waves, 2, layers - 1)),
             sem((waves, 2, layers - 1)),
-            sem((waves, 2, layers - 1)),
-            sem((waves, 2, layers - 1)),
+            sem((waves, 2, layers - 1, 2)),
+            sem((waves, 2, layers - 1, 2)),
             sem((groups, 2)),
             sem((groups, 2)),
         ],
@@ -620,7 +632,7 @@
     count = len(plan)
     mats, outs = refs[:count], refs[count : 2 * count]
     (
-        small_out, own, sib, got, held, inner, final, wide, small_two, small_chip, small_layer,
+        small_out, own, sib, got, held, inner, final, small_two, small_chip, small_layer,
         own_sem, s_send, s_recv, x_send, x_recv, z_send, z_recv, t_send, t_recv, o_sem,
     ) = refs[2 * count :]
     chips = groups // 2
@@ -766,13 +778,9 @@
                 held[c] = own[c, chip] + got[c, 2]
             else:
                 over(1, chips, lambda j: x_copy(c, j).wait_recv())
-                wide[c] = own[c, chip].astype(F32)
-
-                def add(j):
-                    wide[c] += got[c, j - 1].astype(F32)
-
-                over(1, chips, add)
-                held[c] = wide[c].astype(BF16)
+                held[c] = lax.fori_loop(
+                    1, chips, lambda j, acc: acc + got[c, j - 1].astype(F32), own[c, chip].astype(F32)
+                ).astype(BF16)
             pl.when(at_end)(lambda: z_copy(c, 0).start())
 
         @pl.when(jnp.logical_and(inside, due(t, 2)))
@@ -786,16 +794,13 @@
         def _():
             c = t - lags[3]
             z_copy(c, 1).wait_recv()
-            both = held[c] + final[c]
-            inner[c] = both
-            wide[c] = both.astype(F32)
+            inner[c] = held[c] + final[c]
             z_copy(c, 2).start()
 
         @pl.when(jnp.logical_and(at_end, due(t, 4)))
         def _():
             c = t - lags[4]
             z_copy(c, 2).wait_recv()
-            wide[c] = final[c].astype(F32)
 
         @pl.when(t == 1)
         def _():
@@ -816,15 +821,24 @@
 
     lax.fori_loop(0, total + lags[4], body, 0)
 
-    copies = []
-    for c, (m, i, n) in enumerate(pieces):
+    def result(sums, c):
+        m, i, n = pieces[c]
         span = pl.ds(n * lines, lines)
         if len(outs[m].shape) == 3:
             spot = outs[m].at[i, span]
         else:
             spot = outs[m].at[span, pl.ds(i * width, width)]
-        copies.append(pltpu.make_async_copy(wide.at[c], spot, o_sem.at[c]))
-        copies[-1].start()
+        return pltpu.make_async_copy(sums.at[c], spot, o_sem.at[c])
+
+    @pl.when(inside)
+    def _():
+        for c in range(total):
+            result(inner, c).start()
+
+    @pl.when(at_end)
+    def _():
+        for c in range(total):
+            result(final, c).start()
 
     over(1, layers, lambda j: t_copy(2, j).wait_recv())
     acc = small_layer[0]
@@ -851,8 +865,8 @@
             z_copy(c, 2).wait_send()
 
     over(0, total, sent)
-    for copy in copies:
-        copy.wait()
+    for c in range(total):
+        result(final, c).wait()
 
 
 def gradient_sums(small, columns, rows_split):
@@ -866,8 +880,8 @@
     views = [a.reshape(chips, 2, high, a.shape[1]) for a in columns] + [
         a.reshape(chips, 2, n, high, width) for a, n in zip(rows_split, plan[len(columns) :])
     ]
-    shapes = [jax.ShapeDtypeStruct((high, a.shape[1]), F32) for a in columns] + [
-        jax.ShapeDtypeStruct((n, high, width), F32) for n in plan[len(columns) :]
+    shapes = [jax.ShapeDtypeStruct((high, a.shape[1]), BF16) for a in columns] + [
+        jax.ShapeDtypeStruct((n, high, width), BF16) for n in plan[len(columns) :]
     ]
     sem = pltpu.SemaphoreType.DMA
     vmem = pl.BlockSpec(memory_space=pltpu.VMEM)
@@ -885,7 +899,6 @@
             buffers(),
             buffers(),
             buffers(),
-            pltpu.VMEM((total, lines, width), F32),
             pltpu.VMEM(small.shape, F32),
             pltpu.VMEM((chips, *small.shape), F32),
             pltpu.VMEM((layers, *small.shape), F32),
@@ -1152,9 +1165,22 @@
     outs = list(after(tuple(outs), small_sums))
     out_sum = total(outs).astype(BF16).reshape(groups, capacity, width)
     out_back = lax.all_to_all(out_sum, "ep", split_axis=0, concat_axis=0, tiled=True)
+    bucket, qkv_final, out_final, up_final, down_final = after(
+        (bucket, qkv_final, out_final, up_final, down_final), out_sum
+    )
+    unit = jnp.where(bucket[0] < 0, 0.0, 1.0)
+    expert_up_grad, expert_down_grad, qkv_final, out_final, up_final, down_final, out_back = (
+        lax.optimization_barrier(
+            (
+                expert_up_grad * unit,
+                expert_down_grad * unit,
+                *(a.astype(F32) for a in (qkv_final, out_final, up_final, down_final)),
+                out_back,
+            )
+        )
+    )
     expert_out = dot_nn(table, out_back.reshape(slots, width))
     result = (hidden_res + mix0 * dense_out + mix1 * expert_out).astype(BF16)
-
     return (
         result,
         tokens_grad,

time: 582 us -> 555 us (0.954)
  local copies, waits for them, and re-layouts: 25.7 us -> 12.4 us
  Pallas kernels: 373 us -> 360 us
  waiting for transfers between devices: 77.2 us -> 65.3 us
  other arithmetic: 16.5 us -> 28 us
    unnamed x77 -> x71, local copies, waits for them, and re-layouts: 23.6 us -> 10.4 us
    all_to_all x1, waiting for transfers between devices: 12.6 us -> 0.67 us  [on_device(): lax.all_to_all(out_sum, 'ep', split_axis=0, concat_axis=0, tiled=True)]
    pallas_call x1, Pallas kernels: 168 us -> 158 us  [expert_exchange(): pl.pallas_call(functools.partial(exchange_kernel, waves, layers, groups),...]
    mul x0 -> x1, other arithmetic: none -> 8.91 us  [on_device(): expert_down_grad * unit]
  transfers between devices with their start and end apart: 15 -> 15, of which waited for: 6 -> 6; matrix products, arithmetic and copies ran while one was open for 7% -> 10% of each run, Pallas kernels for 65% -> 66%
where the time goes in v6:
time: 555 us; the launch traced here: 546 us
  Pallas kernels  360 us (65%)
  waiting for transfers between devices  65.3 us (12%)
  matrix products  36.9 us (7%)
  starting transfers between devices  28.3 us (5%)
  other arithmetic  28 us (5%)
  between operations  15.1 us (3%)
  local copies, waits for them, and re-layouts  12.4 us (2%)
    pallas_call x1, Pallas kernels, expert_exchange(): pl.pallas_call(functools.partial(exchange_kernel, waves, layers, groups),...  158 us
    pallas_call x1, Pallas kernels, gradient_sums(): pl.pallas_call(functools.partial(sums_kernel, plan, split, layers, groups...  132 us
    ppermute x6, waiting for transfers between devices, hop(): return lax.ppermute(rows, 'dp', pairs)  39 us
    pallas_call x1, Pallas kernels, dense_branch(): pl.pallas_call(dense_kernel, grid=(ff // tile,), in_specs=[whole, whole,...  35.2 us
    pallas_call x1, Pallas kernels, attention_backward(): pl.pallas_call(functools.partial(attn_bwd_kernel, tile), grid=(pairs,), i...  18.9 us
    dot_general x6, matrix products, dot_nn(): lax.dot_general(a, b, (((1,), (0,)), ((), ())), preferred_element_type=F32)  16.5 us
    all_to_all x1, waiting for transfers between devices, on_device(): lax.all_to_all(a, 'ep', split_axis=0, concat_axis=1, tiled=True)  16.2 us
    pallas_call x1, Pallas kernels, attention_forward(): pl.pallas_call(functools.partial(attn_fwd_kernel, tile), grid=(pairs,), i...  15.8 us
  transfers between devices with their start and end apart: 15, of which 6 were waited for; matrix products, arithmetic and copies ran while one was open for 10% of the time, Pallas kernels for 66%

profile of v6, /device:TPU:0, one launch (start us, length us, event | category | flops | bytes accessed | tf_op | source)
XLA Modules:
  0.0 546.0 jit_solution(17266561266919817644)
XLA Ops:
  8.9 3.2 convolution_convert_fusion.4
  12.1 5.3 all-to-all-start
  18.2 1.4 fusion.6
  19.5 16.2 %all-to-all-done = bf16[8,80,1024]{2,1,0:T(8,128)(2,1)S(1)} async-done(((bf16[8,80,1024]{2,1,0:T(8,128)(2,1)}), bf16[8,80,1024]{2,1,0:T(8,128)(2,1)S(1)}, u32[]{:S(2)}, u32[]{:S(2)}) %all-to-all-start) | async-done | bytes 1310752 | tf_op jit(solution)/shard_map/all_to_all | solution.py:1029
  39.1 5.7 %collective-permute-start = (bf16[640,1024]{1,0:T(8,128)(2,1)S(1)}, bf16[640,1024]{1,0:T(8,128)(2,1)}, u32[]{:S(2)}, u32[]{:S(2)}) collective-permute-start(bf16[640,1024]{1,0:T(8,128)(2,1)S(1)} %bitcast.66), channel_id=1, source_target_pairs={{0,8},{8,16},{16,24},{1,9},{9,17},{17,25},{2,10},{10,18},{18,26},{... | collective-permute-start | bytes 3932168 | tf_op jit(solution)/shard_map/ppermute | solution.py:947
  44.7 22.8 %collective-permute-done.1 = bf16[640,1024]{1,0:T(8,128)(2,1)} collective-permute-done((bf16[640,1024]{1,0:T(8,128)(2,1)S(1)}, bf16[640,1024]{1,0:T(8,128)(2,1)}, u32[]{:S(2)}, u32[]{:S(2)}) %collective-permute-start.1) | collective-permute-done | bytes 1310752 | tf_op jit(solution)/shard_map/ppermute | solution.py:947
  68.6 1.8 collective-permute-start.2
  73.3 7.5 %all-gather.5.cloned.1.call-done = bf16[1024,3072]{1,0:T(8,128)(2,1)} async-done(((bf16[128,3072]{1,0:T(8,128)(2,1)}), bf16[1024,3072]{1,0:T(8,128)(2,1)}) %all-gather.5.cloned.1.call-update) | async-done | bytes 6291472 | tf_op jit(solution)/shard_map/all_gather | solution.py:1028
  80.8 6.5 %convolution_convert_fusion.1.q_ref.k_ref.v_ref = bf16[512,3072]{1,0:T(8,128)(2,1)S(1)} fusion(bf16[512,1024]{1,0:T(8,128)(2,1)} %fusion.6, bf16[1024,3072]{1,0:T(8,128)(2,1)} %all-gather.5.cloned.1.call-done), kind=kOutput, calls=%fused_computation.1 | convolution fusion | flops 3222798336 | bytes 10485760 | tf_op jit(solution)/shard_map/dot_general | solution.py:23
  87.3 15.2 %collective-permute-done.3 = bf16[640,1024]{1,0:T(8,128)(2,1)} collective-permute-done((bf16[640,1024]{1,0:T(8,128)(2,1)}, bf16[640,1024]{1,0:T(8,128)(2,1)}, u32[]{:S(2)}, u32[]{:S(2)}) %collective-permute-start.3) | collective-permute-done | bytes 1310752 | tf_op jit(solution)/shard_map/ppermute | solution.py:947
  102.5 1.7 collective-permute-start.4
  105.5 15.8 %attn_fwd.1 = (bf16[512,1024]{1,0:T(8,128)(2,1)S(1)}, f32[512,1024]{1,0:T(8,128)S(1)}) custom-call(s32[1]{0:T(128)S(6)} %copy.26.flag_ref, bf16[512,3072]{1,0:T(8,128)(2,1)S(1)} %convolution_convert_fusion.1.q_ref.k_ref.v_ref, bf16[512,3072]{1,0:T(8,128)(2,1)S(1)} %convolution_convert_fusion.1.q_ref.k_ref.v_ref, ...), custom_call_target="tpu_custom_call" | custom-call | flops 2147483648 | bytes 5242880 | tf_op jit(solution)/shard_map/attn_fwd/pallas_call | solution.py:87
  121.3 1.7 copy-done
  124.3 3.3 fusion.27
  130.8 2.0 convolution_convert_fusion.3
  132.8 157.6 %expert_exchange.1 = (bf16[8,80,1024]{2,1,0:T(8,128)(2,1)}, bf16[8,16,128]{2,1,0:T(8,128)(2,1)}, bf16[8,80,1024]{2,1,0:T(8,128)(2,1)}, bf16[8,80,1024]{2,1,0:T(8...) custom-call(bf16[8,80,1024]{2,1,0:T(8,128)(2,1)} %bitcast.96, ...), custom_call_target="tpu_custom_call" | custom-call | flops 32212254720 | bytes 52428800 | tf_op jit(solution)/shard_map/expert_exchange/pallas_call | solution.py:595
  291.2 1.8 collective-permute-start.6
  294.1 3.2 collective-permute-start.8
  299.0 35.2 %dense_branch.1 = (f32[512,1024]{1,0:T(8,128)S(1)}, f32[512,1024]{1,0:T(8,128)}, bf16[1024,4096]{1,0:T(8,128)(2,1)}, bf16[4096,1024]{1,0:T(8,128)(2,1)}) custom-call(bf16[512,1024]{1,0:T(8,128)(2,1)S(1)} %multiply_convert_fusion.mid_ref, bf16[512,1024]{1,0:T(8,128)(2,1)S(1)} %copy-done.4, bf16[1024,4096]{1,0:T(8,128)(2,1)} %all-gather.9.cloned.1.call-done.up_ref, ...), custom_call_target="tpu_custom_call" | custom-call | flops 512 | bytes 512 | tf_op jit(solution)/shard_map/dense_branch/pallas_call | solution.py:199
  337.2 1.6 multiply_reduce_fusion.1
  343.7 18.9 %attn_bwd.1 = bf16[512,3072]{1,0:T(8,128)(2,1)S(1)} custom-call(s32[1]{0:T(128)S(6)} %copy.26.flag_ref, bf16[512,3072]{1,0:T(8,128)(2,1)S(1)} %copy-done.1, bf16[512,3072]{1,0:T(8,128)(2,1)S(1)} %copy-done.1, bf16[512,3072]{1,0:T(8,128)(2,1)S(1)} %copy-done.1, bf16[512,1024]{1,0:T(8,128)(2,1)S(1)} %convolution_convert_fusion.5.g_ref, f32[512,1024]{1,0:T(8,128)S(1)} %copy-done.6), custom_call_target="tpu_custom_call" | custom-call | flops 512 | bytes 512 | tf_op jit(solution)/shard_map/attn_bwd/pallas_call | solution.py:150
  362.7 5.1 fusion.8
  368.6 2.6 convolution_convert_fusion.2
  371.3 5.5 convolution_convert_fusion
  376.7 132.5 %gradient_sums.1 = (bf16[128,3072]{1,0:T(8,128)(2,1)}, bf16[128,1024]{1,0:T(8,128)(2,1)}, bf16[128,4096]{1,0:T(8,128)(2,1)}, bf16[4,128,1024]{2,1,0:T(8,128)(2,1)}, f32[8,1024]{1,0:T(8,128)}) custom-call(f32[8,1024]{1,0:T(8,128)} %select_maximum_fusion.small_ref, bf16[4,2,128,3072]{3,2,1,0:T(8,128)(2,1)} %bitcast.60, bf16[4,2,128,1024]{3,2,1,0:T(8,128)(2,1)} %bitcast.64, ...), custom_call_target="tpu_custom_call" | custom-call | flops 62914560 | bytes 50331648 | tf_op jit(solution)/shard_map/gradient_sums/pallas_call | solution.py:890
  509.2 4.4 add_convert_fusion
  513.6 3.8 all-to-all-start.1
  517.4 8.9 %broadcast_multiply_fusion = (f32[1024,1024]{1,0:T(8,128)}, f32[1024,1024]{1,0:T(8,128)}) fusion(f32[1024,1024]{1,0:T(8,128)} %get-tuple-element.101, f32[]{:T(128)} %bitcast.32, f32[1024,1024]{1,0:T(8,128)} %get-tuple-element.80), kind=kLoop, calls=%fused_computation.25 | loop fusion | flops 2097152 | bytes 16777220 | tf_op jit(solution)/shard_map/mul | solution.py:1176
  527.6 2.0 fusion.11
  531.8 1.5 convert_element_type.128
  533.3 1.6 convert_element_type.129
  535.7 3.6 add_convert_fusion.1
  (127 shorter events, 31.2 us)
Async XLA Ops:
  12.1 5.4 copy-start.11
  12.1 6.0 %copy-start.30 = (f32[1024]{0:T(1024)S(1)}, f32[1024]{0:T(1024)}, u32[]{:S(2)}) copy-start(f32[1024]{0:T(1024)} %param.16) | copy-start | bytes 12292
  12.1 23.5 %all-to-all-start = ((bf16[8,80,1024]{2,1,0:T(8,128)(2,1)}), bf16[8,80,1024]{2,1,0:T(8,128)(2,1)S(1)}, u32[]{:S(2)}, u32[]{:S(2)}) async-start(bf16[8,80,1024]{2,1,0:T(8,128)(2,1)} %bitcast.67), calls=%async_computation | async-start | bytes 2621440 | tf_op jit(solution)/shard_map/all_to_all | solution.py:1029
  17.5 63.3 %all-gather.5.cloned.1.call-start = ((), (), s32[]{:S(2)}) async-start(), calls=%async_computation.2 | async-start | bytes 7077888 | tf_op jit(solution)/shard_map/all_gather | solution.py:1028
  19.5 52.8 %copy-start.28 = (bf16[1024,2]{0,1:T(2,128)(2,1)S(1)}, bf16[1024,2]{0,1:T(2,128)(2,1)}, u32[]{:S(2)}) copy-start(bf16[1024,2]{0,1:T(2,128)(2,1)} %param.22) | copy-start | bytes 12292
  35.7 51.7 %copy-start.20 = (bf16[8,80,1024]{2,1,0:T(8,128)(2,1)}, bf16[8,80,1024]{2,1,0:T(8,128)(2,1)S(1)}, u32[]{:S(2)}) copy-start(bf16[8,80,1024]{2,1,0:T(8,128)(2,1)S(1)} %all-to-all-done) | copy-start | bytes 3932164
  35.7 88.6 %all-gather.7.cloned.1.call-start = ((), (), s32[]{:S(2)}) async-start(), calls=%async_computation.3 | async-start | bytes 2359296 | tf_op jit(solution)/shard_map/all_gather | solution.py:1028
  36.4 261.3 %all-gather.9.cloned.1.call-start = ((), (), s32[]{:S(2)}) async-start(), calls=%async_computation.4 | async-start | bytes 9437184 | tf_op jit(solution)/shard_map/all_gather | solution.py:1028
  37.2 260.6 %all-gather.11.cloned.1.call-start = ((), (), s32[]{:S(2)}) async-start(), calls=%async_computation.5 | async-start | bytes 9437184 | tf_op jit(solution)/shard_map/all_gather | solution.py:1028
  37.8 29.7 %collective-permute-start.1 = (bf16[640,1024]{1,0:T(8,128)(2,1)S(1)}, bf16[640,1024]{1,0:T(8,128)(2,1)}, u32[]{:S(2)}, u32[]{:S(2)}) collective-permute-start(bf16[640,1024]{1,0:T(8,128)(2,1)S(1)} %bitcast.65), channel_id=1, source_target_pairs={{8,0},{16,8},{24,16},{9,1},{17,9},{25,17},{10,2},{18,10},{26,18},{... | collective-permute-start | bytes 3932168 | tf_op jit(solution)/shard_map/ppermute | solution.py:947
  39.1 29.5 %collective-permute-start = (bf16[640,1024]{1,0:T(8,128)(2,1)S(1)}, bf16[640,1024]{1,0:T(8,128)(2,1)}, u32[]{:S(2)}, u32[]{:S(2)}) collective-permute-start(bf16[640,1024]{1,0:T(8,128)(2,1)S(1)} %bitcast.66), channel_id=1, source_target_pairs={{0,8},{8,16},{16,24},{1,9},{9,17},{17,25},{2,10},{10,18},{18,26},{... | collective-permute-start | bytes 3932168 | tf_op jit(solution)/shard_map/ppermute | solution.py:947
  68.6 18.8 %collective-permute-start.2 = (bf16[640,1024]{1,0:T(8,128)(2,1)}, bf16[640,1024]{1,0:T(8,128)(2,1)}, u32[]{:S(2)}, u32[]{:S(2)}) collective-permute-start(bf16[640,1024]{1,0:T(8,128)(2,1)} %collective-permute-done), channel_id=1, source_target_pairs={{8,16},{16,24},{9,17},{17,25},{10,18},{18,26},{11,19},{19,27},{12,... | collective-permute-start | bytes 3932168 | tf_op jit(solution)/shard_map/ppermute | solution.py:947
  70.3 32.2 %collective-permute-start.3 = (bf16[640,1024]{1,0:T(8,128)(2,1)}, bf16[640,1024]{1,0:T(8,128)(2,1)}, u32[]{:S(2)}, u32[]{:S(2)}) collective-permute-start(bf16[640,1024]{1,0:T(8,128)(2,1)} %collective-permute-done.1), channel_id=1, source_target_pairs={{8,0},{16,8},{9,1},{17,9},{10,2},{18,10},{11,3},{19,11},{12,4},{20... | collective-permute-start | bytes 3932168 | tf_op jit(solution)/shard_map/ppermute | solution.py:947
  102.5 30.3 %collective-permute-start.4 = (bf16[640,1024]{1,0:T(8,128)(2,1)}, bf16[640,1024]{1,0:T(8,128)(2,1)}, u32[]{:S(2)}, u32[]{:S(2)}) collective-permute-start(bf16[640,1024]{1,0:T(8,128)(2,1)} %collective-permute-done.2), channel_id=1, source_target_pairs={{16,24},{17,25},{18,26},{19,27},{20,28},{21,29},{22,30},{23,31}} | collective-permute-start | bytes 3932168 | tf_op jit(solution)/shard_map/ppermute | solution.py:947
  104.2 28.6 %collective-permute-start.5 = (bf16[640,1024]{1,0:T(8,128)(2,1)}, bf16[640,1024]{1,0:T(8,128)(2,1)}, u32[]{:S(2)}, u32[]{:S(2)}) collective-permute-start(bf16[640,1024]{1,0:T(8,128)(2,1)} %collective-permute-done.3), channel_id=1, source_target_pairs={{8,0},{9,1},{10,2},{11,3},{12,4},{13,5},{14,6},{15,7}} | collective-permute-start | bytes 3932168 | tf_op jit(solution)/shard_map/ppermute | solution.py:947
  124.3 3.3 copy-start.7
  291.2 218.0 %collective-permute-start.6 = (bf16[640,1024]{1,0:T(8,128)(2,1)}, bf16[640,1024]{1,0:T(8,128)(2,1)}, u32[]{:S(2)}, u32[]{:S(2)}) collective-permute-start(bf16[640,1024]{1,0:T(8,128)(2,1)} %bitcast.95), channel_id=1, source_target_pairs={{24,0},{0,8},{8,16},{16,24},{25,1},{1,9},{9,17},{17,25},{26,2},{2,... | collective-permute-start | bytes 3932168 | tf_op jit(solution)/shard_map/ppermute | solution.py:975
  293.1 216.1 %collective-permute-start.7 = (bf16[640,1024]{1,0:T(8,128)(2,1)}, bf16[640,1024]{1,0:T(8,128)(2,1)}, u32[]{:S(2)}, u32[]{:S(2)}) collective-permute-start(bf16[640,1024]{1,0:T(8,128)(2,1)} %bitcast.94), channel_id=1, source_target_pairs={{16,0},{24,8},{0,16},{8,24},{17,1},{25,9},{1,17},{9,25},{18,2},{26... | collective-permute-start | bytes 3932168 | tf_op jit(solution)/shard_map/ppermute | solution.py:975
  294.1 215.1 %collective-permute-start.8 = (bf16[640,1024]{1,0:T(8,128)(2,1)}, bf16[640,1024]{1,0:T(8,128)(2,1)}, u32[]{:S(2)}, u32[]{:S(2)}) collective-permute-start(bf16[640,1024]{1,0:T(8,128)(2,1)} %bitcast.93), channel_id=1, source_target_pairs={{8,0},{16,8},{24,16},{0,24},{9,1},{17,9},{25,17},{1,25},{10,2},{18... | collective-permute-start | bytes 3932168 | tf_op jit(solution)/shard_map/ppermute | solution.py:975
  299.0 35.2 %copy-start.15 = (bf16[512,1024]{1,0:T(8,128)(2,1)S(1)}, bf16[512,1024]{1,0:T(8,128)(2,1)}, u32[]{:S(2)}) copy-start(bf16[512,1024]{1,0:T(8,128)(2,1)} %param.25) | copy-start | bytes 3145732
  299.0 36.6 %copy-start.22 = (bf16[8,80,1024]{2,1,0:T(8,128)(2,1)S(1)}, bf16[8,80,1024]{2,1,0:T(8,128)(2,1)}, u32[]{:S(2)}) copy-start(bf16[8,80,1024]{2,1,0:T(8,128)(2,1)} %get-tuple-element.83) | copy-start | bytes 3932164
  340.4 28.3 %copy-start.16 = (f32[512,1024]{1,0:T(8,128)}, f32[512,1024]{1,0:T(8,128)S(1)}, u32[]{:S(2)}) copy-start(f32[512,1024]{1,0:T(8,128)S(1)} %convert_add_fusion) | copy-start | bytes 6291460
  340.4 22.2 %slice-start = ((s8[6291456]{0:T(1024)(128)(4,1)}), s8[4194304]{0:T(1024)(128)(4,1)S(1)}, s32[]{:S(2)}) async-start(s8[6291456]{0:T(1024)(128)(4,1)} %bitcast.89), calls=%async_computation.6 | async-start | bytes 8388608
  343.7 19.0 %copy-start.12 = (bf16[512,1024]{1,0:T(8,128)(2,1)S(1)}, bf16[512,1024]{1,0:T(8,128)(2,1)}, u32[]{:S(2)}) copy-start(bf16[512,1024]{1,0:T(8,128)(2,1)} %param.13) | copy-start | bytes 3145732
  343.7 19.0 %slice-start.1 = ((s8[6291456]{0:T(1024)(128)(4,1)}), s8[2097152]{0:T(1024)(128)(4,1)S(1)}, s32[]{:S(2)}) async-start(s8[6291456]{0:T(1024)(128)(4,1)} %bitcast.89), calls=%async_computation.7 | async-start | bytes 4194304
  362.7 6.0 %copy-start.8 = (bf16[512,1024]{1,0:T(8,128)(2,1)S(1)}, bf16[512,1024]{1,0:T(8,128)(2,1)}, u32[]{:S(2)}) copy-start(bf16[512,1024]{1,0:T(8,128)(2,1)} %copy-done.7) | copy-start | bytes 3145732
  376.7 132.5 %copy-start.21 = (bf16[8,80,1024]{2,1,0:T(8,128)(2,1)S(1)}, bf16[8,80,1024]{2,1,0:T(8,128)(2,1)}, u32[]{:S(2)}) copy-start(bf16[8,80,1024]{2,1,0:T(8,128)(2,1)} %get-tuple-element.91) | copy-start | bytes 3932164
  513.6 21.9 %all-to-all-start.1 = ((bf16[8,80,1024]{2,1,0:T(8,128)(2,1)}), bf16[8,80,1024]{2,1,0:T(8,128)(2,1)S(1)}, u32[]{:S(2)}, u32[]{:S(2)}) async-start(bf16[8,80,1024]{2,1,0:T(8,128)(2,1)} %bitcast.31), calls=%async_computation.1 | async-start | bytes 2621440 | tf_op jit(solution)/shard_map/all_to_all | solution.py:1167
  517.4 9.0 %copy-start.31 = (f32[8,1024]{1,0:T(8,128)S(1)}, f32[8,1024]{1,0:T(8,128)}, u32[]{:S(2)}) copy-start(f32[8,1024]{1,0:T(8,128)} %get-tuple-element.95) | copy-start | bytes 98308
  517.4 10.2 %copy-start.13 = (bf16[512,1024]{1,0:T(8,128)(2,1)S(1)}, bf16[512,1024]{1,0:T(8,128)(2,1)}, u32[]{:S(2)}) copy-start(bf16[512,1024]{1,0:T(8,128)(2,1)} %param.13) | copy-start | bytes 3145732
  517.4 10.2 %copy-start.17 = (f32[512,1024]{1,0:T(8,128)S(1)}, f32[512,1024]{1,0:T(8,128)}, u32[]{:S(2)}) copy-start(f32[512,1024]{1,0:T(8,128)} %copy-done.16) | copy-start | bytes 6291460
  517.4 10.1 %copy-start.18 = (f32[512,1024]{1,0:T(8,128)S(1)}, f32[512,1024]{1,0:T(8,128)}, u32[]{:S(2)}) copy-start(f32[512,1024]{1,0:T(8,128)} %get-tuple-element.126) | copy-start | bytes 6291460
  (18 other events, 35.3 us)
Sparse Core Ops, SparseCore 0:
  35.8 44.9 all-gather.4
  82.7 27.8 all-gather.6
  112.5 68.4 all-gather.8
  182.7 56.6 all-gather.10

commit v7 on v6

--- a/solution.py
+++ b/solution.py
@@ -923,6 +923,87 @@
     return (*outs[: len(columns)], *rows_out, outs[-1])
 
 
+def spread_kernel(layers, groups, slots_ref, own_ref, low_ref, high_ref, a_send, a_recv, z_send, z_recv):
+    last = layers - 1
+    here, me = lax.axis_index("dp"), lax.axis_index("ep")
+    peer = lambda j: lax.rem(me + j, groups)
+    source = lambda j: lax.rem(me + groups - j, groups)
+    up_id, down_id = lax.rem(here + 1, layers), lax.rem(here + last, layers)
+    mesh_id = pl.DeviceIdType.MESH
+
+    def a_copy(j):
+        return pltpu.make_async_remote_copy(
+            slots_ref.at[peer(j)], own_ref.at[me], a_send.at[j], a_recv.at[j],
+            device_id={"ep": peer(j)}, device_id_type=mesh_id,
+        )
+
+    def z_copy(j, way):
+        block = own_ref.at[source(j)]
+        return pltpu.make_async_remote_copy(
+            block, (low_ref, high_ref)[way].at[source(j)], z_send.at[j, way], z_recv.at[j, way],
+            device_id={"dp": up_id if way == 0 else down_id}, device_id_type=mesh_id,
+        )
+
+    def over(first, count, act):
+        def step(j, carry):
+            act(j)
+            return carry
+
+        lax.fori_loop(first, count, step, 0)
+
+    barrier = pltpu.get_barrier_semaphore()
+
+    def greet(where):
+        pl.semaphore_signal(barrier, inc=1, device_id=where, device_id_type=mesh_id)
+
+    over(1, groups, lambda j: greet({"ep": peer(j)}))
+    pl.when(here < last)(lambda: greet({"dp": up_id}))
+    pl.when(here > 0)(lambda: greet({"dp": down_id}))
+    pl.semaphore_wait(barrier, groups - 1 + jnp.where(here < last, 1, 0) + jnp.where(here > 0, 1, 0))
+
+    over(1, groups, lambda j: a_copy(j).start())
+    own_ref[me] = slots_ref[me]
+
+    def pass_on(j):
+        pl.when(here < last)(lambda: z_copy(j, 0).start())
+        pl.when(here > 0)(lambda: z_copy(j, 1).start())
+
+    pass_on(0)
+
+    def arrived(j):
+        a_copy(j).wait_recv()
+        pass_on(j)
+
+    over(1, groups, arrived)
+
+    def settle(j):
+        pl.when(here > 0)(lambda: z_copy(j, 0).wait_recv())
+        pl.when(here < last)(lambda: z_copy(j, 1).wait_recv())
+        pl.when(here < last)(lambda: z_copy(j, 0).wait_send())
+        pl.when(here > 0)(lambda: z_copy(j, 1).wait_send())
+
+    over(0, groups, settle)
+    over(1, groups, lambda j: a_copy(j).wait_send())
+
+
+def spread(slots):
+    layers, groups = lax.axis_size("dp"), lax.axis_size("ep")
+    vmem = pl.BlockSpec(memory_space=pltpu.VMEM)
+    sem = pltpu.SemaphoreType.DMA
+    return pl.pallas_call(
+        functools.partial(spread_kernel, layers, groups),
+        in_specs=[vmem],
+        out_specs=[vmem] * 3,
+        out_shape=[jax.ShapeDtypeStruct(slots.shape, BF16)] * 3,
+        scratch_shapes=[sem((groups,)), sem((groups,)), sem((groups, 2)), sem((groups, 2))],
+        compiler_params=pltpu.CompilerParams(
+            collective_id=2, has_side_effects=True, vmem_limit_bytes=16 << 20
+        ),
+        cost_estimate=cost(slots.size, 4 * slots.size),
+        name="spread",
+    )(slots)
+
+
 def normalise(values_in):
     centred = values_in - jnp.mean(values_in, axis=-1, keepdims=True)
     inverse = lax.rsqrt(jnp.mean(centred * centred, axis=-1, keepdims=True) + 1e-05)
@@ -1046,15 +1127,20 @@
     token_rows = tokens.astype(F32)
     unit1, inverse1 = normalise(token_rows)
     normed_in = (unit1 * ln1_gain).astype(BF16)
-    g_own = exchange_out(pick(cotangent)).reshape(slots, width)
-    normed_in, g_own, qkv_weight = lax.optimization_barrier((normed_in, g_own, qkv_weight))
     qkv_full, out_full, up_full, down_full = (
         gather(qkv_weight),
         gather(out_weight),
         gather(up_weight),
         gather(down_weight),
     )
-    g_low, g_high = [g_own], [g_own]
+    by_kernels = capacity % 16 == 0
+    if by_kernels:
+        g_own, *g_first = [a.reshape(slots, width) for a in spread(pick(cotangent))]
+        g_low, g_high = [g_own, g_first[0]], [g_own, g_first[1]]
+    else:
+        g_own = exchange_out(pick(cotangent)).reshape(slots, width)
+        low, high = both_hops(g_own, g_own, 1)
+        g_low, g_high = [g_own, low], [g_own, high]
 
     def step(lows, highs, *others):
         stage = len(lows)
@@ -1066,7 +1152,6 @@
             highs.append(high)
         return held[2:]
 
-    step(g_low, g_high)
     (normed_in,) = step(g_low, g_high, normed_in)
     qkv_rows = dot_nn(normed_in, qkv_full).astype(BF16)
     (qkv_rows,) = step(g_low, g_high, qkv_rows)
@@ -1091,7 +1176,7 @@
             acc = acc + part.astype(F32)
         return acc
 
-    if capacity % 16 == 0:
+    if by_kernels:
         blocks = lambda many: [g.reshape(groups, capacity, width) for g in many]
         returned, slab, partial_outs, expert_up_grad, expert_down_grad = expert_exchange(
             mid_slots, blocks(g_low), blocks(g_high), mix_pad, expert_up2, expert_down2

time: 555 us -> 531 us (0.957)
  waiting for transfers between devices: 65.3 us -> 28.3 us
  Pallas kernels: 360 us -> 385 us
  starting transfers between devices: 28.3 us -> 18.3 us
    pallas_call x0 -> x1, Pallas kernels: none -> 33 us  [spread(): pl.pallas_call(functools.partial(spread_kernel, layers, groups), in_specs...]
    ppermute x6 -> x4, waiting for transfers between devices: 39 us -> 11.2 us  [hop(): return lax.ppermute(rows, 'dp', pairs)]
    all_to_all x1 -> x0, waiting for transfers between devices: 16.2 us -> none  [on_device(): lax.all_to_all(a, 'ep', split_axis=0, concat_axis=1, tiled=True)]
    pallas_call x1, Pallas kernels: 158 us -> 149 us  [expert_exchange(): pl.pallas_call(functools.partial(exchange_kernel, waves, layers, groups),...]
    ppermute x6 -> x4, starting transfers between devices: 13 us -> 6.08 us  [hop(): return lax.ppermute(rows, 'dp', pairs)]
    all_gather x4, waiting for transfers between devices: 7.56 us -> 13.9 us  [on_device(): gather = lambda w: lax.all_gather(w, 'ep', axis=0, tiled=True)]
    unnamed x71 -> x81, local copies, waits for them, and re-layouts: 10.4 us -> 11.5 us
  transfers between devices with their start and end apart: 15 -> 12, of which waited for: 6 -> 4; matrix products, arithmetic and copies ran while one was open for 10% -> 11% of each run, Pallas kernels for 66% -> 74%
where the time goes in v7:
time: 531 us; the launch traced here: 522 us
  Pallas kernels  385 us (73%)
  matrix products  34.2 us (6%)
  waiting for transfers between devices  28.3 us (5%)
  other arithmetic  27.3 us (5%)
  starting transfers between devices  18.3 us (3%)
  between operations  15.1 us (3%)
  local copies, waits for them, and re-layouts  13.6 us (3%)
    pallas_call x1, Pallas kernels, expert_exchange(): pl.pallas_call(functools.partial(exchange_kernel, waves, layers, groups),...  149 us
    pallas_call x1, Pallas kernels, gradient_sums(): pl.pallas_call(functools.partial(sums_kernel, plan, split, layers, groups...  133 us
    pallas_call x1, Pallas kernels, dense_branch(): pl.pallas_call(dense_kernel, grid=(ff // tile,), in_specs=[whole, whole,...  35.2 us
    pallas_call x1, Pallas kernels, spread(): pl.pallas_call(functools.partial(spread_kernel, layers, groups), in_specs...  33 us
    pallas_call x1, Pallas kernels, attention_backward(): pl.pallas_call(functools.partial(attn_bwd_kernel, tile), grid=(pairs,), i...  18.9 us
    dot_general x6, matrix products, dot_nn(): lax.dot_general(a, b, (((1,), (0,)), ((), ())), preferred_element_type=F32)  16 us
    pallas_call x1, Pallas kernels, attention_forward(): pl.pallas_call(functools.partial(attn_fwd_kernel, tile), grid=(pairs,), i...  15.8 us
    all_gather x4, waiting for transfers between devices, on_device(): gather = lambda w: lax.all_gather(w, 'ep', axis=0, tiled=True)  13.9 us
  transfers between devices with their start and end apart: 12, of which 4 were waited for; matrix products, arithmetic and copies ran while one was open for 11% of the time, Pallas kernels for 74%

profile of v7, /device:TPU:0, one launch (start us, length us, event | category | flops | bytes accessed | tf_op | source)
XLA Modules:
  0.0 522.2 jit_solution(18161846393588262802)
XLA Ops:
  11.3 33.0 %spread.1 = (bf16[8,80,1024]{2,1,0:T(8,128)(2,1)S(1)}, bf16[8,80,1024]{2,1,0:T(8,128)(2,1)S(1)}, bf16[8,80,1024]{2,1,0:T(8,128)(2,1)S(1)}) custom-call(bf16[8,80,1024]{2,1,0:T(8,128)(2,1)S(1)} %bitcast.58), custom_call_target="tpu_custom_call" | custom-call | flops 655360 | bytes 2621440 | tf_op jit(solution)/shard_map/spread/pallas_call | solution.py:993
  46.0 1.4 fusion.6
  47.4 1.8 collective-permute-start
  52.1 13.9 %all-gather.5.cloned.1.call-done = bf16[1024,3072]{1,0:T(8,128)(2,1)} async-done(((bf16[128,3072]{1,0:T(8,128)(2,1)}), bf16[1024,3072]{1,0:T(8,128)(2,1)}) %all-gather.5.cloned.1.call-update) | async-done | bytes 6291472 | tf_op jit(solution)/shard_map/all_gather | solution.py:1109
  65.9 6.5 %convolution_convert_fusion.1.q_ref.k_ref.v_ref = bf16[512,3072]{1,0:T(8,128)(2,1)S(1)} fusion(bf16[512,1024]{1,0:T(8,128)(2,1)} %fusion.6, bf16[1024,3072]{1,0:T(8,128)(2,1)} %all-gather.5.cloned.1.call-done), kind=kOutput, calls=%fused_computation.1 | convolution fusion | flops 3222798336 | bytes 10485760 | tf_op jit(solution)/shard_map/dot_general | solution.py:23
  72.5 9.3 %collective-permute-done.1 = bf16[640,1024]{1,0:T(8,128)(2,1)} collective-permute-done((bf16[640,1024]{1,0:T(8,128)(2,1)S(1)}, bf16[640,1024]{1,0:T(8,128)(2,1)}, u32[]{:S(2)}, u32[]{:S(2)}) %collective-permute-start.1) | collective-permute-done | bytes 1310752 | tf_op jit(solution)/shard_map/ppermute | solution.py:1028
  81.8 1.8 collective-permute-start.2
  84.8 15.8 %attn_fwd.1 = (bf16[512,1024]{1,0:T(8,128)(2,1)S(1)}, f32[512,1024]{1,0:T(8,128)S(1)}) custom-call(s32[1]{0:T(128)S(6)} %copy.26.flag_ref, bf16[512,3072]{1,0:T(8,128)(2,1)S(1)} %convolution_convert_fusion.1.q_ref.k_ref.v_ref, bf16[512,3072]{1,0:T(8,128)(2,1)S(1)} %convolution_convert_fusion.1.q_ref.k_ref.v_ref, ...), custom_call_target="tpu_custom_call" | custom-call | flops 2147483648 | bytes 5242880 | tf_op jit(solution)/shard_map/attn_fwd/pallas_call | solution.py:87
  100.7 1.7 copy-done
  102.3 1.3 copy-done.5
  103.6 3.6 fusion.27
  110.4 2.0 convolution_convert_fusion.3
  112.4 1.9 collective-permute-done.3
  114.3 149.4 %expert_exchange.1 = (bf16[8,80,1024]{2,1,0:T(8,128)(2,1)}, bf16[8,16,128]{2,1,0:T(8,128)(2,1)}, bf16[8,80,1024]{2,1,0:T(8,128)(2,1)}, bf16[8,80,1024]{2,1,0:T(8...) custom-call(bf16[8,80,1024]{2,1,0:T(8,128)(2,1)} %bitcast.96, ...), custom_call_target="tpu_custom_call" | custom-call | flops 32212254720 | bytes 52428800 | tf_op jit(solution)/shard_map/expert_exchange/pallas_call | solution.py:595
  264.6 5.5 %collective-permute-start.4 = (bf16[640,1024]{1,0:T(8,128)(2,1)}, bf16[640,1024]{1,0:T(8,128)(2,1)}, u32[]{:S(2)}, u32[]{:S(2)}) collective-permute-start(bf16[640,1024]{1,0:T(8,128)(2,1)} %bitcast.95), channel_id=1, source_target_pairs={{24,0},{0,8},{8,16},{16,24},{25,1},{1,9},{9,17},{17,25},{26,2},{2,... | collective-permute-start | bytes 3932168 | tf_op jit(solution)/shard_map/ppermute | solution.py:1056
  270.1 2.8 collective-permute-start.6
  274.5 35.2 %dense_branch.1 = (f32[512,1024]{1,0:T(8,128)S(1)}, f32[512,1024]{1,0:T(8,128)}, bf16[1024,4096]{1,0:T(8,128)(2,1)}, bf16[4096,1024]{1,0:T(8,128)(2,1)}) custom-call(bf16[512,1024]{1,0:T(8,128)(2,1)S(1)} %multiply_convert_fusion.mid_ref, bf16[512,1024]{1,0:T(8,128)(2,1)S(1)} %copy-done.4, bf16[1024,4096]{1,0:T(8,128)(2,1)} %all-gather.9.cloned.1.call-done.up_ref, ...), custom_call_target="tpu_custom_call" | custom-call | flops 512 | bytes 512 | tf_op jit(solution)/shard_map/dense_branch/pallas_call | solution.py:199
  312.7 1.6 multiply_reduce_fusion.1
  317.2 1.3 copy-done.1
  319.2 18.9 %attn_bwd.1 = bf16[512,3072]{1,0:T(8,128)(2,1)S(1)} custom-call(s32[1]{0:T(128)S(6)} %copy.26.flag_ref, bf16[512,3072]{1,0:T(8,128)(2,1)S(1)} %copy-done.1, bf16[512,3072]{1,0:T(8,128)(2,1)S(1)} %copy-done.1, bf16[512,3072]{1,0:T(8,128)(2,1)S(1)} %copy-done.1, bf16[512,1024]{1,0:T(8,128)(2,1)S(1)} %convolution_convert_fusion.5.g_ref, f32[512,1024]{1,0:T(8,128)S(1)} %copy-done.6), custom_call_target="tpu_custom_call" | custom-call | flops 512 | bytes 512 | tf_op jit(solution)/shard_map/attn_bwd/pallas_call | solution.py:150
  338.2 5.1 fusion.8
  344.2 2.6 convolution_convert_fusion.2
  346.8 5.5 %convolution_convert_fusion = bf16[1024,3072]{1,0:T(8,128)(2,1)} fusion(bf16[512,1024]{1,0:T(8,128)(2,1)S(1)} %copy-done.29, bf16[512,3072]{1,0:T(8,128)(2,1)S(1)} %attn_bwd.1), kind=kOutput, calls=%fused_computation | convolution fusion | flops 3224371200 | bytes 10485760 | tf_op jit(solution)/shard_map/dot_general | solution.py:31
  352.3 133.1 %gradient_sums.1 = (bf16[128,3072]{1,0:T(8,128)(2,1)}, bf16[128,1024]{1,0:T(8,128)(2,1)}, bf16[128,4096]{1,0:T(8,128)(2,1)}, bf16[4,128,1024]{2,1,0:T(8,128)(2,1)}, f32[8,1024]{1,0:T(8,128)}) custom-call(f32[8,1024]{1,0:T(8,128)} %select_maximum_fusion.small_ref, bf16[4,2,128,3072]{3,2,1,0:T(8,128)(2,1)} %bitcast.63, bf16[4,2,128,1024]{3,2,1,0:T(8,128)(2,1)} %bitcast.67, ...), custom_call_target="tpu_custom_call" | custom-call | flops 62914560 | bytes 50331648 | tf_op jit(solution)/shard_map/gradient_sums/pallas_call | solution.py:890
  485.5 4.4 add_convert_fusion
  489.8 3.8 all-to-all-start
  493.7 8.8 %broadcast_multiply_fusion = (f32[1024,1024]{1,0:T(8,128)}, f32[1024,1024]{1,0:T(8,128)}) fusion(f32[1024,1024]{1,0:T(8,128)} %get-tuple-element.97, f32[]{:T(128)} %bitcast.32, f32[1024,1024]{1,0:T(8,128)} %get-tuple-element.76), kind=kLoop, calls=%fused_computation.25 | loop fusion | flops 2097152 | bytes 16777220 | tf_op jit(solution)/shard_map/mul | solution.py:1261
  503.4 1.3 convert_element_type.126
  504.7 1.5 convert_element_type.128
  506.2 1.6 convert_element_type.129
  509.2 2.0 fusion.11
  511.8 3.6 add_convert_fusion.1
  (132 shorter events, 25.1 us)
Async XLA Ops:
  7.2 3.1 copy-start.18
  7.2 58.7 %all-gather.5.cloned.1.call-start = ((), (), s32[]{:S(2)}) async-start(), calls=%async_computation.1 | async-start | bytes 7077888 | tf_op jit(solution)/shard_map/all_gather | solution.py:1109
  7.9 95.7 %all-gather.7.cloned.1.call-start = ((), (), s32[]{:S(2)}) async-start(), calls=%async_computation.2 | async-start | bytes 2359296 | tf_op jit(solution)/shard_map/all_gather | solution.py:1109
  8.7 264.6 %all-gather.9.cloned.1.call-start = ((), (), s32[]{:S(2)}) async-start(), calls=%async_computation.3 | async-start | bytes 9437184 | tf_op jit(solution)/shard_map/all_gather | solution.py:1109
  9.4 263.9 %all-gather.11.cloned.1.call-start = ((), (), s32[]{:S(2)}) async-start(), calls=%async_computation.4 | async-start | bytes 9437184 | tf_op jit(solution)/shard_map/all_gather | solution.py:1109
  10.3 35.1 %copy-start.14 = (bf16[512,1024]{1,0:T(8,128)(2,1)S(1)}, bf16[512,1024]{1,0:T(8,128)(2,1)}, u32[]{:S(2)}) copy-start(bf16[512,1024]{1,0:T(8,128)(2,1)} %param.13) | copy-start | bytes 3145732
  11.3 34.7 %copy-start.34 = (f32[1024]{0:T(1024)S(1)}, f32[1024]{0:T(1024)}, u32[]{:S(2)}) copy-start(f32[1024]{0:T(1024)} %param.16) | copy-start | bytes 12292
  45.4 3.8 copy-start.9
  45.4 5.7 %copy-start.32 = (bf16[1024,2]{0,1:T(2,128)(2,1)S(1)}, bf16[1024,2]{0,1:T(2,128)(2,1)}, u32[]{:S(2)}) copy-start(bf16[1024,2]{0,1:T(2,128)(2,1)} %param.22) | copy-start | bytes 12292
  47.4 25.1 %collective-permute-start = (bf16[640,1024]{1,0:T(8,128)(2,1)S(1)}, bf16[640,1024]{1,0:T(8,128)(2,1)}, u32[]{:S(2)}, u32[]{:S(2)}) collective-permute-start(bf16[640,1024]{1,0:T(8,128)(2,1)S(1)} %bitcast.59), channel_id=1, source_target_pairs={{8,16},{16,24},{9,17},{17,25},{10,18},{18,26},{11,19},{19,27},{12,... | collective-permute-start | bytes 3932168 | tf_op jit(solution)/shard_map/ppermute | solution.py:1028
  49.2 32.6 %collective-permute-start.1 = (bf16[640,1024]{1,0:T(8,128)(2,1)S(1)}, bf16[640,1024]{1,0:T(8,128)(2,1)}, u32[]{:S(2)}, u32[]{:S(2)}) collective-permute-start(bf16[640,1024]{1,0:T(8,128)(2,1)S(1)} %bitcast.60), channel_id=1, source_target_pairs={{8,0},{16,8},{9,1},{17,9},{10,2},{18,10},{11,3},{19,11},{12,4},{20... | collective-permute-start | bytes 3932168 | tf_op jit(solution)/shard_map/ppermute | solution.py:1028
  72.5 31.2 %copy-start.15 = (bf16[512,1024]{1,0:T(8,128)(2,1)S(1)}, bf16[512,1024]{1,0:T(8,128)(2,1)}, u32[]{:S(2)}) copy-start(bf16[512,1024]{1,0:T(8,128)(2,1)} %param.13) | copy-start | bytes 3145732
  81.8 30.6 %collective-permute-start.2 = (bf16[640,1024]{1,0:T(8,128)(2,1)}, bf16[640,1024]{1,0:T(8,128)(2,1)}, u32[]{:S(2)}, u32[]{:S(2)}) collective-permute-start(bf16[640,1024]{1,0:T(8,128)(2,1)} %collective-permute-done), channel_id=1, source_target_pairs={{16,24},{17,25},{18,26},{19,27},{20,28},{21,29},{22,30},{23,31}} | collective-permute-start | bytes 3932168 | tf_op jit(solution)/shard_map/ppermute | solution.py:1028
  83.5 30.7 %collective-permute-start.3 = (bf16[640,1024]{1,0:T(8,128)(2,1)}, bf16[640,1024]{1,0:T(8,128)(2,1)}, u32[]{:S(2)}, u32[]{:S(2)}) collective-permute-start(bf16[640,1024]{1,0:T(8,128)(2,1)} %collective-permute-done.1), channel_id=1, source_target_pairs={{8,0},{9,1},{10,2},{11,3},{12,4},{13,5},{14,6},{15,7}} | collective-permute-start | bytes 3932168 | tf_op jit(solution)/shard_map/ppermute | solution.py:1028
  103.6 3.6 copy-start.10
  264.6 220.9 %collective-permute-start.4 = (bf16[640,1024]{1,0:T(8,128)(2,1)}, bf16[640,1024]{1,0:T(8,128)(2,1)}, u32[]{:S(2)}, u32[]{:S(2)}) collective-permute-start(bf16[640,1024]{1,0:T(8,128)(2,1)} %bitcast.95), channel_id=1, source_target_pairs={{24,0},{0,8},{8,16},{16,24},{25,1},{1,9},{9,17},{17,25},{26,2},{2,... | collective-permute-start | bytes 3932168 | tf_op jit(solution)/shard_map/ppermute | solution.py:1056
  270.1 215.4 %collective-permute-start.5 = (bf16[640,1024]{1,0:T(8,128)(2,1)}, bf16[640,1024]{1,0:T(8,128)(2,1)}, u32[]{:S(2)}, u32[]{:S(2)}) collective-permute-start(bf16[640,1024]{1,0:T(8,128)(2,1)} %bitcast.94), channel_id=1, source_target_pairs={{16,0},{24,8},{0,16},{8,24},{17,1},{25,9},{1,17},{9,25},{18,2},{26... | collective-permute-start | bytes 3932168 | tf_op jit(solution)/shard_map/ppermute | solution.py:1056
  270.1 215.4 %collective-permute-start.6 = (bf16[640,1024]{1,0:T(8,128)(2,1)}, bf16[640,1024]{1,0:T(8,128)(2,1)}, u32[]{:S(2)}, u32[]{:S(2)}) collective-permute-start(bf16[640,1024]{1,0:T(8,128)(2,1)} %bitcast.93), channel_id=1, source_target_pairs={{8,0},{16,8},{24,16},{0,24},{9,1},{17,9},{25,17},{1,25},{10,2},{18... | collective-permute-start | bytes 3932168 | tf_op jit(solution)/shard_map/ppermute | solution.py:1056
  274.5 35.2 %copy-start.20 = (bf16[512,1024]{1,0:T(8,128)(2,1)S(1)}, bf16[512,1024]{1,0:T(8,128)(2,1)}, u32[]{:S(2)}) copy-start(bf16[512,1024]{1,0:T(8,128)(2,1)} %param.25) | copy-start | bytes 3145732
  274.5 36.6 %copy-start.26 = (bf16[8,80,1024]{2,1,0:T(8,128)(2,1)S(1)}, bf16[8,80,1024]{2,1,0:T(8,128)(2,1)}, u32[]{:S(2)}) copy-start(bf16[8,80,1024]{2,1,0:T(8,128)(2,1)} %get-tuple-element.79) | copy-start | bytes 3932164
  315.9 28.2 %copy-start.21 = (f32[512,1024]{1,0:T(8,128)}, f32[512,1024]{1,0:T(8,128)S(1)}, u32[]{:S(2)}) copy-start(f32[512,1024]{1,0:T(8,128)S(1)} %convert_add_fusion) | copy-start | bytes 6291460
  315.9 3.3 copy-start.6
  315.9 22.2 %slice-start = ((s8[6291456]{0:T(1024)(128)(4,1)}), s8[4194304]{0:T(1024)(128)(4,1)S(1)}, s32[]{:S(2)}) async-start(s8[6291456]{0:T(1024)(128)(4,1)} %bitcast.89), calls=%async_computation.5 | async-start | bytes 8388608
  319.2 19.0 %copy-start.16 = (bf16[512,1024]{1,0:T(8,128)(2,1)S(1)}, bf16[512,1024]{1,0:T(8,128)(2,1)}, u32[]{:S(2)}) copy-start(bf16[512,1024]{1,0:T(8,128)(2,1)} %param.13) | copy-start | bytes 3145732
  319.2 19.0 %slice-start.1 = ((s8[6291456]{0:T(1024)(128)(4,1)}), s8[2097152]{0:T(1024)(128)(4,1)S(1)}, s32[]{:S(2)}) async-start(s8[6291456]{0:T(1024)(128)(4,1)} %bitcast.89), calls=%async_computation.6 | async-start | bytes 4194304
  338.2 6.0 %copy-start.11 = (bf16[512,1024]{1,0:T(8,128)(2,1)S(1)}, bf16[512,1024]{1,0:T(8,128)(2,1)}, u32[]{:S(2)}) copy-start(bf16[512,1024]{1,0:T(8,128)(2,1)} %copy-done.10) | copy-start | bytes 3145732
  352.3 133.2 %copy-start.25 = (bf16[8,80,1024]{2,1,0:T(8,128)(2,1)S(1)}, bf16[8,80,1024]{2,1,0:T(8,128)(2,1)}, u32[]{:S(2)}) copy-start(bf16[8,80,1024]{2,1,0:T(8,128)(2,1)} %get-tuple-element.87) | copy-start | bytes 3932164
  489.8 21.9 %all-to-all-start = ((bf16[8,80,1024]{2,1,0:T(8,128)(2,1)}), bf16[8,80,1024]{2,1,0:T(8,128)(2,1)S(1)}, u32[]{:S(2)}, u32[]{:S(2)}) async-start(bf16[8,80,1024]{2,1,0:T(8,128)(2,1)} %bitcast.31), calls=%async_computation | async-start | bytes 2621440 | tf_op jit(solution)/shard_map/all_to_all | solution.py:1252
  493.6 8.9 %copy-start.31 = (bf16[128,1024]{1,0:T(8,128)(2,1)S(1)}, bf16[128,1024]{1,0:T(8,128)(2,1)}, u32[]{:S(2)}) copy-start(bf16[128,1024]{1,0:T(8,128)(2,1)} %get-tuple-element.99) | copy-start | bytes 786436
  493.6 9.7 %copy-start.30 = (bf16[128,3072]{1,0:T(8,128)(2,1)S(1)}, bf16[128,3072]{1,0:T(8,128)(2,1)}, u32[]{:S(2)}) copy-start(bf16[128,3072]{1,0:T(8,128)(2,1)} %get-tuple-element.98) | copy-start | bytes 2359300
  504.7 3.1 copy-start.35
  504.7 4.3 copy-start.23
  (20 other events, 39.1 us)
Sparse Core Ops, SparseCore 0:
  9.9 55.9 all-gather.4
  67.8 27.9 all-gather.6
  97.7 68.4 all-gather.8
  167.9 56.3 all-gather.10

commit v8 on v7

--- a/solution.py
+++ b/solution.py
@@ -37,6 +37,13 @@
     half = 0.5 * (1.0 + t)
     slope = half + (0.5 * v) * (1.0 - t * t) * (ROOT + (3.0 * ROOT * CUBE) * sq)
     return v * half, slope
+
+
+def two_shares(first, second):
+    small = jnp.exp(-jnp.abs(second - first))
+    lead = 1.0 / (1.0 + small)
+    ahead = second >= first
+    return jnp.where(ahead, small * lead, lead), jnp.where(ahead, lead, small * lead)
 
 
 def params(vmem_mib):
@@ -80,7 +87,7 @@
         lse_ref[row0 : row0 + tile, :] = jnp.where(first, lses[0], lses[1])
 
 
-def attention_forward(qkv, flag, tile=256):
+def attention_forward(qkv, flag, tile=512):
     length, width = qkv.shape[0], qkv.shape[1] // 3
     pairs = width // PAIR
     spec = lambda off: pl.BlockSpec((length, PAIR), lambda j: (0, off + j))
@@ -217,7 +224,7 @@
     mid = mid_ref[...]
     g = g_ref[...].astype(F32)
     logits = dot_nn(mid, mix_ref[...])
-    share = 1.0 / (1.0 + jnp.exp(logits[:, 0:1] - logits[:, 1:2]))
+    share = two_shares(logits[:, 0:1], logits[:, 1:2])[1]
     eg = (share * g).astype(BF16)
     eg_ref[...] = eg
     act, slope = gelu_pair(dot_nn(mid, up_ref[...]))
@@ -432,7 +439,7 @@
             [g_refs[k, source(w * each + i)] for k in ks for i in range(each)], axis=0
         ).astype(F32)
         logits = dot_nn(mid, mix_ref[...])
-        share = 1.0 / (1.0 + jnp.exp(logits[:, 0:1] - logits[:, 1:2]))
+        share = two_shares(logits[:, 0:1], logits[:, 1:2])[1]
         eg = (share * g).astype(BF16)
         act, slope = gelu_pair(dot_nn(mid, up_ref[...]))
         act = act.astype(BF16)
@@ -923,7 +930,9 @@
     return (*outs[: len(columns)], *rows_out, outs[-1])
 
 
-def spread_kernel(layers, groups, slots_ref, own_ref, low_ref, high_ref, a_send, a_recv, z_send, z_recv):
+def spread_kernel(
+    layers, groups, slots_ref, own_ref, low_ref, high_ref, low_two, high_two, a_send, a_recv, z_send, z_recv
+):
     last = layers - 1
     here, me = lax.axis_index("dp"), lax.axis_index("ep")
     peer = lambda j: lax.rem(me + j, groups)
@@ -937,10 +946,12 @@
             device_id={"ep": peer(j)}, device_id_type=mesh_id,
         )
 
-    def z_copy(j, way):
-        block = own_ref.at[source(j)]
+    def z_copy(j, way, s=0):
+        src = (own_ref, (low_ref, high_ref)[way])[s]
+        dst = ((low_ref, high_ref), (low_two, high_two))[s][way]
+        n = 2 * s + way
         return pltpu.make_async_remote_copy(
-            block, (low_ref, high_ref)[way].at[source(j)], z_send.at[j, way], z_recv.at[j, way],
+            src.at[source(j)], dst.at[source(j)], z_send.at[j, n], z_recv.at[j, n],
             device_id={"dp": up_id if way == 0 else down_id}, device_id_type=mesh_id,
         )
 
@@ -970,15 +981,32 @@
 
     pass_on(0)
 
+    def forward(j):
+        pl.when(here > 0)(lambda: z_copy(j, 0).wait_recv())
+        pl.when(here < last)(lambda: z_copy(j, 1).wait_recv())
+
+        @pl.when(jnp.logical_and(here > 0, here < last))
+        def _():
+            z_copy(j, 0, 1).start()
+            z_copy(j, 1, 1).start()
+
     def arrived(j):
         a_copy(j).wait_recv()
         pass_on(j)
+        forward(j - 1)
 
     over(1, groups, arrived)
+    forward(groups - 1)
 
     def settle(j):
-        pl.when(here > 0)(lambda: z_copy(j, 0).wait_recv())
-        pl.when(here < last)(lambda: z_copy(j, 1).wait_recv())
+        pl.when(here > 1)(lambda: z_copy(j, 0, 1).wait_recv())
+        pl.when(here < last - 1)(lambda: z_copy(j, 1, 1).wait_recv())
+
+        @pl.when(jnp.logical_and(here > 0, here < last))
+        def _():
+            z_copy(j, 0, 1).wait_send()
+            z_copy(j, 1, 1).wait_send()
+
         pl.when(here < last)(lambda: z_copy(j, 0).wait_send())
         pl.when(here > 0)(lambda: z_copy(j, 1).wait_send())
 
@@ -993,9 +1021,9 @@
     return pl.pallas_call(
         functools.partial(spread_kernel, layers, groups),
         in_specs=[vmem],
-        out_specs=[vmem] * 3,
-        out_shape=[jax.ShapeDtypeStruct(slots.shape, BF16)] * 3,
-        scratch_shapes=[sem((groups,)), sem((groups,)), sem((groups, 2)), sem((groups, 2))],
+        out_specs=[vmem] * 5,
+        out_shape=[jax.ShapeDtypeStruct(slots.shape, BF16)] * 5,
+        scratch_shapes=[sem((groups,)), sem((groups,)), sem((groups, 4)), sem((groups, 4))],
         compiler_params=pltpu.CompilerParams(
             collective_id=2, has_side_effects=True, vmem_limit_bytes=16 << 20
         ),
@@ -1133,10 +1161,10 @@
         gather(up_weight),
         gather(down_weight),
     )
-    by_kernels = capacity % 16 == 0
+    by_kernels = capacity % 16 == 0 and layers > 2
     if by_kernels:
         g_own, *g_first = [a.reshape(slots, width) for a in spread(pick(cotangent))]
-        g_low, g_high = [g_own, g_first[0]], [g_own, g_first[1]]
+        g_low, g_high = [g_own, *g_first[0::2]], [g_own, *g_first[1::2]]
     else:
         g_own = exchange_out(pick(cotangent)).reshape(slots, width)
         low, high = both_hops(g_own, g_own, 1)
@@ -1154,7 +1182,8 @@
 
     (normed_in,) = step(g_low, g_high, normed_in)
     qkv_rows = dot_nn(normed_in, qkv_full).astype(BF16)
-    (qkv_rows,) = step(g_low, g_high, qkv_rows)
+    while len(g_low) < layers:
+        (qkv_rows,) = step(g_low, g_high, qkv_rows)
     attended, lse = attention_forward(qkv_rows, bucket)
     hidden_res = token_rows + dot_nn(attended, out_full)
     unit2, inverse2 = normalise(hidden_res)
@@ -1164,8 +1193,7 @@
 
     grad_out = cotangent.astype(F32)
     logits = dot_nn(mid_low, mix_weight)
-    mix1 = 1.0 / (1.0 + jnp.exp(logits[:, 0:1] - logits[:, 1:2]))
-    mix0 = 1.0 / (1.0 + jnp.exp(logits[:, 1:2] - logits[:, 0:1]))
+    mix0, mix1 = two_shares(logits[:, 0:1], logits[:, 1:2])
     dense_grad = (mix0 * grad_out).astype(BF16)
     scatter = lambda a: lax.psum_scatter(a.astype(BF16), "ep", scatter_dimension=0, tiled=True)
     back = lambda k, a: shifted(a, layers - k) if k else a

time: 531 us -> 528 us (level)
  Pallas kernels: 385 us -> 410 us
  waiting for transfers between devices: 28.3 us -> 3.74 us
    pallas_call x1, Pallas kernels: 33 us -> 64.5 us  [spread(): pl.pallas_call(functools.partial(spread_kernel, layers, groups), in_specs...]
    all_gather x4, waiting for transfers between devices: 13.9 us -> 0.04 us  [on_device(): gather = lambda w: lax.all_gather(w, 'ep', axis=0, tiled=True)]
    ppermute x4 -> x2, waiting for transfers between devices: 11.2 us -> 0.51 us  [hop(): return lax.ppermute(rows, 'dp', pairs)]
  transfers between devices with their start and end apart: 12 -> 10, of which waited for: 4 -> 2; matrix products, arithmetic and copies ran while one was open for 11% -> 11% of each run, Pallas kernels for 74% -> 79%
where the time goes in v8:
time: 528 us; the launch traced here: 520 us
  Pallas kernels  410 us (78%)
  matrix products  34.3 us (6%)
  other arithmetic  27.5 us (5%)
  starting transfers between devices  15.9 us (3%)
  between operations  15.1 us (3%)
  local copies, waits for them, and re-layouts  13.4 us (3%)
    pallas_call x1, Pallas kernels, expert_exchange(): pl.pallas_call(functools.partial(exchange_kernel, waves, layers, groups),...  147 us
    pallas_call x1, Pallas kernels, gradient_sums(): pl.pallas_call(functools.partial(sums_kernel, plan, split, layers, groups...  133 us
    pallas_call x1, Pallas kernels, spread(): pl.pallas_call(functools.partial(spread_kernel, layers, groups), in_specs...  64.5 us
    pallas_call x1, Pallas kernels, dense_branch(): pl.pallas_call(dense_kernel, grid=(ff // tile,), in_specs=[whole, whole,...  35.2 us
    pallas_call x1, Pallas kernels, attention_backward(): pl.pallas_call(functools.partial(attn_bwd_kernel, tile), grid=(pairs,), i...  18.9 us
    dot_general x6, matrix products, dot_nn(): lax.dot_general(a, b, (((1,), (0,)), ((), ())), preferred_element_type=F32)  16.2 us
    pallas_call x1, Pallas kernels, attention_forward(): pl.pallas_call(functools.partial(attn_fwd_kernel, tile), grid=(pairs,), i...  11.4 us
    unnamed x81, local copies, waits for them, and re-layouts  11.3 us
  transfers between devices with their start and end apart: 10, of which 2 were waited for; matrix products, arithmetic and copies ran while one was open for 11% of the time, Pallas kernels for 79%

profile of v8, /device:TPU:0, one launch (start us, length us, event | category | flops | bytes accessed | tf_op | source)
XLA Modules:
  0.0 520.0 jit_solution(12834906033188285091)
XLA Ops:
  11.3 64.5 %spread.1 = (bf16[8,80,1024]{2,1,0:T(8,128)(2,1)S(1)}, bf16[8,80,1024]{2,1,0:T(8,128)(2,1)S(1)}, bf16[8,80,1024]{2,1,0:T(8,128)(2,1)S(1)}, bf16[8,80,1024]{2,1,0:T(8,128)(2,1)S(1)}, bf16[8,80,1024]{2,1,0:T(8,128)(2,1)}) custom-call(bf16[8,80,1024]{2,1,0:T(8,128)(2,1)S(1)} %bitcast.56), custom_call_target="tpu_custom_call" | custom-call | flops 655360 | bytes 2621440 | tf_op jit(solution)/shard_map/spread/pallas_call | solution.py:1021
  77.6 1.6 fusion.6
  79.2 1.8 collective-permute-start
  80.9 1.3 collective-permute-start.1
  83.9 6.9 %convolution_convert_fusion.1.q_ref.k_ref.v_ref = bf16[512,3072]{1,0:T(8,128)(2,1)S(1)} fusion(bf16[512,1024]{1,0:T(8,128)(2,1)} %fusion.6, bf16[1024,3072]{1,0:T(8,128)(2,1)} %all-gather.5.cloned.1.call-done), kind=kOutput, calls=%fused_computation.1 | convolution fusion | flops 3222798336 | bytes 10485760 | tf_op jit(solution)/shard_map/dot_general | solution.py:23
  90.7 11.4 %attn_fwd.1 = (bf16[512,1024]{1,0:T(8,128)(2,1)S(1)}, f32[512,1024]{1,0:T(8,128)S(1)}) custom-call(s32[1]{0:T(128)S(6)} %copy.26.flag_ref, bf16[512,3072]{1,0:T(8,128)(2,1)S(1)} %convolution_convert_fusion.1.q_ref.k_ref.v_ref, bf16[512,3072]{1,0:T(8,128)(2,1)S(1)} %convolution_convert_fusion.1.q_ref.k_ref.v_ref, ...), custom_call_target="tpu_custom_call" | custom-call | flops 2147483648 | bytes 5242880 | tf_op jit(solution)/shard_map/attn_fwd/pallas_call | solution.py:94
  102.2 1.7 copy-done
  103.9 1.3 copy-done.5
  105.2 3.4 fusion.27
  110.0 2.0 convolution_convert_fusion.3
  112.9 1.2 fusion.13.dg_ref
  114.1 146.6 %expert_exchange.1 = (bf16[8,80,1024]{2,1,0:T(8,128)(2,1)}, bf16[8,16,128]{2,1,0:T(8,128)(2,1)}, bf16[8,80,1024]{2,1,0:T(8,128)(2,1)}, bf16[8,80,1024]{2,1,0:T(8...) custom-call(bf16[8,80,1024]{2,1,0:T(8,128)(2,1)} %bitcast.93, ...), custom_call_target="tpu_custom_call" | custom-call | flops 32212254720 | bytes 52428800 | tf_op jit(solution)/shard_map/expert_exchange/pallas_call | solution.py:602
  261.6 3.4 collective-permute-start.2
  265.1 2.3 collective-permute-start.3
  267.3 3.2 collective-permute-start.4
  272.2 35.2 %dense_branch.1 = (f32[512,1024]{1,0:T(8,128)S(1)}, f32[512,1024]{1,0:T(8,128)}, bf16[1024,4096]{1,0:T(8,128)(2,1)}, bf16[4096,1024]{1,0:T(8,128)(2,1)}) custom-call(bf16[512,1024]{1,0:T(8,128)(2,1)S(1)} %multiply_convert_fusion.mid_ref, bf16[512,1024]{1,0:T(8,128)(2,1)S(1)} %copy-done.4, bf16[1024,4096]{1,0:T(8,128)(2,1)} %all-gather.9.cloned.1.call-done.up_ref, ...), custom_call_target="tpu_custom_call" | custom-call | flops 512 | bytes 512 | tf_op jit(solution)/shard_map/dense_branch/pallas_call | solution.py:206
  310.4 1.6 multiply_reduce_fusion.1
  313.6 1.3 convolution_convert_fusion.5.g_ref
  314.9 1.3 copy-done.1
  316.9 18.9 %attn_bwd.1 = bf16[512,3072]{1,0:T(8,128)(2,1)S(1)} custom-call(s32[1]{0:T(128)S(6)} %copy.26.flag_ref, bf16[512,3072]{1,0:T(8,128)(2,1)S(1)} %copy-done.1, bf16[512,3072]{1,0:T(8,128)(2,1)S(1)} %copy-done.1, bf16[512,3072]{1,0:T(8,128)(2,1)S(1)} %copy-done.1, bf16[512,1024]{1,0:T(8,128)(2,1)S(1)} %convolution_convert_fusion.5.g_ref, f32[512,1024]{1,0:T(8,128)S(1)} %copy-done.6), custom_call_target="tpu_custom_call" | custom-call | flops 512 | bytes 512 | tf_op jit(solution)/shard_map/attn_bwd/pallas_call | solution.py:157
  335.9 5.1 fusion.8
  341.8 2.6 convolution_convert_fusion.2
  344.5 5.4 %convolution_convert_fusion = bf16[1024,3072]{1,0:T(8,128)(2,1)} fusion(bf16[512,1024]{1,0:T(8,128)(2,1)S(1)} %copy-done.29, bf16[512,3072]{1,0:T(8,128)(2,1)S(1)} %attn_bwd.1), kind=kOutput, calls=%fused_computation | convolution fusion | flops 3224371200 | bytes 10485760 | tf_op jit(solution)/shard_map/dot_general | solution.py:31
  349.9 133.4 %gradient_sums.1 = (bf16[128,3072]{1,0:T(8,128)(2,1)}, bf16[128,1024]{1,0:T(8,128)(2,1)}, bf16[128,4096]{1,0:T(8,128)(2,1)}, bf16[4,128,1024]{2,1,0:T(8,128)(2,1)}, f32[8,1024]{1,0:T(8,128)}) custom-call(f32[8,1024]{1,0:T(8,128)} %select_maximum_fusion.small_ref, bf16[4,2,128,3072]{3,2,1,0:T(8,128)(2,1)} %bitcast.60, bf16[4,2,128,1024]{3,2,1,0:T(8,128)(2,1)} %bitcast.64, ...), custom_call_target="tpu_custom_call" | custom-call | flops 62914560 | bytes 50331648 | tf_op jit(solution)/shard_map/gradient_sums/pallas_call | solution.py:897
  483.3 4.3 add_convert_fusion
  487.7 3.8 all-to-all-start
  491.5 8.8 %broadcast_multiply_fusion = (f32[1024,1024]{1,0:T(8,128)}, f32[1024,1024]{1,0:T(8,128)}) fusion(f32[1024,1024]{1,0:T(8,128)} %get-tuple-element.95, f32[]{:T(128)} %bitcast.30, f32[1024,1024]{1,0:T(8,128)} %get-tuple-element.74), kind=kLoop, calls=%fused_computation.25 | loop fusion | flops 2097152 | bytes 16777220 | tf_op jit(solution)/shard_map/mul | solution.py:1289
  501.2 1.3 convert_element_type.126
  502.5 1.5 convert_element_type.128
  504.0 1.6 convert_element_type.129
  507.0 2.0 fusion.11
  509.6 3.6 add_convert_fusion.1
  (128 shorter events, 20.3 us)
Async XLA Ops:
  7.2 2.8 copy-start.36
  7.2 3.1 copy-start.18
  7.2 76.7 %all-gather.5.cloned.1.call-start = ((), (), s32[]{:S(2)}) async-start(), calls=%async_computation.1 | async-start | bytes 7077888 | tf_op jit(solution)/shard_map/all_gather | solution.py:1137
  7.9 97.3 %all-gather.7.cloned.1.call-start = ((), (), s32[]{:S(2)}) async-start(), calls=%async_computation.2 | async-start | bytes 2359296 | tf_op jit(solution)/shard_map/all_gather | solution.py:1137
  8.7 262.3 %all-gather.9.cloned.1.call-start = ((), (), s32[]{:S(2)}) async-start(), calls=%async_computation.3 | async-start | bytes 9437184 | tf_op jit(solution)/shard_map/all_gather | solution.py:1137
  9.4 261.5 %all-gather.11.cloned.1.call-start = ((), (), s32[]{:S(2)}) async-start(), calls=%async_computation.4 | async-start | bytes 9437184 | tf_op jit(solution)/shard_map/all_gather | solution.py:1137
  10.3 66.6 %copy-start.15 = (bf16[512,1024]{1,0:T(8,128)(2,1)S(1)}, bf16[512,1024]{1,0:T(8,128)(2,1)}, u32[]{:S(2)}) copy-start(bf16[512,1024]{1,0:T(8,128)(2,1)} %param.13) | copy-start | bytes 3145732
  11.3 66.3 %copy-start.34 = (f32[1024]{0:T(1024)S(1)}, f32[1024]{0:T(1024)}, u32[]{:S(2)}) copy-start(f32[1024]{0:T(1024)} %param.16) | copy-start | bytes 12292
  76.9 6.0 %copy-start.32 = (bf16[1024,2]{0,1:T(2,128)(2,1)S(1)}, bf16[1024,2]{0,1:T(2,128)(2,1)}, u32[]{:S(2)}) copy-start(bf16[1024,2]{0,1:T(2,128)(2,1)} %param.22) | copy-start | bytes 12292
  79.2 32.8 %collective-permute-start = (bf16[640,1024]{1,0:T(8,128)(2,1)S(1)}, bf16[640,1024]{1,0:T(8,128)(2,1)}, u32[]{:S(2)}, u32[]{:S(2)}) collective-permute-start(bf16[640,1024]{1,0:T(8,128)(2,1)S(1)} %bitcast.57), channel_id=1, source_target_pairs={{16,24},{17,25},{18,26},{19,27},{20,28},{21,29},{22,30},{23,31}} | collective-permute-start | bytes 3932168 | tf_op jit(solution)/shard_map/ppermute | solution.py:1056
  80.9 31.5 %collective-permute-start.1 = (bf16[640,1024]{1,0:T(8,128)(2,1)}, bf16[640,1024]{1,0:T(8,128)(2,1)}, u32[]{:S(2)}, u32[]{:S(2)}) collective-permute-start(bf16[640,1024]{1,0:T(8,128)(2,1)} %bitcast.5), channel_id=1, source_target_pairs={{8,0},{9,1},{10,2},{11,3},{12,4},{13,5},{14,6},{15,7}} | collective-permute-start | bytes 3932168 | tf_op jit(solution)/shard_map/ppermute | solution.py:1056
  105.2 3.4 copy-start.11
  110.0 2.9 copy-start.19
  261.6 221.6 %collective-permute-start.2 = (bf16[640,1024]{1,0:T(8,128)(2,1)}, bf16[640,1024]{1,0:T(8,128)(2,1)}, u32[]{:S(2)}, u32[]{:S(2)}) collective-permute-start(bf16[640,1024]{1,0:T(8,128)(2,1)} %bitcast.92), channel_id=1, source_target_pairs={{24,0},{0,8},{8,16},{16,24},{25,1},{1,9},{9,17},{17,25},{26,2},{2,... | collective-permute-start | bytes 3932168 | tf_op jit(solution)/shard_map/ppermute | solution.py:1084
  265.1 218.2 %collective-permute-start.3 = (bf16[640,1024]{1,0:T(8,128)(2,1)}, bf16[640,1024]{1,0:T(8,128)(2,1)}, u32[]{:S(2)}, u32[]{:S(2)}) collective-permute-start(bf16[640,1024]{1,0:T(8,128)(2,1)} %bitcast.91), channel_id=1, source_target_pairs={{16,0},{24,8},{0,16},{8,24},{17,1},{25,9},{1,17},{9,25},{18,2},{26... | collective-permute-start | bytes 3932168 | tf_op jit(solution)/shard_map/ppermute | solution.py:1084
  267.3 216.0 %collective-permute-start.4 = (bf16[640,1024]{1,0:T(8,128)(2,1)}, bf16[640,1024]{1,0:T(8,128)(2,1)}, u32[]{:S(2)}, u32[]{:S(2)}) collective-permute-start(bf16[640,1024]{1,0:T(8,128)(2,1)} %bitcast.90), channel_id=1, source_target_pairs={{8,0},{16,8},{24,16},{0,24},{9,1},{17,9},{25,17},{1,25},{10,2},{18... | collective-permute-start | bytes 3932168 | tf_op jit(solution)/shard_map/ppermute | solution.py:1084
  272.2 35.2 %copy-start.20 = (bf16[512,1024]{1,0:T(8,128)(2,1)S(1)}, bf16[512,1024]{1,0:T(8,128)(2,1)}, u32[]{:S(2)}) copy-start(bf16[512,1024]{1,0:T(8,128)(2,1)} %param.25) | copy-start | bytes 3145732
  272.2 36.6 %copy-start.26 = (bf16[8,80,1024]{2,1,0:T(8,128)(2,1)S(1)}, bf16[8,80,1024]{2,1,0:T(8,128)(2,1)}, u32[]{:S(2)}) copy-start(bf16[8,80,1024]{2,1,0:T(8,128)(2,1)} %get-tuple-element.77) | copy-start | bytes 3932164
  307.4 3.0 copy-start.24
  313.6 28.2 %copy-start.21 = (f32[512,1024]{1,0:T(8,128)}, f32[512,1024]{1,0:T(8,128)S(1)}, u32[]{:S(2)}) copy-start(f32[512,1024]{1,0:T(8,128)S(1)} %convert_add_fusion) | copy-start | bytes 6291460
  313.6 3.3 copy-start.6
  313.6 22.2 %slice-start = ((s8[6291456]{0:T(1024)(128)(4,1)}), s8[4194304]{0:T(1024)(128)(4,1)S(1)}, s32[]{:S(2)}) async-start(s8[6291456]{0:T(1024)(128)(4,1)} %bitcast.86), calls=%async_computation.5 | async-start | bytes 8388608
  316.9 19.0 %copy-start.16 = (bf16[512,1024]{1,0:T(8,128)(2,1)S(1)}, bf16[512,1024]{1,0:T(8,128)(2,1)}, u32[]{:S(2)}) copy-start(bf16[512,1024]{1,0:T(8,128)(2,1)} %param.13) | copy-start | bytes 3145732
  316.9 19.0 %slice-start.1 = ((s8[6291456]{0:T(1024)(128)(4,1)}), s8[2097152]{0:T(1024)(128)(4,1)S(1)}, s32[]{:S(2)}) async-start(s8[6291456]{0:T(1024)(128)(4,1)} %bitcast.86), calls=%async_computation.6 | async-start | bytes 4194304
  335.9 6.0 %copy-start.12 = (bf16[512,1024]{1,0:T(8,128)(2,1)S(1)}, bf16[512,1024]{1,0:T(8,128)(2,1)}, u32[]{:S(2)}) copy-start(bf16[512,1024]{1,0:T(8,128)(2,1)} %copy-done.11) | copy-start | bytes 3145732
  349.9 133.4 %copy-start.25 = (bf16[8,80,1024]{2,1,0:T(8,128)(2,1)S(1)}, bf16[8,80,1024]{2,1,0:T(8,128)(2,1)}, u32[]{:S(2)}) copy-start(bf16[8,80,1024]{2,1,0:T(8,128)(2,1)} %get-tuple-element.85) | copy-start | bytes 3932164
  487.7 21.9 %all-to-all-start = ((bf16[8,80,1024]{2,1,0:T(8,128)(2,1)}), bf16[8,80,1024]{2,1,0:T(8,128)(2,1)S(1)}, u32[]{:S(2)}, u32[]{:S(2)}) async-start(bf16[8,80,1024]{2,1,0:T(8,128)(2,1)} %bitcast.29), calls=%async_computation | async-start | bytes 2621440 | tf_op jit(solution)/shard_map/all_to_all | solution.py:1280
  491.5 8.9 %copy-start.31 = (bf16[128,1024]{1,0:T(8,128)(2,1)S(1)}, bf16[128,1024]{1,0:T(8,128)(2,1)}, u32[]{:S(2)}) copy-start(bf16[128,1024]{1,0:T(8,128)(2,1)} %get-tuple-element.97) | copy-start | bytes 786436
  491.5 9.7 %copy-start.30 = (bf16[128,3072]{1,0:T(8,128)(2,1)S(1)}, bf16[128,3072]{1,0:T(8,128)(2,1)}, u32[]{:S(2)}) copy-start(bf16[128,3072]{1,0:T(8,128)(2,1)} %get-tuple-element.96) | copy-start | bytes 2359300
  502.5 3.1 copy-start.35
  502.5 4.3 copy-start.23
  504.0 3.0 copy-start.22
  (18 other events, 33.8 us)
Sparse Core Ops, SparseCore 0:
  9.9 55.9 all-gather.4
  67.8 27.8 all-gather.6
  97.6 63.1 all-gather.8
  162.6 59.3 all-gather.10
